TPU v7x, 128 devices: a whole 4x4x4 slice. The times are simulated.
128 devices in a mesh: gx: 16 (over z, y), gy: 8 (over x, core).
Axes of the slice: x: 4, y: 4, z: 4, core: 2. Of those that a mesh axis runs over, the one named last changes fastest.
Arguments:
- state: float32 [5, 120, 65536], P(None, None, ('gx', 'gy')), may hold values from -6 to 6
- coef: float32 [5, 5, 65536], P(None, None, ('gx', 'gy')), may hold values from -3 to 3
- basis_quad: float32 [216, 120], replicated, may hold values from -0.5 to 0.5
- test_deriv: float32 [120, 216], replicated, may hold values from -0.3125 to 0.3125
- trace_vec: float32 [120], replicated, may hold values from -0.5 to 0.5
- lift_vec: float32 [120], replicated, may hold values from -3 to 3
- tent_height: float32 [3, 8192], P(None, ('gx', 'gy')), may hold values from 0.2 to 0.4
- elem_tent: int32 [3, 65536], P(None, ('gx', 'gy')), may hold values from 0 to 8191, as said below
Outputs:
- final_state: float32 [5, 120, 65536], P(None, None, ('gx', 'gy'))
Inputs may be any that keep to these rules, and one draw needn't show every extreme that they name: `elem_tent`: tent t is owned by device t // 64 of the devices numbered with gx slowest. At every level the owner of an element's tent is the element's own device or one of its four neighbours along gx or gy, with wrap-around. At a level no device hands more than 64 of its elements to one neighbour; in every level some device hands exactly 64 to a neighbour, and some device receives exactly 64 from each of its four neighbours.
All inputs are finite; a program needn't handle non-finite values.
Results may differ from a plain program's by a relative error of at most 0.00011.
Values sent between devices are 32-bit elements; how exact they have to be, the bound alone decides.
No kernel may reach another device: no remote copies, remote signals or barrier semaphores. Data moves between devices by JAX's collectives and lax.ppermute only.
A program may use at most 128 MiB of HBM per device.

v0:
```python
import functools

import jax
import jax.numpy as jnp
from jax import lax
from jax.experimental import pallas as pl
from jax.experimental.pallas import tpu as pltpu
from jax.sharding import PartitionSpec as P


F32 = jnp.float32
BF16 = jnp.bfloat16
HIGHEST = lax.Precision.HIGHEST
ROWS = 48
BACK = 16
SLOTS = 5
HALVES = 2


def split(x):
    high = x.astype(BF16)
    return high, (x - high.astype(F32)).astype(BF16)


def exact_dot(left, right):
    return jnp.dot(left, right, precision=HIGHEST, preferred_element_type=F32)


def dot_rows(left, right):
    return lax.dot_general(
        left, right, (((1,), (1,)), ((), ())), precision=HIGHEST, preferred_element_type=F32
    )


def partners(index, size):
    even = index + 1 - 2 * lax.rem(index, 2)
    odd = lax.rem(index - 1 + 2 * lax.rem(index, 2) + size, size)
    return even, odd


def tent_columns(tents, me, size_first, size_second, tent_dev):
    first = lax.div(me, size_second)
    second = lax.rem(me, size_second)
    first_even, first_odd = partners(first, size_first)
    second_even, second_odd = partners(second, size_second)
    owners = [
        first_even * size_second + second,
        first_odd * size_second + second,
        first * size_second + second_even,
        first * size_second + second_odd,
    ]
    column = tents - (me - 4) * tent_dev
    for slot, owner in enumerate(owners):
        inside = (tents >= owner * tent_dev) & (tents < (owner + 1) * tent_dev)
        column = jnp.where(inside, tents - (owner - slot) * tent_dev, column)
    return column


def members(tents, me, shape):
    size_first, size_second, tent_dev = shape
    column = tent_columns(tents, me, size_first, size_second, tent_dev)
    full = (SLOTS * tent_dev, column.shape[1])
    lines = lax.broadcasted_iota(jnp.int32, full, 0)
    return jnp.where(lines == column, 1.0, 0.0).astype(BF16)


def mix(coef, values):
    mixed = []
    for target in range(len(values)):
        total = coef[target, 0:1, :] * values[0]
        for source in range(1, len(values)):
            total = total + coef[target, source : source + 1, :] * values[source]
        mixed.append(total)
    return mixed


def tent_sums(coef, member, traces, aux, vals, messages, heights, kappa):
    fields = len(traces)
    once = mix(coef, traces)
    twice = mix(coef, once)
    vals[...] = jnp.zeros_like(vals)
    aux[...] = jnp.zeros_like(aux)
    for f in range(fields):
        vals[f : f + 1, :] = traces[f][0:1]
        vals[5 + f : 6 + f, :] = once[f][1:2]
        vals[10 + f : 11 + f, :] = twice[f][2:3] - kappa * once[f][0:1]
        vals[15 + 5 * f : 20 + 5 * f, :] = coef[f]
        aux[f : f + 1, :] = traces[f][0:1]
        aux[5 + f : 6 + f, :] = once[f][1:2]
        aux[10 + f : 11 + f, :] = twice[f][2:3]
    vals[40:41, :] = jnp.ones_like(vals[40:41, :])
    high, low = split(vals[...])
    both = jnp.concatenate([high, low], axis=0)
    sums = lax.dot_general(
        both, member, (((1,), (1,)), ((), ())), preferred_element_type=F32
    )
    sums = sums[:ROWS] + sums[ROWS:]
    tent_dev = messages[0].shape[1]
    for slot in range(SLOTS):
        messages[slot][...] = sums[:, slot * tent_dev : (slot + 1) * tent_dev]
        if heights is not None:
            messages[slot][41:44, :] = heights[...]


def opening_kernel(shape, me, basis_in, test_in, trace_in, lift_in, state_in, coef_in, *rest):
    heights_in, tents_in, smat, rows3, lift_row, aux, *rest = rest
    messages = rest[:SLOTS]
    vals, basis, test, trace, lift, state, coef, heights, tents, sems = rest[SLOTS:]
    sources = (basis_in, test_in, trace_in, lift_in, state_in, coef_in, heights_in, tents_in)
    targets = (basis, test, trace, lift, state, coef, heights, tents)
    copies = [
        pltpu.make_async_copy(source, target, sems.at[k])
        for k, (source, target) in enumerate(zip(sources, targets))
    ]
    for copy in copies:
        copy.start()
    copies[0].wait()
    copies[1].wait()
    s = lax.dot_general(
        test[...],
        basis[...],
        (((0,), (0,)), ((), ())),
        precision=HIGHEST,
        preferred_element_type=F32,
    )
    smat[...] = s
    copies[2].wait()
    copies[3].wait()
    t0 = trace[...].reshape(1, s.shape[0])
    t1 = exact_dot(t0, s)
    t2 = exact_dot(t1, s)
    rows3[...] = jnp.zeros_like(rows3)
    rows3[0:1, :] = t0
    rows3[1:2, :] = t1
    rows3[2:3, :] = t2
    lift_row[...] = lift[...].reshape(1, s.shape[0])
    kappa = jnp.sum(t1 * lift_row[...], axis=1, keepdims=True)
    columns = rows3[...].T
    wide = [
        jnp.broadcast_to(columns[:, k : k + 1], (columns.shape[0], 128)) for k in range(3)
    ]
    copies[7].wait()
    member = members(tents[0:1, :], me[0], shape)
    copies[4].wait()
    fields = state.shape[0]
    traces = []
    for f in range(fields):
        parts = []
        for lane in range(state.shape[2] // 128):
            block = state[f, :, lane * 128 : (lane + 1) * 128]
            parts.append(
                jnp.concatenate(
                    [jnp.sum(block * wide[k], axis=0, keepdims=True) for k in range(3)], axis=0
                )
            )
        traces.append(jnp.concatenate(parts, axis=1))
    copies[5].wait()
    copies[6].wait()
    tent_sums(coef, member, traces, aux, vals, messages, heights, kappa)


def powers_kernel(smat, rows3, lift, state, stack, lcols, kappas, projections, rows, lrows):
    basis = smat.shape[0]
    s1 = smat[...]
    s2 = exact_dot(s1, s1)
    s3 = exact_dot(s2, s1)
    s4 = exact_dot(s2, s2)
    stack[...] = jnp.zeros_like(stack)
    half = stack.shape[1] // 2
    for power, matrix in enumerate((s1, s2 / 2.0, s3 / 6.0)):
        high, low = split(matrix)
        for side in range(2):
            stack[power * half : power * half + basis, side * half : side * half + basis] = high
            stack[
                (3 + power) * half : (3 + power) * half + basis,
                side * half : side * half + basis,
            ] = low
    rows[...] = jnp.zeros_like(rows)
    lrows[...] = jnp.zeros_like(lrows)
    rows[0:2, :] = rows3[0:2, :]
    rows[2:4, :] = exact_dot(rows3[0:2, :], s2)
    rows[4:8, :] = exact_dot(rows[0:4, :], s4)
    rows[8:9, :] = exact_dot(rows[4:5, :], s4)
    lrows[0:1, :] = lift[...]
    lrows[1:2, :] = dot_rows(lift[...], s1)
    lrows[2:4, :] = dot_rows(lrows[0:2, :], s2)
    lrows[4:8, :] = dot_rows(lrows[0:4, :], s4)
    lrows[8:9, :] = dot_rows(lrows[4:5, :], s4)
    lcols[...] = lrows[...].T
    kappas[...] = jnp.broadcast_to(
        jnp.sum(rows[...] * lift[...], axis=1, keepdims=True), kappas.shape
    )
    for f in range(state.shape[0]):
        projections[f] = exact_dot(rows[...], state[f])


def owner_kernel(kappas, own, *rest):
    *received, out = rest
    total = own[...]
    for ref in received:
        total = total + ref[...]
    mean = total / jnp.maximum(total[40:41], 1.0)
    first = mean[0:5]
    out[...] = jnp.zeros_like(out)
    out[0:10, :] = mean[0:10]
    kappa = kappas[1:2, 0 : out.shape[1]]
    for g in range(5):
        moved = jnp.sum(mean[15 + 5 * g : 20 + 5 * g] * first, axis=0, keepdims=True)
        out[10 + g : 11 + g, :] = mean[10 + g : 11 + g] + kappa * moved


def gather(tables, table, member):
    tent_dev = tables[0].shape[1]
    for slot in range(SLOTS):
        table[:, slot * tent_dev : (slot + 1) * tent_dev] = tables[slot]
    high, low = split(table[...])
    found = jnp.dot(
        jnp.concatenate([high, low], axis=0), member, preferred_element_type=F32
    )
    count = table.shape[0]
    return found[:count] + found[count:]


def heights_kernel(shape, me, tents, *rest):
    *messages, out, table = rest
    for level in range(tents.shape[0]):
        member = members(tents[level : level + 1, :], me[0], shape)
        found = gather([m[32:48, :] for m in messages], table, member)
        out[level : level + 1, :] = found[9 + level : 10 + level]


def lift_weights(coef, height, means, aux, kappas):
    kappa0 = kappas[0:1, :]
    kappa1 = kappas[1:2, :]
    fields = coef.shape[0]
    first = [means[f : f + 1] - aux[f : f + 1, :] for f in range(fields)]
    second = [
        means[5 + f : 6 + f] - aux[5 + f : 6 + f, :] - kappa0 * first[f] for f in range(fields)
    ]
    moved_first = mix(coef, first)
    moved_second = mix(coef, second)
    moved_twice = mix(coef, moved_first)
    half = height * height / 2.0
    sixth = height * height * height / 6.0
    weights = []
    for f in range(fields):
        third = (
            means[10 + f : 11 + f]
            - aux[10 + f : 11 + f, :]
            - kappa1 * moved_first[f]
            - kappa0 * second[f]
        )
        weights.append(
            (
                height * first[f] + half * second[f] + sixth * third,
                half * moved_first[f] + sixth * moved_second[f],
                sixth * moved_twice[f],
            )
        )
    return weights


def element_kernel(shape, level, count, me, tents, coef, heights, kappas, old_aux, proj, *rest):
    tables = rest[:SLOTS]
    weights_out, proj_out, aux, *messages = rest[SLOTS:-2]
    vals, table = rest[-2:]
    fields = coef.shape[0]
    member = members(tents[level : level + 1, :], me[0], shape)
    means = gather([t[...] for t in tables], table, member)
    height = heights[level : level + 1, :]
    weights = lift_weights(coef, height, means, old_aux, kappas)
    weights_out[...] = jnp.zeros_like(weights_out)
    for f in range(fields):
        for k in range(3):
            weights_out[f, k : k + 1, :] = weights[f][k]
    state = mix(coef, [proj[f, 3 : 3 + count, :] for f in range(fields)])
    state = [proj[f, 2 : 2 + count, :] + height / 3.0 * state[f] for f in range(fields)]
    state = mix(coef, state)
    state = [proj[f, 1 : 1 + count, :] + height / 2.0 * state[f] for f in range(fields)]
    state = mix(coef, state)
    fresh = []
    for f in range(fields):
        value = proj[f, 0:count, :] + height * state[f]
        for k in range(3):
            value = value + kappas[k : k + count, :] * weights[f][k]
        fresh.append(value)
        proj_out[f, 0:count, :] = value
    following = members(tents[level + 1 : level + 2, :], me[0], shape)
    tent_sums(coef, following, [v[0:3] for v in fresh], aux, vals, messages, None, kappas[1:2, :])


def level_kernel(level, offset, state, coef, heights, stack, out, packed, powers):
    fields, basis, width = out.shape
    half = packed.shape[0] // 2
    base = offset if state.shape[2] > width else 0
    packed[...] = jnp.zeros_like(packed)
    for f in range(fields):
        high, low = split(state[f, :, base : base + width])
        packed[0:basis, :] = high
        packed[half : half + basis, :] = low
        product = jnp.dot(stack[...], packed[...], preferred_element_type=F32)
        powers[f] = product[: 3 * half] + product[3 * half :]

    def lanes(tile, carry):
        near = pl.multiple_of(tile * 128, 128)
        at = pl.multiple_of(offset + near, 128)
        place = pl.multiple_of(base + near, 128)
        height = heights[level : level + 1, pl.ds(at, 128)]
        factor = [
            [
                jnp.broadcast_to(height * coef[g, f : f + 1, pl.ds(at, 128)], (8, 128))
                for f in range(fields)
            ]
            for g in range(fields)
        ]

        def combine(start, values):
            mixed = []
            for g in range(fields):
                total = start[g]
                for f in range(fields):
                    total = total + factor[g][f] * values[f]
                mixed.append(total)
            return mixed

        def lines(group, inner):
            top = pl.multiple_of(group * 8, 8)

            def power(k):
                return [
                    powers[f, pl.ds(k * half + top, 8), pl.ds(near, 128)] for f in range(fields)
                ]

            value = combine(power(1), power(2))
            value = combine(power(0), value)
            start = [state[f, pl.ds(top, 8), pl.ds(place, 128)] for f in range(fields)]
            value = combine(start, value)
            for f in range(fields):
                out[f, pl.ds(top, 8), pl.ds(near, 128)] = value[f]
            return inner

        return lax.fori_loop(0, basis // 8, lines, carry, unroll=3)

    lax.fori_loop(0, width // 128, lanes, 0)


def advance(coef, height, held, count):
    fields = coef.shape[0]
    value = mix(coef, [held[f, 5 : 5 + count, :] for f in range(fields)])
    value = [held[f, 6 : 6 + count, :] + height / 3.0 * value[f] for f in range(fields)]
    value = mix(coef, value)
    value = [held[f, 7 : 7 + count, :] + height / 2.0 * value[f] for f in range(fields)]
    value = mix(coef, value)
    return [held[f, 8 : 8 + count, :] + height * value[f] for f in range(fields)]


def lift_kernel(coef, heights, weights0, weights1, lcols, *rest):
    *blocks, out, held = rest
    fields, _, n_elem = out.shape
    width = n_elem // len(blocks)
    held[...] = jnp.zeros_like(held)
    for f in range(fields):
        held[f, 8:11, :] = weights0[f, 0:3, :]
    value = advance(coef, heights[1:2, :], held, 6)
    for f in range(fields):
        held[f, 8:14, :] = value[f]
        held[f, 8:11, :] = held[f, 8:11, :] + weights1[f, 0:3, :]
    value = advance(coef, heights[2:3, :], held, 9)
    high, low = split(lcols[...])
    left = jnp.concatenate([high, high, low], axis=1)
    for f in range(fields):
        held[f, 8:17, :] = value[f]
        right_high, right_low = split(held[f, 8:24, :])
        right = jnp.concatenate([right_high, right_low, right_high], axis=0)
        added = jnp.dot(left, right, preferred_element_type=F32)
        for k, block in enumerate(blocks):
            at = slice(k * width, (k + 1) * width)
            out[f, :, at] = block[f] + added[:, at]


def closing_kernel(shape, level, me, tents, coef, heights, kappas, old_aux, lcols, state, *rest):
    tables = rest[:SLOTS]
    out, table, held, sems = rest[SLOTS:]
    fields, basis, n_elem = state.shape
    member = members(tents[level : level + 1, :], me[0], shape)
    means = gather([t[...] for t in tables], table, member)
    height = heights[level : level + 1, :]
    weights = lift_weights(coef, height, means, old_aux, kappas)
    wide = [jnp.broadcast_to(lcols[:, k : k + 1], (basis, 128)) for k in range(3)]
    copies = []
    for f in range(fields):
        for lane in range(n_elem // 128):
            at = slice(lane * 128, (lane + 1) * 128)
            value = state[f, :, at]
            for k in range(3):
                value = value + wide[k] * weights[f][k][:, at]
            held[f, :, at] = value
        copies.append(pltpu.make_async_copy(held.at[f], out.at[f], sems.at[f]))
        copies[-1].start()
    for copy in copies:
        copy.wait()


def call(kernel, outs, args, scratch=(), scalars=0, flops=1000000, space=pltpu.VMEM, out_space=pltpu.VMEM, limit=40):
    specs = [
        pl.BlockSpec(memory_space=pltpu.SMEM if i < scalars else space)
        for i in range(len(args))
    ]
    single = not isinstance(outs, (list, tuple))
    shapes = [outs] if single else list(outs)
    moved = sum(4 * s.size for s in shapes) + sum(4 * a.size for a in args)
    result = pl.pallas_call(
        kernel,
        out_shape=shapes,
        in_specs=specs,
        out_specs=[pl.BlockSpec(memory_space=out_space)] * len(shapes),
        scratch_shapes=list(scratch),
        cost_estimate=pl.CostEstimate(flops=flops, bytes_accessed=moved, transcendentals=0),
        compiler_params=pltpu.CompilerParams(vmem_limit_bytes=min(limit * 1024 * 1024, 67043328)),
    )(*args)
    return result[0] if single else result


def shaped(*dims, dtype=F32):
    return jax.ShapeDtypeStruct(dims, dtype)


def swap(x, axis, odd):
    size = lax.axis_size(axis)
    pairs = []
    for i in range(size):
        mate = (i - 1 + 2 * (i % 2)) % size if odd else i + 1 - 2 * (i % 2)
        pairs.append((i, mate))
    return lax.ppermute(x, axis, pairs)


ROUTES = ((1, "gx", True), (0, "gx", False), (3, "gy", True), (2, "gy", False))


def exchange(pieces):
    received = [None] * 4
    for slot, axis, odd in ROUTES:
        received[slot] = swap(pieces[slot], axis, odd)
    return received


def slab(state, coef, basis_quad, test_deriv, trace_vec, lift_vec, tent_height, elem_tent):
    size_first = lax.axis_size("gx")
    size_second = lax.axis_size("gy")
    fields, basis, n_elem = state.shape
    levels, tent_dev = tent_height.shape
    shape = (size_first, size_second, tent_dev)
    me = (lax.axis_index("gx") * size_second + lax.axis_index("gy")).reshape(1)
    message = [shaped(ROWS, tent_dev)] * SLOTS
    aux_shape = shaped(BACK, n_elem)
    vals = pltpu.VMEM((ROWS, n_elem), F32)
    table = pltpu.VMEM((BACK, SLOTS * tent_dev), F32)

    smat, rows3, lift, aux, *out = call(
        functools.partial(opening_kernel, shape),
        [shaped(basis, basis), shaped(8, basis), shaped(1, basis), aux_shape] + message,
        (
            me,
            *(
                pltpu.with_memory_space_constraint(x, pltpu.HBM)
                for x in (
                    basis_quad,
                    test_deriv.T,
                    trace_vec,
                    lift_vec,
                    state,
                    coef,
                    tent_height,
                    elem_tent,
                )
            ),
        ),
        [
            vals,
            pltpu.VMEM(basis_quad.shape, F32),
            pltpu.VMEM(test_deriv.shape[::-1], F32),
            pltpu.VMEM(trace_vec.shape, F32),
            pltpu.VMEM(lift_vec.shape, F32),
            pltpu.VMEM(state.shape, F32),
            pltpu.VMEM(coef.shape, F32),
            pltpu.VMEM(tent_height.shape, F32),
            pltpu.VMEM(elem_tent.shape, jnp.int32),
            pltpu.SemaphoreType.DMA((8,)),
        ],
        1,
        space=pltpu.HBM,
    )
    stack, lcols, kappas, proj = call(
        powers_kernel,
        [
            shaped(768, 256, dtype=BF16),
            shaped(basis, 16),
            shaped(16, n_elem),
            shaped(fields, 16, n_elem),
        ],
        (smat, rows3, lift, state),
        [pltpu.VMEM((16, basis), F32), pltpu.VMEM((16, basis), F32)],
        flops=100000000,
    )
    blocks = [state] * HALVES
    width = n_elem // HALVES
    weights = []
    heights = None

    def advance_block(level, half):
        blocks[half] = call(
            functools.partial(level_kernel, level, half * width),
            shaped(fields, basis, width),
            (blocks[half], coef, heights, stack),
            [pltpu.VMEM((256, width), BF16), pltpu.VMEM((fields, 384, width), F32)],
            flops=1000000000,
        )

    for level in range(levels):
        received = exchange(out[:4])
        means = call(owner_kernel, shaped(BACK, tent_dev), (kappas, out[4], *received))
        back = exchange([means] * 4)
        if level == 0:
            heights = call(
                functools.partial(heights_kernel, shape),
                shaped(8, n_elem),
                (me, elem_tent, *received, out[4]),
                [table],
                1,
                flops=10000000,
            )
        for half in range(HALVES):
            advance_block(level, half)
        if level < levels - 1:
            weight, proj, aux, *out = call(
                functools.partial(element_kernel, shape, level, 6 - 3 * level),
                [shaped(fields, 8, n_elem), shaped(fields, 8, n_elem), aux_shape] + message,
                (me, elem_tent, coef, heights, kappas, aux, proj, *back, means),
                [vals, table],
                1,
            )
            weights.append(weight)
    values = call(
        lift_kernel,
        shaped(fields, basis, n_elem),
        (coef, heights, weights[0], weights[1], lcols, *blocks),
        [pltpu.VMEM((fields, 24, n_elem), F32)],
        flops=100000000,
    )
    return call(
        functools.partial(closing_kernel, shape, levels - 1),
        shaped(fields, basis, n_elem),
        (me, elem_tent, coef, heights, kappas, aux, lcols, values, *back, means),
        [table, pltpu.VMEM(state.shape, F32), pltpu.SemaphoreType.DMA((fields,))],
        1,
        out_space=pltpu.HBM,
    )


def solution(mesh):
    placed = (
        P(None, None, ("gx", "gy")),
        P(None, None, ("gx", "gy")),
        P(),
        P(),
        P(),
        P(),
        P(None, ("gx", "gy")),
        P(None, ("gx", "gy")),
    )
    return jax.shard_map(
        slab,
        mesh=mesh,
        in_specs=placed,
        out_specs=P(None, None, ("gx", "gy")),
        check_vma=False,
    )
```

profile of v0, /device:TPU:1, one launch (start us, length us, event | category | flops | bytes accessed | tf_op | source)
XLA Modules:
  0.0 63.6 jit_solution(1513072882712261250)
XLA Ops:
  0.0 3.0 %shard_map.82 = (f32[120,120]{1,0:T(8,128)S(1)}, f32[8,120]{1,0:T(8,128)S(1)}, f32[1,120]{1,0:T(1,128)S(1)}, f32[16,512]{1,0:T(8,128)S(1)}, f32[48,64]{1,0:T(8,1...) custom-call(s32[1]{0:T(128)} %bitcast.me, ...), custom_call_target="tpu_custom_call" | custom-call | flops 1000000 | bytes 1651364 | tf_op jit(solution)/shard_map/pallas_call | solution.py:412
  3.0 2.2 %collective-permute-start = (f32[48,64]{1,0:T(8,128)S(1)}, f32[48,64]{1,0:T(8,128)S(1)}, u32[]{:S(2)}, u32[]{:S(2)}) collective-permute-start(f32[48,64]{1,0:T(8,128)S(1)} %get-tuple-element.33), channel_id=1, source_target_pairs={{0,8},{8,0},{16,24},{24,16},{32,40},{40,32},{48,56},{56,48},{64,72... | collective-permute-start | bytes 36872 | tf_op jit(solution)/shard_map/ppermute | solution.py:434
  5.2 5.4 %collective-permute-start.1 = (f32[48,64]{1,0:T(8,128)S(1)}, f32[48,64]{1,0:T(8,128)S(1)}, u32[]{:S(2)}, u32[]{:S(2)}) collective-permute-start(f32[48,64]{1,0:T(8,128)S(1)} %get-tuple-element.34), channel_id=1, source_target_pairs={{0,120},{8,16},{16,8},{24,32},{32,24},{40,48},{48,40},{56,64},{64,... | collective-permute-start | bytes 36872 | tf_op jit(solution)/shard_map/ppermute | solution.py:434
  10.6 1.2 %collective-permute-start.2 = (f32[48,64]{1,0:T(8,128)S(1)}, f32[48,64]{1,0:T(8,128)S(1)}, u32[]{:S(2)}, u32[]{:S(2)}) collective-permute-start(f32[48,64]{1,0:T(8,128)S(1)} %get-tuple-element.35), channel_id=1, source_target_pairs={{0,1},{1,0},{2,3},{3,2},{4,5},{5,4},{6,7},{7,6},{8,9},{9,8},{10,11... | collective-permute-start | bytes 36872 | tf_op jit(solution)/shard_map/ppermute | solution.py:434
  11.8 1.1 %collective-permute-start.3 = (f32[48,64]{1,0:T(8,128)S(1)}, f32[48,64]{1,0:T(8,128)S(1)}, u32[]{:S(2)}, u32[]{:S(2)}) collective-permute-start(f32[48,64]{1,0:T(8,128)S(1)} %get-tuple-element.36), channel_id=1, source_target_pairs={{0,7},{1,2},{2,1},{3,4},{4,3},{5,6},{6,5},{7,0},{8,15},{9,10},{10,... | collective-permute-start | bytes 36872 | tf_op jit(solution)/shard_map/ppermute | solution.py:434
  12.9 2.5 %shard_map.84 = (bf16[768,256]{1,0:T(8,128)(2,1)S(1)}, f32[120,16]{1,0:T(8,128)S(1)}, f32[16,512]{1,0:T(8,128)S(1)}, f32[5,16,512]{2,1,0:T(8,128)S(1)}) custom-call(f32[120,120]{1,0:T(8,128)S(1)} %get-tuple-element.38.smat, f32[8,120]{1,0:T(8,128)S(1)} %get-tuple-element.39.rows3, f32[1,120]{1,0:T(1,128)S(1)} %get-tuple-element.40.lift, ...), custom_call_target="tpu_custom_call" | custom-call | flops 100000000 | bytes 2281440 | tf_op jit(solution)/shard_map/pallas_call | solution.py:412
  15.5 0.0 collective-permute-done.2.rest_2_
  15.5 0.0 collective-permute-done.3.rest_3_
  15.5 0.8 %collective-permute-start.7 = (f32[16,64]{1,0:T(8,128)S(1)}, f32[16,64]{1,0:T(8,128)S(1)}, u32[]{:S(2)}, u32[]{:S(2)}) collective-permute-start(f32[16,64]{1,0:T(8,128)S(1)} %shard_map.85.rest_4_), channel_id=1, source_target_pairs={{0,7},{1,2},{2,1},{3,4},{4,3},{5,6},{6,5},{7,0},{8,15},{9,10},{10,... | collective-permute-start | bytes 12296 | tf_op jit(solution)/shard_map/ppermute | solution.py:434
  16.3 3.0 %collective-permute-start.6 = (f32[16,64]{1,0:T(8,128)S(1)}, f32[16,64]{1,0:T(8,128)S(1)}, u32[]{:S(2)}, u32[]{:S(2)}) collective-permute-start(f32[16,64]{1,0:T(8,128)S(1)} %shard_map.85.rest_4_), channel_id=1, source_target_pairs={{0,1},{1,0},{2,3},{3,2},{4,5},{5,4},{6,7},{7,6},{8,9},{9,8},{10,11... | collective-permute-start | bytes 12296 | tf_op jit(solution)/shard_map/ppermute | solution.py:434
  19.3 0.6 %collective-permute-start.5 = (f32[16,64]{1,0:T(8,128)S(1)}, f32[16,64]{1,0:T(8,128)S(1)}, u32[]{:S(2)}, u32[]{:S(2)}) collective-permute-start(f32[16,64]{1,0:T(8,128)S(1)} %shard_map.85.rest_4_), channel_id=1, source_target_pairs={{0,120},{8,16},{16,8},{24,32},{32,24},{40,48},{48,40},{56,64},{64,... | collective-permute-start | bytes 12296 | tf_op jit(solution)/shard_map/ppermute | solution.py:434
  19.9 0.0 collective-permute-start.4
  19.9 0.3 shard_map.83.heights
  20.2 1.4 %shard_map.92.state = f32[5,120,256]{2,1,0:T(8,128)S(1)} custom-call(f32[5,120,512]{2,1,0:T(8,128)S(1)} %copy-done, f32[5,5,512]{2,1,0:T(8,128)S(1)} %copy-done.1, f32[8,512]{1,0:T(8,128)S(1)} %shard_map.83.heights, bf16[768,256]{1,0:T(8,128)(2,1)S(1)} %get-tuple-element.55.stack), custom_call_target="tpu_custom_call" | custom-call | flops 1000000000 | bytes 2697216 | tf_op jit(solution)/shard_map/pallas_call | solution.py:412
  21.7 1.4 %shard_map.89.state = f32[5,120,256]{2,1,0:T(8,128)S(1)} custom-call(f32[5,120,512]{2,1,0:T(8,128)S(1)} %copy-done, f32[5,5,512]{2,1,0:T(8,128)S(1)} %copy-done.1, f32[8,512]{1,0:T(8,128)S(1)} %shard_map.83.heights, bf16[768,256]{1,0:T(8,128)(2,1)S(1)} %get-tuple-element.55.stack), custom_call_target="tpu_custom_call" | custom-call | flops 1000000000 | bytes 2697216 | tf_op jit(solution)/shard_map/pallas_call | solution.py:412
  23.1 1.4 %shard_map.93.state = f32[5,120,256]{2,1,0:T(8,128)S(1)} custom-call(f32[5,120,256]{2,1,0:T(8,128)S(1)} %shard_map.92.state, f32[5,5,512]{2,1,0:T(8,128)S(1)} %copy-done.1, f32[8,512]{1,0:T(8,128)S(1)} %shard_map.83.heights, bf16[768,256]{1,0:T(8,128)(2,1)S(1)} %get-tuple-element.55.stack), custom_call_target="tpu_custom_call" | custom-call | flops 1000000000 | bytes 2082816 | tf_op jit(solution)/shard_map/pallas_call | solution.py:412
  24.5 0.6 collective-permute-done.5.rest_1_
  25.1 0.0 collective-permute-done.4.rest_0_
  25.1 0.9 %shard_map.86 = (f32[5,8,512]{2,1,0:T(8,128)S(1)}, f32[5,8,512]{2,1,0:T(8,128)S(1)}, f32[16,512]{1,0:T(8,128)S(1)}, f32[48,64]{1,0:T(8,128)S(1)}, f32[48,64]{1,0...) custom-call(s32[1]{0:T(128)} %bitcast.me, s32[3,512]{1,0:T(4,128)S(1)} %copy-done.2, ...), custom_call_target="tpu_custom_call" | custom-call | flops 1000000 | bytes 581636 | tf_op jit(solution)/shard_map/pallas_call | solution.py:412
  26.0 1.0 %collective-permute-start.8 = (f32[48,64]{1,0:T(8,128)S(1)}, f32[48,64]{1,0:T(8,128)S(1)}, u32[]{:S(2)}, u32[]{:S(2)}) collective-permute-start(f32[48,64]{1,0:T(8,128)S(1)} %get-tuple-element.47), channel_id=1, source_target_pairs={{0,8},{8,0},{16,24},{24,16},{32,40},{40,32},{48,56},{56,48},{64,72... | collective-permute-start | bytes 36872 | tf_op jit(solution)/shard_map/ppermute | solution.py:434
  27.0 4.2 %collective-permute-start.9 = (f32[48,64]{1,0:T(8,128)S(1)}, f32[48,64]{1,0:T(8,128)S(1)}, u32[]{:S(2)}, u32[]{:S(2)}) collective-permute-start(f32[48,64]{1,0:T(8,128)S(1)} %get-tuple-element.48), channel_id=1, source_target_pairs={{0,120},{8,16},{16,8},{24,32},{32,24},{40,48},{48,40},{56,64},{64,... | collective-permute-start | bytes 36872 | tf_op jit(solution)/shard_map/ppermute | solution.py:434
  31.1 1.1 %collective-permute-start.10 = (f32[48,64]{1,0:T(8,128)S(1)}, f32[48,64]{1,0:T(8,128)S(1)}, u32[]{:S(2)}, u32[]{:S(2)}) collective-permute-start(f32[48,64]{1,0:T(8,128)S(1)} %get-tuple-element.49), channel_id=1, source_target_pairs={{0,1},{1,0},{2,3},{3,2},{4,5},{5,4},{6,7},{7,6},{8,9},{9,8},{10,11... | collective-permute-start | bytes 36872 | tf_op jit(solution)/shard_map/ppermute | solution.py:434
  32.3 0.0 collective-permute-start.11
  32.3 1.4 %shard_map.94.rest_1_ = f32[5,120,256]{2,1,0:T(8,128)S(1)} custom-call(f32[5,120,256]{2,1,0:T(8,128)S(1)} %shard_map.93.state, f32[5,5,512]{2,1,0:T(8,128)S(1)} %copy-done.1, f32[8,512]{1,0:T(8,128)S(1)} %shard_map.83.heights, bf16[768,256]{1,0:T(8,128)(2,1)S(1)} %get-tuple-element.55.stack), custom_call_target="tpu_custom_call" | custom-call | flops 1000000000 | bytes 2082816 | tf_op jit(solution)/shard_map/pallas_call | solution.py:412
  33.7 0.0 collective-permute-done.8.rest_0_
  33.7 0.0 collective-permute-done.10.rest_2_
  33.7 2.1 %collective-permute-done.11.rest_3_ = f32[48,64]{1,0:T(8,128)S(1)} collective-permute-done((f32[48,64]{1,0:T(8,128)S(1)}, f32[48,64]{1,0:T(8,128)S(1)}, u32[]{:S(2)}, u32[]{:S(2)}) %collective-permute-start.11) | collective-permute-done | bytes 12320 | tf_op jit(solution)/shard_map/ppermute | solution.py:434
  35.8 0.9 %collective-permute-start.15 = (f32[16,64]{1,0:T(8,128)S(1)}, f32[16,64]{1,0:T(8,128)S(1)}, u32[]{:S(2)}, u32[]{:S(2)}) collective-permute-start(f32[16,64]{1,0:T(8,128)S(1)} %shard_map.87.rest_4_), channel_id=1, source_target_pairs={{0,7},{1,2},{2,1},{3,4},{4,3},{5,6},{6,5},{7,0},{8,15},{9,10},{10,... | collective-permute-start | bytes 12296 | tf_op jit(solution)/shard_map/ppermute | solution.py:434
  36.7 1.7 %collective-permute-start.14 = (f32[16,64]{1,0:T(8,128)S(1)}, f32[16,64]{1,0:T(8,128)S(1)}, u32[]{:S(2)}, u32[]{:S(2)}) collective-permute-start(f32[16,64]{1,0:T(8,128)S(1)} %shard_map.87.rest_4_), channel_id=1, source_target_pairs={{0,1},{1,0},{2,3},{3,2},{4,5},{5,4},{6,7},{7,6},{8,9},{9,8},{10,11... | collective-permute-start | bytes 12296 | tf_op jit(solution)/shard_map/ppermute | solution.py:434
  38.4 1.7 %collective-permute-start.13 = (f32[16,64]{1,0:T(8,128)S(1)}, f32[16,64]{1,0:T(8,128)S(1)}, u32[]{:S(2)}, u32[]{:S(2)}) collective-permute-start(f32[16,64]{1,0:T(8,128)S(1)} %shard_map.87.rest_4_), channel_id=1, source_target_pairs={{0,120},{8,16},{16,8},{24,32},{32,24},{40,48},{48,40},{56,64},{64,... | collective-permute-start | bytes 12296 | tf_op jit(solution)/shard_map/ppermute | solution.py:434
  40.1 1.4 %shard_map.90.state = f32[5,120,256]{2,1,0:T(8,128)S(1)} custom-call(f32[5,120,256]{2,1,0:T(8,128)S(1)} %shard_map.89.state, f32[5,5,512]{2,1,0:T(8,128)S(1)} %copy-done.1, f32[8,512]{1,0:T(8,128)S(1)} %shard_map.83.heights, bf16[768,256]{1,0:T(8,128)(2,1)S(1)} %get-tuple-element.55.stack), custom_call_target="tpu_custom_call" | custom-call | flops 1000000000 | bytes 2082816 | tf_op jit(solution)/shard_map/pallas_call | solution.py:412
  41.5 0.0 collective-permute-done.15.rest_3_
  41.5 0.0 collective-permute-done.14.rest_2_
  41.6 2.7 %collective-permute-done.13.rest_1_ = f32[16,64]{1,0:T(8,128)S(1)} collective-permute-done((f32[16,64]{1,0:T(8,128)S(1)}, f32[16,64]{1,0:T(8,128)S(1)}, u32[]{:S(2)}, u32[]{:S(2)}) %collective-permute-start.13) | collective-permute-done | bytes 4128 | tf_op jit(solution)/shard_map/ppermute | solution.py:434
  44.2 1.4 %shard_map.88 = (f32[5,8,512]{2,1,0:T(8,128)S(1)}, f32[5,8,512]{2,1,0:T(8,128)}, f32[16,512]{1,0:T(8,128)S(1)}, f32[48,64]{1,0:T(8,128)S(1)}, f32[48,64]{1,0:T(8...) custom-call(s32[1]{0:T(128)} %bitcast.me, s32[3,512]{1,0:T(4,128)S(1)} %copy-done.2, ...), custom_call_target="tpu_custom_call" | custom-call | flops 1000000 | bytes 499716 | tf_op jit(solution)/shard_map/pallas_call | solution.py:412
  45.6 1.9 %collective-permute-start.17 = (f32[48,64]{1,0:T(8,128)S(1)}, f32[48,64]{1,0:T(8,128)S(1)}, u32[]{:S(2)}, u32[]{:S(2)}) collective-permute-start(f32[48,64]{1,0:T(8,128)S(1)} %get-tuple-element.58), channel_id=1, source_target_pairs={{0,120},{8,16},{16,8},{24,32},{32,24},{40,48},{48,40},{56,64},{64,... | collective-permute-start | bytes 36872 | tf_op jit(solution)/shard_map/ppermute | solution.py:434
  47.5 1.3 %collective-permute-start.18 = (f32[48,64]{1,0:T(8,128)S(1)}, f32[48,64]{1,0:T(8,128)S(1)}, u32[]{:S(2)}, u32[]{:S(2)}) collective-permute-start(f32[48,64]{1,0:T(8,128)S(1)} %get-tuple-element.59), channel_id=1, source_target_pairs={{0,1},{1,0},{2,3},{3,2},{4,5},{5,4},{6,7},{7,6},{8,9},{9,8},{10,11... | collective-permute-start | bytes 36872 | tf_op jit(solution)/shard_map/ppermute | solution.py:434
  48.8 0.0 collective-permute-start.19
  48.8 1.4 %shard_map.91.rest_0_ = f32[5,120,256]{2,1,0:T(8,128)S(1)} custom-call(f32[5,120,256]{2,1,0:T(8,128)S(1)} %shard_map.90.state, f32[5,5,512]{2,1,0:T(8,128)S(1)} %copy-done.1, f32[8,512]{1,0:T(8,128)S(1)} %shard_map.83.heights, bf16[768,256]{1,0:T(8,128)(2,1)S(1)} %get-tuple-element.55.stack), custom_call_target="tpu_custom_call" | custom-call | flops 1000000000 | bytes 2082816 | tf_op jit(solution)/shard_map/pallas_call | solution.py:412
  50.2 1.4 %collective-permute-done.17.rest_1_ = f32[48,64]{1,0:T(8,128)S(1)} collective-permute-done((f32[48,64]{1,0:T(8,128)S(1)}, f32[48,64]{1,0:T(8,128)S(1)}, u32[]{:S(2)}, u32[]{:S(2)}) %collective-permute-start.17) | collective-permute-done | bytes 12320 | tf_op jit(solution)/shard_map/ppermute | solution.py:434
  51.6 0.0 collective-permute-done.18.rest_2_
  51.6 0.7 %collective-permute-done.19.rest_3_ = f32[48,64]{1,0:T(8,128)S(1)} collective-permute-done((f32[48,64]{1,0:T(8,128)S(1)}, f32[48,64]{1,0:T(8,128)S(1)}, u32[]{:S(2)}, u32[]{:S(2)}) %collective-permute-start.19) | collective-permute-done | bytes 12320 | tf_op jit(solution)/shard_map/ppermute | solution.py:434
  52.4 1.3 %collective-permute-start.23 = (f32[16,64]{1,0:T(8,128)S(1)}, f32[16,64]{1,0:T(8,128)S(1)}, u32[]{:S(2)}, u32[]{:S(2)}) collective-permute-start(f32[16,64]{1,0:T(8,128)S(1)} %shard_map.96.rest_4_), channel_id=1, source_target_pairs={{0,7},{1,2},{2,1},{3,4},{4,3},{5,6},{6,5},{7,0},{8,15},{9,10},{10,... | collective-permute-start | bytes 12296 | tf_op jit(solution)/shard_map/ppermute | solution.py:434
  53.7 2.3 %collective-permute-start.22 = (f32[16,64]{1,0:T(8,128)S(1)}, f32[16,64]{1,0:T(8,128)S(1)}, u32[]{:S(2)}, u32[]{:S(2)}) collective-permute-start(f32[16,64]{1,0:T(8,128)S(1)} %shard_map.96.rest_4_), channel_id=1, source_target_pairs={{0,1},{1,0},{2,3},{3,2},{4,5},{5,4},{6,7},{7,6},{8,9},{9,8},{10,11... | collective-permute-start | bytes 12296 | tf_op jit(solution)/shard_map/ppermute | solution.py:434
  56.0 2.4 %collective-permute-start.21 = (f32[16,64]{1,0:T(8,128)S(1)}, f32[16,64]{1,0:T(8,128)S(1)}, u32[]{:S(2)}, u32[]{:S(2)}) collective-permute-start(f32[16,64]{1,0:T(8,128)S(1)} %shard_map.96.rest_4_), channel_id=1, source_target_pairs={{0,120},{8,16},{16,8},{24,32},{32,24},{40,48},{48,40},{56,64},{64,... | collective-permute-start | bytes 12296 | tf_op jit(solution)/shard_map/ppermute | solution.py:434
  58.4 0.7 %shard_map.95.state = f32[5,120,512]{2,1,0:T(8,128)S(1)} custom-call(f32[5,5,512]{2,1,0:T(8,128)S(1)} %copy-done.1, f32[8,512]{1,0:T(8,128)S(1)} %shard_map.83.heights, f32[5,8,512]{2,1,0:T(8,128)S(1)} %get-tuple-element.53.weights0, f32[5,8,512]{2,1,0:T(8,128)S(1)} %get-tuple-element.54.weights1, f32[120,16]{1,0:T(8,128)S(1)} %get-tuple-element.52.lcols, ...), custom_call_target="tpu_custom_call" | custom-call | flops 100000000 | bytes 2696704 | tf_op jit(solution)/shard_map/pallas_call | solution.py:412
  59.1 2.7 %collective-permute-done.21.rest_1_ = f32[16,64]{1,0:T(8,128)S(1)} collective-permute-done((f32[16,64]{1,0:T(8,128)S(1)}, f32[16,64]{1,0:T(8,128)S(1)}, u32[]{:S(2)}, u32[]{:S(2)}) %collective-permute-start.21) | collective-permute-done | bytes 4128 | tf_op jit(solution)/shard_map/ppermute | solution.py:434
  61.8 1.6 %shard_map.97 = f32[5,120,512]{2,1,0:T(8,128)} custom-call(s32[1]{0:T(128)} %bitcast.me, s32[3,512]{1,0:T(4,128)S(1)} %copy-done.2, f32[5,5,512]{2,1,0:T(8,128)S(1)} %copy-done.1, f32[8,512]{1,0:T(8,128)S(1)} %shard_map.83.heights, f32[16,512]{1,0:T(8,128)S(1)} %get-tuple-element.41.kappas, f32[16,512]{1,0:T(8,128)S(1)} %get-tuple-element.51.old_aux, ...), custom_call_target="tpu_custom_call" | custom-call | flops 1000000 | bytes 2625028 | tf_op jit(solution)/shard_map/pallas_call | solution.py:412
  (22 shorter events, 0.1 us)
Async XLA Ops:
  0.0 12.9 %copy-start = (f32[5,120,512]{2,1,0:T(8,128)S(1)}, f32[5,120,512]{2,1,0:T(8,128)}, u32[]{:S(2)}) copy-start(f32[5,120,512]{2,1,0:T(8,128)} %state.5) | copy-start | bytes 3686404
  0.0 19.9 %copy-start.2 = (s32[3,512]{1,0:T(4,128)S(1)}, s32[3,512]{1,0:T(4,128)}, u32[]{:S(2)}) copy-start(s32[3,512]{1,0:T(4,128)} %tents.7) | copy-start | bytes 18436
  0.0 20.2 %copy-start.1 = (f32[5,5,512]{2,1,0:T(8,128)S(1)}, f32[5,5,512]{2,1,0:T(8,128)}, u32[]{:S(2)}) copy-start(f32[5,5,512]{2,1,0:T(8,128)} %coef.19) | copy-start | bytes 153604
  3.0 12.4 %collective-permute-start = (f32[48,64]{1,0:T(8,128)S(1)}, f32[48,64]{1,0:T(8,128)S(1)}, u32[]{:S(2)}, u32[]{:S(2)}) collective-permute-start(f32[48,64]{1,0:T(8,128)S(1)} %get-tuple-element.33), channel_id=1, source_target_pairs={{0,8},{8,0},{16,24},{24,16},{32,40},{40,32},{48,56},{56,48},{64,72... | collective-permute-start | bytes 36872 | tf_op jit(solution)/shard_map/ppermute | solution.py:434
  5.2 10.2 %collective-permute-start.1 = (f32[48,64]{1,0:T(8,128)S(1)}, f32[48,64]{1,0:T(8,128)S(1)}, u32[]{:S(2)}, u32[]{:S(2)}) collective-permute-start(f32[48,64]{1,0:T(8,128)S(1)} %get-tuple-element.34), channel_id=1, source_target_pairs={{0,120},{8,16},{16,8},{24,32},{32,24},{40,48},{48,40},{56,64},{64,... | collective-permute-start | bytes 36872 | tf_op jit(solution)/shard_map/ppermute | solution.py:434
  10.6 4.9 %collective-permute-start.2 = (f32[48,64]{1,0:T(8,128)S(1)}, f32[48,64]{1,0:T(8,128)S(1)}, u32[]{:S(2)}, u32[]{:S(2)}) collective-permute-start(f32[48,64]{1,0:T(8,128)S(1)} %get-tuple-element.35), channel_id=1, source_target_pairs={{0,1},{1,0},{2,3},{3,2},{4,5},{5,4},{6,7},{7,6},{8,9},{9,8},{10,11... | collective-permute-start | bytes 36872 | tf_op jit(solution)/shard_map/ppermute | solution.py:434
  11.8 3.6 %collective-permute-start.3 = (f32[48,64]{1,0:T(8,128)S(1)}, f32[48,64]{1,0:T(8,128)S(1)}, u32[]{:S(2)}, u32[]{:S(2)}) collective-permute-start(f32[48,64]{1,0:T(8,128)S(1)} %get-tuple-element.36), channel_id=1, source_target_pairs={{0,7},{1,2},{2,1},{3,4},{4,3},{5,6},{6,5},{7,0},{8,15},{9,10},{10,... | collective-permute-start | bytes 36872 | tf_op jit(solution)/shard_map/ppermute | solution.py:434
  15.5 9.0 %collective-permute-start.7 = (f32[16,64]{1,0:T(8,128)S(1)}, f32[16,64]{1,0:T(8,128)S(1)}, u32[]{:S(2)}, u32[]{:S(2)}) collective-permute-start(f32[16,64]{1,0:T(8,128)S(1)} %shard_map.85.rest_4_), channel_id=1, source_target_pairs={{0,7},{1,2},{2,1},{3,4},{4,3},{5,6},{6,5},{7,0},{8,15},{9,10},{10,... | collective-permute-start | bytes 12296 | tf_op jit(solution)/shard_map/ppermute | solution.py:434
  16.3 8.2 %collective-permute-start.6 = (f32[16,64]{1,0:T(8,128)S(1)}, f32[16,64]{1,0:T(8,128)S(1)}, u32[]{:S(2)}, u32[]{:S(2)}) collective-permute-start(f32[16,64]{1,0:T(8,128)S(1)} %shard_map.85.rest_4_), channel_id=1, source_target_pairs={{0,1},{1,0},{2,3},{3,2},{4,5},{5,4},{6,7},{7,6},{8,9},{9,8},{10,11... | collective-permute-start | bytes 12296 | tf_op jit(solution)/shard_map/ppermute | solution.py:434
  19.3 5.8 %collective-permute-start.5 = (f32[16,64]{1,0:T(8,128)S(1)}, f32[16,64]{1,0:T(8,128)S(1)}, u32[]{:S(2)}, u32[]{:S(2)}) collective-permute-start(f32[16,64]{1,0:T(8,128)S(1)} %shard_map.85.rest_4_), channel_id=1, source_target_pairs={{0,120},{8,16},{16,8},{24,32},{32,24},{40,48},{48,40},{56,64},{64,... | collective-permute-start | bytes 12296 | tf_op jit(solution)/shard_map/ppermute | solution.py:434
  19.9 5.2 %collective-permute-start.4 = (f32[16,64]{1,0:T(8,128)S(1)}, f32[16,64]{1,0:T(8,128)S(1)}, u32[]{:S(2)}, u32[]{:S(2)}) collective-permute-start(f32[16,64]{1,0:T(8,128)S(1)} %shard_map.85.rest_4_), channel_id=1, source_target_pairs={{0,8},{8,0},{16,24},{24,16},{32,40},{40,32},{48,56},{56,48},{64,72... | collective-permute-start | bytes 12296 | tf_op jit(solution)/shard_map/ppermute | solution.py:434
  26.0 7.6 %collective-permute-start.8 = (f32[48,64]{1,0:T(8,128)S(1)}, f32[48,64]{1,0:T(8,128)S(1)}, u32[]{:S(2)}, u32[]{:S(2)}) collective-permute-start(f32[48,64]{1,0:T(8,128)S(1)} %get-tuple-element.47), channel_id=1, source_target_pairs={{0,8},{8,0},{16,24},{24,16},{32,40},{40,32},{48,56},{56,48},{64,72... | collective-permute-start | bytes 36872 | tf_op jit(solution)/shard_map/ppermute | solution.py:434
  27.0 6.7 %collective-permute-start.9 = (f32[48,64]{1,0:T(8,128)S(1)}, f32[48,64]{1,0:T(8,128)S(1)}, u32[]{:S(2)}, u32[]{:S(2)}) collective-permute-start(f32[48,64]{1,0:T(8,128)S(1)} %get-tuple-element.48), channel_id=1, source_target_pairs={{0,120},{8,16},{16,8},{24,32},{32,24},{40,48},{48,40},{56,64},{64,... | collective-permute-start | bytes 36872 | tf_op jit(solution)/shard_map/ppermute | solution.py:434
  31.1 2.6 %collective-permute-start.10 = (f32[48,64]{1,0:T(8,128)S(1)}, f32[48,64]{1,0:T(8,128)S(1)}, u32[]{:S(2)}, u32[]{:S(2)}) collective-permute-start(f32[48,64]{1,0:T(8,128)S(1)} %get-tuple-element.49), channel_id=1, source_target_pairs={{0,1},{1,0},{2,3},{3,2},{4,5},{5,4},{6,7},{7,6},{8,9},{9,8},{10,11... | collective-permute-start | bytes 36872 | tf_op jit(solution)/shard_map/ppermute | solution.py:434
  32.3 3.5 %collective-permute-start.11 = (f32[48,64]{1,0:T(8,128)S(1)}, f32[48,64]{1,0:T(8,128)S(1)}, u32[]{:S(2)}, u32[]{:S(2)}) collective-permute-start(f32[48,64]{1,0:T(8,128)S(1)} %get-tuple-element.50), channel_id=1, source_target_pairs={{0,7},{1,2},{2,1},{3,4},{4,3},{5,6},{6,5},{7,0},{8,15},{9,10},{10,... | collective-permute-start | bytes 36872 | tf_op jit(solution)/shard_map/ppermute | solution.py:434
  35.8 5.7 %collective-permute-start.15 = (f32[16,64]{1,0:T(8,128)S(1)}, f32[16,64]{1,0:T(8,128)S(1)}, u32[]{:S(2)}, u32[]{:S(2)}) collective-permute-start(f32[16,64]{1,0:T(8,128)S(1)} %shard_map.87.rest_4_), channel_id=1, source_target_pairs={{0,7},{1,2},{2,1},{3,4},{4,3},{5,6},{6,5},{7,0},{8,15},{9,10},{10,... | collective-permute-start | bytes 12296 | tf_op jit(solution)/shard_map/ppermute | solution.py:434
  36.7 4.8 %collective-permute-start.14 = (f32[16,64]{1,0:T(8,128)S(1)}, f32[16,64]{1,0:T(8,128)S(1)}, u32[]{:S(2)}, u32[]{:S(2)}) collective-permute-start(f32[16,64]{1,0:T(8,128)S(1)} %shard_map.87.rest_4_), channel_id=1, source_target_pairs={{0,1},{1,0},{2,3},{3,2},{4,5},{5,4},{6,7},{7,6},{8,9},{9,8},{10,11... | collective-permute-start | bytes 12296 | tf_op jit(solution)/shard_map/ppermute | solution.py:434
  38.4 5.8 %collective-permute-start.13 = (f32[16,64]{1,0:T(8,128)S(1)}, f32[16,64]{1,0:T(8,128)S(1)}, u32[]{:S(2)}, u32[]{:S(2)}) collective-permute-start(f32[16,64]{1,0:T(8,128)S(1)} %shard_map.87.rest_4_), channel_id=1, source_target_pairs={{0,120},{8,16},{16,8},{24,32},{32,24},{40,48},{48,40},{56,64},{64,... | collective-permute-start | bytes 12296 | tf_op jit(solution)/shard_map/ppermute | solution.py:434
  40.1 4.1 %collective-permute-start.12 = (f32[16,64]{1,0:T(8,128)S(1)}, f32[16,64]{1,0:T(8,128)S(1)}, u32[]{:S(2)}, u32[]{:S(2)}) collective-permute-start(f32[16,64]{1,0:T(8,128)S(1)} %shard_map.87.rest_4_), channel_id=1, source_target_pairs={{0,8},{8,0},{16,24},{24,16},{32,40},{40,32},{48,56},{56,48},{64,72... | collective-permute-start | bytes 12296 | tf_op jit(solution)/shard_map/ppermute | solution.py:434
  45.6 4.6 %collective-permute-start.16 = (f32[48,64]{1,0:T(8,128)S(1)}, f32[48,64]{1,0:T(8,128)S(1)}, u32[]{:S(2)}, u32[]{:S(2)}) collective-permute-start(f32[48,64]{1,0:T(8,128)S(1)} %get-tuple-element.57), channel_id=1, source_target_pairs={{0,8},{8,0},{16,24},{24,16},{32,40},{40,32},{48,56},{56,48},{64,72... | collective-permute-start | bytes 36872 | tf_op jit(solution)/shard_map/ppermute | solution.py:434
  45.6 6.0 %collective-permute-start.17 = (f32[48,64]{1,0:T(8,128)S(1)}, f32[48,64]{1,0:T(8,128)S(1)}, u32[]{:S(2)}, u32[]{:S(2)}) collective-permute-start(f32[48,64]{1,0:T(8,128)S(1)} %get-tuple-element.58), channel_id=1, source_target_pairs={{0,120},{8,16},{16,8},{24,32},{32,24},{40,48},{48,40},{56,64},{64,... | collective-permute-start | bytes 36872 | tf_op jit(solution)/shard_map/ppermute | solution.py:434
  47.5 4.1 %collective-permute-start.18 = (f32[48,64]{1,0:T(8,128)S(1)}, f32[48,64]{1,0:T(8,128)S(1)}, u32[]{:S(2)}, u32[]{:S(2)}) collective-permute-start(f32[48,64]{1,0:T(8,128)S(1)} %get-tuple-element.59), channel_id=1, source_target_pairs={{0,1},{1,0},{2,3},{3,2},{4,5},{5,4},{6,7},{7,6},{8,9},{9,8},{10,11... | collective-permute-start | bytes 36872 | tf_op jit(solution)/shard_map/ppermute | solution.py:434
  48.8 3.5 %collective-permute-start.19 = (f32[48,64]{1,0:T(8,128)S(1)}, f32[48,64]{1,0:T(8,128)S(1)}, u32[]{:S(2)}, u32[]{:S(2)}) collective-permute-start(f32[48,64]{1,0:T(8,128)S(1)} %get-tuple-element.60), channel_id=1, source_target_pairs={{0,7},{1,2},{2,1},{3,4},{4,3},{5,6},{6,5},{7,0},{8,15},{9,10},{10,... | collective-permute-start | bytes 36872 | tf_op jit(solution)/shard_map/ppermute | solution.py:434
  52.4 6.7 %collective-permute-start.23 = (f32[16,64]{1,0:T(8,128)S(1)}, f32[16,64]{1,0:T(8,128)S(1)}, u32[]{:S(2)}, u32[]{:S(2)}) collective-permute-start(f32[16,64]{1,0:T(8,128)S(1)} %shard_map.96.rest_4_), channel_id=1, source_target_pairs={{0,7},{1,2},{2,1},{3,4},{4,3},{5,6},{6,5},{7,0},{8,15},{9,10},{10,... | collective-permute-start | bytes 12296 | tf_op jit(solution)/shard_map/ppermute | solution.py:434
  53.7 5.4 %collective-permute-start.22 = (f32[16,64]{1,0:T(8,128)S(1)}, f32[16,64]{1,0:T(8,128)S(1)}, u32[]{:S(2)}, u32[]{:S(2)}) collective-permute-start(f32[16,64]{1,0:T(8,128)S(1)} %shard_map.96.rest_4_), channel_id=1, source_target_pairs={{0,1},{1,0},{2,3},{3,2},{4,5},{5,4},{6,7},{7,6},{8,9},{9,8},{10,11... | collective-permute-start | bytes 12296 | tf_op jit(solution)/shard_map/ppermute | solution.py:434
  56.0 5.8 %collective-permute-start.21 = (f32[16,64]{1,0:T(8,128)S(1)}, f32[16,64]{1,0:T(8,128)S(1)}, u32[]{:S(2)}, u32[]{:S(2)}) collective-permute-start(f32[16,64]{1,0:T(8,128)S(1)} %shard_map.96.rest_4_), channel_id=1, source_target_pairs={{0,120},{8,16},{16,8},{24,32},{32,24},{40,48},{48,40},{56,64},{64,... | collective-permute-start | bytes 12296 | tf_op jit(solution)/shard_map/ppermute | solution.py:434
  58.4 3.4 %collective-permute-start.20 = (f32[16,64]{1,0:T(8,128)S(1)}, f32[16,64]{1,0:T(8,128)S(1)}, u32[]{:S(2)}, u32[]{:S(2)}) collective-permute-start(f32[16,64]{1,0:T(8,128)S(1)} %shard_map.96.rest_4_), channel_id=1, source_target_pairs={{0,8},{8,0},{16,24},{24,16},{32,40},{40,32},{48,56},{56,48},{64,72... | collective-permute-start | bytes 12296 | tf_op jit(solution)/shard_map/ppermute | solution.py:434
where the time goes:
time: 63.7 us; the launch traced here: 63.6 us
  starting transfers between devices  34 us (53%)
  Pallas kernels  18.9 us (30%)
  waiting for transfers between devices  10.3 us (16%)
    ppermute x24, starting transfers between devices, swap(): return lax.ppermute(x, axis, pairs)  34 us
    pallas_call x16, Pallas kernels, call(): pl.pallas_call(kernel, out_shape=shapes, in_specs=specs, out_specs=[pl.Bl...  18.9 us
    ppermute x24, waiting for transfers between devices, swap(): return lax.ppermute(x, axis, pairs)  10.3 us
  transfers between devices with their start and end apart: 24, of which 6 were waited for; matrix products, arithmetic and copies ran while one was open for 0% of the time, Pallas kernels for 19%

commit v1 on v0

--- a/solution.py
+++ b/solution.py
@@ -103,78 +103,72 @@
 
 
 def opening_kernel(shape, me, basis_in, test_in, trace_in, lift_in, state_in, coef_in, *rest):
-    heights_in, tents_in, smat, rows3, lift_row, aux, *rest = rest
+    heights_in, tents_in, rows3, lift_row, aux, *rest = rest
     messages = rest[:SLOTS]
-    vals, basis, test, trace, lift, state, coef, heights, tents, sems = rest[SLOTS:]
-    sources = (basis_in, test_in, trace_in, lift_in, state_in, coef_in, heights_in, tents_in)
-    targets = (basis, test, trace, lift, state, coef, heights, tents)
+    vals, basis, test, trace, lift, state, coef, heights, tents, wide, found, sems = rest[SLOTS:]
+    sources = (test_in, trace_in, basis_in, lift_in, tents_in, state_in, coef_in, heights_in)
+    targets = (test, trace, basis, lift, tents, state, coef, heights)
     copies = [
         pltpu.make_async_copy(source, target, sems.at[k])
         for k, (source, target) in enumerate(zip(sources, targets))
     ]
     for copy in copies:
         copy.start()
-    copies[0].wait()
-    copies[1].wait()
-    s = lax.dot_general(
+    count = trace.shape[0]
+    copies[4].wait()
+    member = members(tents[0:1, :], me[0], shape)
+    for k in range(4):
+        copies[k].wait()
+    row = trace[...].reshape(1, count)
+    rows3[...] = jnp.zeros_like(rows3)
+    rows3[0:1, :] = row
+    for k in (1, 2):
+        tested = jnp.sum(test[...] * row, axis=1, keepdims=True)
+        row = jnp.sum(basis[...] * tested, axis=0, keepdims=True)
+        rows3[k : k + 1, :] = row
+    lift_row[...] = lift[...].reshape(1, count)
+    kappa = jnp.sum(rows3[1:2, :] * lift_row[...], axis=1, keepdims=True)
+    columns = rows3[...].T
+    for k in range(3):
+        wide[k] = jnp.broadcast_to(columns[:, k : k + 1], (count, 128))
+    copies[5].wait()
+    fields = state.shape[0]
+    for pair in range(state.shape[2] // 256):
+        lanes = [slice(pair * 256 + part * 128, pair * 256 + part * 128 + 128) for part in range(2)]
+        totals = {}
+        for group in range(count // 8):
+            lines = slice(group * 8, group * 8 + 8)
+            vector = [wide[k, lines, :] for k in range(3)]
+            for f in range(fields):
+                for part in range(2):
+                    block = state[f, lines, lanes[part]]
+                    for k in range(3):
+                        term = block * vector[k]
+                        held = totals.get((f, part, k))
+                        totals[f, part, k] = term if held is None else held + term
+        for (f, part, k), total in totals.items():
+            found[f, k : k + 1, lanes[part]] = jnp.sum(total, axis=0, keepdims=True)
+    copies[6].wait()
+    copies[7].wait()
+    traces = [found[f, 0:3, :] for f in range(fields)]
+    tent_sums(coef, member, traces, aux, vals, messages, heights, kappa)
+
+
+def powers_kernel(basis, test, rows3, lift, stack, rstack, lcols, kappas, rows, lrows):
+    s1 = lax.dot_general(
         test[...],
         basis[...],
         (((0,), (0,)), ((), ())),
         precision=HIGHEST,
         preferred_element_type=F32,
     )
-    smat[...] = s
-    copies[2].wait()
-    copies[3].wait()
-    t0 = trace[...].reshape(1, s.shape[0])
-    t1 = exact_dot(t0, s)
-    t2 = exact_dot(t1, s)
-    rows3[...] = jnp.zeros_like(rows3)
-    rows3[0:1, :] = t0
-    rows3[1:2, :] = t1
-    rows3[2:3, :] = t2
-    lift_row[...] = lift[...].reshape(1, s.shape[0])
-    kappa = jnp.sum(t1 * lift_row[...], axis=1, keepdims=True)
-    columns = rows3[...].T
-    wide = [
-        jnp.broadcast_to(columns[:, k : k + 1], (columns.shape[0], 128)) for k in range(3)
-    ]
-    copies[7].wait()
-    member = members(tents[0:1, :], me[0], shape)
-    copies[4].wait()
-    fields = state.shape[0]
-    traces = []
-    for f in range(fields):
-        parts = []
-        for lane in range(state.shape[2] // 128):
-            block = state[f, :, lane * 128 : (lane + 1) * 128]
-            parts.append(
-                jnp.concatenate(
-                    [jnp.sum(block * wide[k], axis=0, keepdims=True) for k in range(3)], axis=0
-                )
-            )
-        traces.append(jnp.concatenate(parts, axis=1))
-    copies[5].wait()
-    copies[6].wait()
-    tent_sums(coef, member, traces, aux, vals, messages, heights, kappa)
-
-
-def powers_kernel(smat, rows3, lift, state, stack, lcols, kappas, projections, rows, lrows):
-    basis = smat.shape[0]
-    s1 = smat[...]
+    count = s1.shape[0]
     s2 = exact_dot(s1, s1)
     s3 = exact_dot(s2, s1)
     s4 = exact_dot(s2, s2)
     stack[...] = jnp.zeros_like(stack)
+    rstack[...] = jnp.zeros_like(rstack)
     half = stack.shape[1] // 2
-    for power, matrix in enumerate((s1, s2 / 2.0, s3 / 6.0)):
-        high, low = split(matrix)
-        for side in range(2):
-            stack[power * half : power * half + basis, side * half : side * half + basis] = high
-            stack[
-                (3 + power) * half : (3 + power) * half + basis,
-                side * half : side * half + basis,
-            ] = low
     rows[...] = jnp.zeros_like(rows)
     lrows[...] = jnp.zeros_like(lrows)
     rows[0:2, :] = rows3[0:2, :]
@@ -190,8 +184,30 @@
     kappas[...] = jnp.broadcast_to(
         jnp.sum(rows[...] * lift[...], axis=1, keepdims=True), kappas.shape
     )
-    for f in range(state.shape[0]):
-        projections[f] = exact_dot(rows[...], state[f])
+    row_high, row_low = split(rows[...])
+    for side in range(2):
+        columns = slice(side * half, side * half + count)
+        for power, matrix in enumerate((s1, s2 / 2.0, s3 / 6.0)):
+            high, low = split(matrix)
+            stack[power * half : power * half + count, columns] = high
+            stack[(3 + power) * half : (3 + power) * half + count, columns] = low
+        rstack[0:16, columns] = row_high
+        rstack[16:32, columns] = row_low
+
+
+def projections_kernel(rstack, state, out, packed):
+    fields, count, n_elem = state.shape
+    width = packed.shape[1]
+    half = packed.shape[0] // 2
+    packed[...] = jnp.zeros_like(packed)
+    for f in range(fields):
+        for block in range(n_elem // width):
+            at = slice(block * width, (block + 1) * width)
+            high, low = split(state[f, :, at])
+            packed[0:count, :] = high
+            packed[half : half + count, :] = low
+            product = jnp.dot(rstack[...], packed[...], preferred_element_type=F32)
+            out[f, :, at] = product[:16] + product[16:]
 
 
 def owner_kernel(kappas, own, *rest):
@@ -262,7 +278,8 @@
 
 def element_kernel(shape, level, count, me, tents, coef, heights, kappas, old_aux, proj, *rest):
     tables = rest[:SLOTS]
-    weights_out, proj_out, aux, *messages = rest[SLOTS:-2]
+    weights_out, aux, *messages = rest[SLOTS : 2 * SLOTS + 2]
+    proj_out = rest[2 * SLOTS + 2] if count > 3 else None
     vals, table = rest[-2:]
     fields = coef.shape[0]
     member = members(tents[level : level + 1, :], me[0], shape)
@@ -284,7 +301,8 @@
         for k in range(3):
             value = value + kappas[k : k + count, :] * weights[f][k]
         fresh.append(value)
-        proj_out[f, 0:count, :] = value
+        if proj_out is not None:
+            proj_out[f, 0:count, :] = value
     following = members(tents[level + 1 : level + 2, :], me[0], shape)
     tent_sums(coef, following, [v[0:3] for v in fresh], aux, vals, messages, None, kappas[1:2, :])
 
@@ -380,21 +398,32 @@
 
 def closing_kernel(shape, level, me, tents, coef, heights, kappas, old_aux, lcols, state, *rest):
     tables = rest[:SLOTS]
-    out, table, held, sems = rest[SLOTS:]
+    out, table, held, wide, sems = rest[SLOTS:]
     fields, basis, n_elem = state.shape
     member = members(tents[level : level + 1, :], me[0], shape)
     means = gather([t[...] for t in tables], table, member)
     height = heights[level : level + 1, :]
     weights = lift_weights(coef, height, means, old_aux, kappas)
-    wide = [jnp.broadcast_to(lcols[:, k : k + 1], (basis, 128)) for k in range(3)]
+    for k in range(3):
+        wide[k] = jnp.broadcast_to(lcols[:, k : k + 1], (basis, 128))
     copies = []
     for f in range(fields):
-        for lane in range(n_elem // 128):
-            at = slice(lane * 128, (lane + 1) * 128)
-            value = state[f, :, at]
-            for k in range(3):
-                value = value + wide[k] * weights[f][k][:, at]
-            held[f, :, at] = value
+        for pair in range(n_elem // 256):
+            lanes = [
+                slice(pair * 256 + part * 128, pair * 256 + part * 128 + 128) for part in range(2)
+            ]
+            scale = [
+                [jnp.broadcast_to(weights[f][k][:, at], (8, 128)) for k in range(3)]
+                for at in lanes
+            ]
+            for group in range(basis // 8):
+                lines = slice(group * 8, group * 8 + 8)
+                vector = [wide[k, lines, :] for k in range(3)]
+                for part in range(2):
+                    value = state[f, lines, lanes[part]]
+                    for k in range(3):
+                        value = value + vector[k] * scale[part][k]
+                    held[f, lines, lanes[part]] = value
         copies.append(pltpu.make_async_copy(held.at[f], out.at[f], sems.at[f]))
         copies[-1].start()
     for copy in copies:
@@ -456,9 +485,9 @@
     vals = pltpu.VMEM((ROWS, n_elem), F32)
     table = pltpu.VMEM((BACK, SLOTS * tent_dev), F32)
 
-    smat, rows3, lift, aux, *out = call(
+    rows3, lift, aux, *out = call(
         functools.partial(opening_kernel, shape),
-        [shaped(basis, basis), shaped(8, basis), shaped(1, basis), aux_shape] + message,
+        [shaped(8, basis), shaped(1, basis), aux_shape] + message,
         (
             me,
             *(
@@ -485,22 +514,31 @@
             pltpu.VMEM(coef.shape, F32),
             pltpu.VMEM(tent_height.shape, F32),
             pltpu.VMEM(elem_tent.shape, jnp.int32),
+            pltpu.VMEM((3, basis, 128), F32),
+            pltpu.VMEM((fields, 8, n_elem), F32),
             pltpu.SemaphoreType.DMA((8,)),
         ],
         1,
         space=pltpu.HBM,
     )
-    stack, lcols, kappas, proj = call(
+    stack, rstack, lcols, kappas = call(
         powers_kernel,
         [
             shaped(768, 256, dtype=BF16),
+            shaped(32, 256, dtype=BF16),
             shaped(basis, 16),
             shaped(16, n_elem),
-            shaped(fields, 16, n_elem),
         ],
-        (smat, rows3, lift, state),
+        (basis_quad, test_deriv.T, rows3, lift),
         [pltpu.VMEM((16, basis), F32), pltpu.VMEM((16, basis), F32)],
         flops=100000000,
+    )
+    proj = call(
+        projections_kernel,
+        shaped(fields, 16, n_elem),
+        (rstack, state),
+        [pltpu.VMEM((256, 256), BF16)],
+        flops=300000000,
     )
     blocks = [state] * HALVES
     width = n_elem // HALVES
@@ -532,14 +570,17 @@
         for half in range(HALVES):
             advance_block(level, half)
         if level < levels - 1:
-            weight, proj, aux, *out = call(
+            more = [shaped(fields, 8, n_elem)] if level < levels - 2 else []
+            weight, aux, *out = call(
                 functools.partial(element_kernel, shape, level, 6 - 3 * level),
-                [shaped(fields, 8, n_elem), shaped(fields, 8, n_elem), aux_shape] + message,
+                [shaped(fields, 8, n_elem), aux_shape] + message + more,
                 (me, elem_tent, coef, heights, kappas, aux, proj, *back, means),
                 [vals, table],
                 1,
             )
             weights.append(weight)
+            if more:
+                proj = out.pop()
     values = call(
         lift_kernel,
         shaped(fields, basis, n_elem),
@@ -551,7 +592,12 @@
         functools.partial(closing_kernel, shape, levels - 1),
         shaped(fields, basis, n_elem),
         (me, elem_tent, coef, heights, kappas, aux, lcols, values, *back, means),
-        [table, pltpu.VMEM(state.shape, F32), pltpu.SemaphoreType.DMA((fields,))],
+        [
+            table,
+            pltpu.VMEM(state.shape, F32),
+            pltpu.VMEM((3, basis, 128), F32),
+            pltpu.SemaphoreType.DMA((fields,)),
+        ],
         1,
         out_space=pltpu.HBM,
     )

time: 63.7 us -> 62.7 us (0.984)
  Pallas kernels: 18.9 us -> 17.9 us
    pallas_call x16 -> x17, Pallas kernels: 18.9 us -> 17.9 us  [call(): pl.pallas_call(kernel, out_shape=shapes, in_specs=specs, out_specs=[pl.Bl...]
where the time goes in v1:
time: 62.7 us; the launch traced here: 62.6 us
  starting transfers between devices  33.8 us (54%)
  Pallas kernels  17.9 us (29%)
  waiting for transfers between devices  10.5 us (17%)
    ppermute x24, starting transfers between devices, swap(): return lax.ppermute(x, axis, pairs)  33.8 us
    pallas_call x17, Pallas kernels, call(): pl.pallas_call(kernel, out_shape=shapes, in_specs=specs, out_specs=[pl.Bl...  17.9 us
    ppermute x24, waiting for transfers between devices, swap(): return lax.ppermute(x, axis, pairs)  10.5 us
  transfers between devices with their start and end apart: 24, of which 6 were waited for; matrix products, arithmetic and copies ran while one was open for 0% of the time, Pallas kernels for 19%

profile of v1, /device:TPU:1, one launch (start us, length us, event | category | flops | bytes accessed | tf_op | source)
XLA Modules:
  0.0 62.6 jit_solution(11203268025519086807)
XLA Ops:
  0.0 2.4 %shard_map.82 = (f32[8,120]{1,0:T(8,128)S(1)}, f32[1,120]{1,0:T(1,128)S(1)}, f32[16,512]{1,0:T(8,128)S(1)}, f32[48,64]{1,0:T(8,128)S(1)}, f32[48,64]{1,0:T(8,128...) custom-call(s32[1]{0:T(128)} %bitcast.me, f32[216,120]{1,0:T(8,128)} %basis.1, ...), custom_call_target="tpu_custom_call" | custom-call | flops 1000000 | bytes 1593764 | tf_op jit(solution)/shard_map/pallas_call | solution.py:441
  2.4 0.0 copy-start.2
  2.4 0.0 copy-start.1
  2.5 2.2 %collective-permute-start = (f32[48,64]{1,0:T(8,128)S(1)}, f32[48,64]{1,0:T(8,128)S(1)}, u32[]{:S(2)}, u32[]{:S(2)}) collective-permute-start(f32[48,64]{1,0:T(8,128)S(1)} %get-tuple-element.32), channel_id=1, source_target_pairs={{0,8},{8,0},{16,24},{24,16},{32,40},{40,32},{48,56},{56,48},{64,72... | collective-permute-start | bytes 36872 | tf_op jit(solution)/shard_map/ppermute | solution.py:463
  4.7 5.4 %collective-permute-start.1 = (f32[48,64]{1,0:T(8,128)S(1)}, f32[48,64]{1,0:T(8,128)S(1)}, u32[]{:S(2)}, u32[]{:S(2)}) collective-permute-start(f32[48,64]{1,0:T(8,128)S(1)} %get-tuple-element.33), channel_id=1, source_target_pairs={{0,120},{8,16},{16,8},{24,32},{32,24},{40,48},{48,40},{56,64},{64,... | collective-permute-start | bytes 36872 | tf_op jit(solution)/shard_map/ppermute | solution.py:463
  10.0 1.2 %collective-permute-start.2 = (f32[48,64]{1,0:T(8,128)S(1)}, f32[48,64]{1,0:T(8,128)S(1)}, u32[]{:S(2)}, u32[]{:S(2)}) collective-permute-start(f32[48,64]{1,0:T(8,128)S(1)} %get-tuple-element.34), channel_id=1, source_target_pairs={{0,1},{1,0},{2,3},{3,2},{4,5},{5,4},{6,7},{7,6},{8,9},{9,8},{10,11... | collective-permute-start | bytes 36872 | tf_op jit(solution)/shard_map/ppermute | solution.py:463
  11.3 1.1 %collective-permute-start.3 = (f32[48,64]{1,0:T(8,128)S(1)}, f32[48,64]{1,0:T(8,128)S(1)}, u32[]{:S(2)}, u32[]{:S(2)}) collective-permute-start(f32[48,64]{1,0:T(8,128)S(1)} %get-tuple-element.35), channel_id=1, source_target_pairs={{0,7},{1,2},{2,1},{3,4},{4,3},{5,6},{6,5},{7,0},{8,15},{9,10},{10,... | collective-permute-start | bytes 36872 | tf_op jit(solution)/shard_map/ppermute | solution.py:463
  12.4 2.4 %shard_map.84 = (bf16[768,256]{1,0:T(8,128)(2,1)S(1)}, bf16[32,256]{1,0:T(8,128)(2,1)S(1)}, f32[120,16]{1,0:T(8,128)S(1)}, f32[16,512]{1,0:T(8,128)S(1)}) custom-call(f32[216,120]{1,0:T(8,128)S(1)} %copy-done.3, f32[216,120]{1,0:T(8,128)S(1)} %bitcast.3, f32[8,120]{1,0:T(8,128)S(1)} %get-tuple-element.37.rows3, f32[1,120]{1,0:T(1,128)S(1)} %get-tuple-element.38.lift), custom_call_target="tpu_custom_call" | custom-call | flops 100000000 | bytes 1071328 | tf_op jit(solution)/shard_map/pallas_call | solution.py:441
  14.7 0.3 shard_map.85.proj
  15.1 0.0 collective-permute-done.2.rest_2_
  15.1 0.7 %collective-permute-start.7 = (f32[16,64]{1,0:T(8,128)S(1)}, f32[16,64]{1,0:T(8,128)S(1)}, u32[]{:S(2)}, u32[]{:S(2)}) collective-permute-start(f32[16,64]{1,0:T(8,128)S(1)} %shard_map.86.rest_4_), channel_id=1, source_target_pairs={{0,7},{1,2},{2,1},{3,4},{4,3},{5,6},{6,5},{7,0},{8,15},{9,10},{10,... | collective-permute-start | bytes 12296 | tf_op jit(solution)/shard_map/ppermute | solution.py:463
  15.9 2.8 %collective-permute-start.6 = (f32[16,64]{1,0:T(8,128)S(1)}, f32[16,64]{1,0:T(8,128)S(1)}, u32[]{:S(2)}, u32[]{:S(2)}) collective-permute-start(f32[16,64]{1,0:T(8,128)S(1)} %shard_map.86.rest_4_), channel_id=1, source_target_pairs={{0,1},{1,0},{2,3},{3,2},{4,5},{5,4},{6,7},{7,6},{8,9},{9,8},{10,11... | collective-permute-start | bytes 12296 | tf_op jit(solution)/shard_map/ppermute | solution.py:463
  18.7 0.6 %collective-permute-start.5 = (f32[16,64]{1,0:T(8,128)S(1)}, f32[16,64]{1,0:T(8,128)S(1)}, u32[]{:S(2)}, u32[]{:S(2)}) collective-permute-start(f32[16,64]{1,0:T(8,128)S(1)} %shard_map.86.rest_4_), channel_id=1, source_target_pairs={{0,120},{8,16},{16,8},{24,32},{32,24},{40,48},{48,40},{56,64},{64,... | collective-permute-start | bytes 12296 | tf_op jit(solution)/shard_map/ppermute | solution.py:463
  19.4 0.0 collective-permute-start.4
  19.4 0.3 shard_map.83.heights
  19.7 1.4 %shard_map.93.state = f32[5,120,256]{2,1,0:T(8,128)S(1)} custom-call(f32[5,120,512]{2,1,0:T(8,128)S(1)} %copy-done, f32[5,5,512]{2,1,0:T(8,128)S(1)} %copy-done.1, f32[8,512]{1,0:T(8,128)S(1)} %shard_map.83.heights, bf16[768,256]{1,0:T(8,128)(2,1)S(1)} %get-tuple-element.53.stack), custom_call_target="tpu_custom_call" | custom-call | flops 1000000000 | bytes 2697216 | tf_op jit(solution)/shard_map/pallas_call | solution.py:441
  21.1 1.4 %shard_map.90.state = f32[5,120,256]{2,1,0:T(8,128)S(1)} custom-call(f32[5,120,512]{2,1,0:T(8,128)S(1)} %copy-done, f32[5,5,512]{2,1,0:T(8,128)S(1)} %copy-done.1, f32[8,512]{1,0:T(8,128)S(1)} %shard_map.83.heights, bf16[768,256]{1,0:T(8,128)(2,1)S(1)} %get-tuple-element.53.stack), custom_call_target="tpu_custom_call" | custom-call | flops 1000000000 | bytes 2697216 | tf_op jit(solution)/shard_map/pallas_call | solution.py:441
  22.5 1.4 %shard_map.94.state = f32[5,120,256]{2,1,0:T(8,128)S(1)} custom-call(f32[5,120,256]{2,1,0:T(8,128)S(1)} %shard_map.93.state, f32[5,5,512]{2,1,0:T(8,128)S(1)} %copy-done.1, f32[8,512]{1,0:T(8,128)S(1)} %shard_map.83.heights, bf16[768,256]{1,0:T(8,128)(2,1)S(1)} %get-tuple-element.53.stack), custom_call_target="tpu_custom_call" | custom-call | flops 1000000000 | bytes 2082816 | tf_op jit(solution)/shard_map/pallas_call | solution.py:441
  23.9 0.0 collective-permute-done.7.rest_3_
  23.9 0.0 collective-permute-done.6.rest_2_
  23.9 0.6 collective-permute-done.5.rest_1_
  24.5 0.0 collective-permute-done.4.rest_0_
  24.5 0.9 %shard_map.87 = (f32[5,8,512]{2,1,0:T(8,128)S(1)}, f32[16,512]{1,0:T(8,128)S(1)}, f32[48,64]{1,0:T(8,128)S(1)}, f32[48,64]{1,0:T(8,128)S(1)}, f32[48,64]{1,0:T(8...) custom-call(s32[1]{0:T(128)} %bitcast.me, s32[3,512]{1,0:T(4,128)S(1)} %copy-done.2, ...), custom_call_target="tpu_custom_call" | custom-call | flops 1000000 | bytes 581636 | tf_op jit(solution)/shard_map/pallas_call | solution.py:441
  25.4 1.0 %collective-permute-start.8 = (f32[48,64]{1,0:T(8,128)S(1)}, f32[48,64]{1,0:T(8,128)S(1)}, u32[]{:S(2)}, u32[]{:S(2)}) collective-permute-start(f32[48,64]{1,0:T(8,128)S(1)} %get-tuple-element.45), channel_id=1, source_target_pairs={{0,8},{8,0},{16,24},{24,16},{32,40},{40,32},{48,56},{56,48},{64,72... | collective-permute-start | bytes 36872 | tf_op jit(solution)/shard_map/ppermute | solution.py:463
  26.4 4.1 %collective-permute-start.9 = (f32[48,64]{1,0:T(8,128)S(1)}, f32[48,64]{1,0:T(8,128)S(1)}, u32[]{:S(2)}, u32[]{:S(2)}) collective-permute-start(f32[48,64]{1,0:T(8,128)S(1)} %get-tuple-element.46), channel_id=1, source_target_pairs={{0,120},{8,16},{16,8},{24,32},{32,24},{40,48},{48,40},{56,64},{64,... | collective-permute-start | bytes 36872 | tf_op jit(solution)/shard_map/ppermute | solution.py:463
  30.6 1.1 %collective-permute-start.10 = (f32[48,64]{1,0:T(8,128)S(1)}, f32[48,64]{1,0:T(8,128)S(1)}, u32[]{:S(2)}, u32[]{:S(2)}) collective-permute-start(f32[48,64]{1,0:T(8,128)S(1)} %get-tuple-element.47), channel_id=1, source_target_pairs={{0,1},{1,0},{2,3},{3,2},{4,5},{5,4},{6,7},{7,6},{8,9},{9,8},{10,11... | collective-permute-start | bytes 36872 | tf_op jit(solution)/shard_map/ppermute | solution.py:463
  31.7 1.4 %shard_map.95.rest_1_ = f32[5,120,256]{2,1,0:T(8,128)S(1)} custom-call(f32[5,120,256]{2,1,0:T(8,128)S(1)} %shard_map.94.state, f32[5,5,512]{2,1,0:T(8,128)S(1)} %copy-done.1, f32[8,512]{1,0:T(8,128)S(1)} %shard_map.83.heights, bf16[768,256]{1,0:T(8,128)(2,1)S(1)} %get-tuple-element.53.stack), custom_call_target="tpu_custom_call" | custom-call | flops 1000000000 | bytes 2082816 | tf_op jit(solution)/shard_map/pallas_call | solution.py:441
  33.1 0.0 collective-permute-done.9.rest_1_
  33.1 2.1 %collective-permute-done.11.rest_3_ = f32[48,64]{1,0:T(8,128)S(1)} collective-permute-done((f32[48,64]{1,0:T(8,128)S(1)}, f32[48,64]{1,0:T(8,128)S(1)}, u32[]{:S(2)}, u32[]{:S(2)}) %collective-permute-start.11) | collective-permute-done | bytes 12320 | tf_op jit(solution)/shard_map/ppermute | solution.py:463
  35.3 0.9 %collective-permute-start.15 = (f32[16,64]{1,0:T(8,128)S(1)}, f32[16,64]{1,0:T(8,128)S(1)}, u32[]{:S(2)}, u32[]{:S(2)}) collective-permute-start(f32[16,64]{1,0:T(8,128)S(1)} %shard_map.88.rest_4_), channel_id=1, source_target_pairs={{0,7},{1,2},{2,1},{3,4},{4,3},{5,6},{6,5},{7,0},{8,15},{9,10},{10,... | collective-permute-start | bytes 12296 | tf_op jit(solution)/shard_map/ppermute | solution.py:463
  36.1 1.9 %collective-permute-start.14 = (f32[16,64]{1,0:T(8,128)S(1)}, f32[16,64]{1,0:T(8,128)S(1)}, u32[]{:S(2)}, u32[]{:S(2)}) collective-permute-start(f32[16,64]{1,0:T(8,128)S(1)} %shard_map.88.rest_4_), channel_id=1, source_target_pairs={{0,1},{1,0},{2,3},{3,2},{4,5},{5,4},{6,7},{7,6},{8,9},{9,8},{10,11... | collective-permute-start | bytes 12296 | tf_op jit(solution)/shard_map/ppermute | solution.py:463
  38.0 1.6 %collective-permute-start.13 = (f32[16,64]{1,0:T(8,128)S(1)}, f32[16,64]{1,0:T(8,128)S(1)}, u32[]{:S(2)}, u32[]{:S(2)}) collective-permute-start(f32[16,64]{1,0:T(8,128)S(1)} %shard_map.88.rest_4_), channel_id=1, source_target_pairs={{0,120},{8,16},{16,8},{24,32},{32,24},{40,48},{48,40},{56,64},{64,... | collective-permute-start | bytes 12296 | tf_op jit(solution)/shard_map/ppermute | solution.py:463
  39.6 1.4 %shard_map.91.state = f32[5,120,256]{2,1,0:T(8,128)S(1)} custom-call(f32[5,120,256]{2,1,0:T(8,128)S(1)} %shard_map.90.state, f32[5,5,512]{2,1,0:T(8,128)S(1)} %copy-done.1, f32[8,512]{1,0:T(8,128)S(1)} %shard_map.83.heights, bf16[768,256]{1,0:T(8,128)(2,1)S(1)} %get-tuple-element.53.stack), custom_call_target="tpu_custom_call" | custom-call | flops 1000000000 | bytes 2082816 | tf_op jit(solution)/shard_map/pallas_call | solution.py:441
  41.0 2.9 %collective-permute-done.13.rest_1_ = f32[16,64]{1,0:T(8,128)S(1)} collective-permute-done((f32[16,64]{1,0:T(8,128)S(1)}, f32[16,64]{1,0:T(8,128)S(1)}, u32[]{:S(2)}, u32[]{:S(2)}) %collective-permute-start.13) | collective-permute-done | bytes 4128 | tf_op jit(solution)/shard_map/ppermute | solution.py:463
  43.8 0.9 %shard_map.89 = (f32[5,8,512]{2,1,0:T(8,128)S(1)}, f32[16,512]{1,0:T(8,128)S(1)}, f32[48,64]{1,0:T(8,128)S(1)}, f32[48,64]{1,0:T(8,128)S(1)}, f32[48,64]{1,0:T(8...) custom-call(s32[1]{0:T(128)} %bitcast.me, s32[3,512]{1,0:T(4,128)S(1)} %copy-done.2, f32[5,5,512]{2,1,0:T(8,128)S(1)} %copy-done.1, ...), custom_call_target="tpu_custom_call" | custom-call | flops 1000000 | bytes 417796 | tf_op jit(solution)/shard_map/pallas_call | solution.py:441
  44.7 0.1 collective-permute-start.16
  44.8 1.9 %collective-permute-start.17 = (f32[48,64]{1,0:T(8,128)S(1)}, f32[48,64]{1,0:T(8,128)S(1)}, u32[]{:S(2)}, u32[]{:S(2)}) collective-permute-start(f32[48,64]{1,0:T(8,128)S(1)} %get-tuple-element.56), channel_id=1, source_target_pairs={{0,120},{8,16},{16,8},{24,32},{32,24},{40,48},{48,40},{56,64},{64,... | collective-permute-start | bytes 36872 | tf_op jit(solution)/shard_map/ppermute | solution.py:463
  46.6 1.4 %collective-permute-start.18 = (f32[48,64]{1,0:T(8,128)S(1)}, f32[48,64]{1,0:T(8,128)S(1)}, u32[]{:S(2)}, u32[]{:S(2)}) collective-permute-start(f32[48,64]{1,0:T(8,128)S(1)} %get-tuple-element.57), channel_id=1, source_target_pairs={{0,1},{1,0},{2,3},{3,2},{4,5},{5,4},{6,7},{7,6},{8,9},{9,8},{10,11... | collective-permute-start | bytes 36872 | tf_op jit(solution)/shard_map/ppermute | solution.py:463
  48.1 0.0 collective-permute-start.19
  48.1 1.4 %shard_map.92.rest_0_ = f32[5,120,256]{2,1,0:T(8,128)S(1)} custom-call(f32[5,120,256]{2,1,0:T(8,128)S(1)} %shard_map.91.state, f32[5,5,512]{2,1,0:T(8,128)S(1)} %copy-done.1, f32[8,512]{1,0:T(8,128)S(1)} %shard_map.83.heights, bf16[768,256]{1,0:T(8,128)(2,1)S(1)} %get-tuple-element.53.stack), custom_call_target="tpu_custom_call" | custom-call | flops 1000000000 | bytes 2082816 | tf_op jit(solution)/shard_map/pallas_call | solution.py:441
  49.5 1.4 %collective-permute-done.17.rest_1_ = f32[48,64]{1,0:T(8,128)S(1)} collective-permute-done((f32[48,64]{1,0:T(8,128)S(1)}, f32[48,64]{1,0:T(8,128)S(1)}, u32[]{:S(2)}, u32[]{:S(2)}) %collective-permute-start.17) | collective-permute-done | bytes 12320 | tf_op jit(solution)/shard_map/ppermute | solution.py:463
  50.9 0.7 %collective-permute-done.19.rest_3_ = f32[48,64]{1,0:T(8,128)S(1)} collective-permute-done((f32[48,64]{1,0:T(8,128)S(1)}, f32[48,64]{1,0:T(8,128)S(1)}, u32[]{:S(2)}, u32[]{:S(2)}) %collective-permute-start.19) | collective-permute-done | bytes 12320 | tf_op jit(solution)/shard_map/ppermute | solution.py:463
  51.6 1.1 %collective-permute-start.23 = (f32[16,64]{1,0:T(8,128)S(1)}, f32[16,64]{1,0:T(8,128)S(1)}, u32[]{:S(2)}, u32[]{:S(2)}) collective-permute-start(f32[16,64]{1,0:T(8,128)S(1)} %shard_map.97.rest_4_), channel_id=1, source_target_pairs={{0,7},{1,2},{2,1},{3,4},{4,3},{5,6},{6,5},{7,0},{8,15},{9,10},{10,... | collective-permute-start | bytes 12296 | tf_op jit(solution)/shard_map/ppermute | solution.py:463
  52.7 2.3 %collective-permute-start.22 = (f32[16,64]{1,0:T(8,128)S(1)}, f32[16,64]{1,0:T(8,128)S(1)}, u32[]{:S(2)}, u32[]{:S(2)}) collective-permute-start(f32[16,64]{1,0:T(8,128)S(1)} %shard_map.97.rest_4_), channel_id=1, source_target_pairs={{0,1},{1,0},{2,3},{3,2},{4,5},{5,4},{6,7},{7,6},{8,9},{9,8},{10,11... | collective-permute-start | bytes 12296 | tf_op jit(solution)/shard_map/ppermute | solution.py:463
  55.0 2.4 %collective-permute-start.21 = (f32[16,64]{1,0:T(8,128)S(1)}, f32[16,64]{1,0:T(8,128)S(1)}, u32[]{:S(2)}, u32[]{:S(2)}) collective-permute-start(f32[16,64]{1,0:T(8,128)S(1)} %shard_map.97.rest_4_), channel_id=1, source_target_pairs={{0,120},{8,16},{16,8},{24,32},{32,24},{40,48},{48,40},{56,64},{64,... | collective-permute-start | bytes 12296 | tf_op jit(solution)/shard_map/ppermute | solution.py:463
  57.4 0.7 %shard_map.96.state = f32[5,120,512]{2,1,0:T(8,128)S(1)} custom-call(f32[5,5,512]{2,1,0:T(8,128)S(1)} %copy-done.1, f32[8,512]{1,0:T(8,128)S(1)} %shard_map.83.heights, f32[5,8,512]{2,1,0:T(8,128)S(1)} %get-tuple-element.51.weights0, f32[5,8,512]{2,1,0:T(8,128)S(1)} %get-tuple-element.52.weights1, f32[120,16]{1,0:T(8,128)S(1)} %get-tuple-element.50.lcols, ...), custom_call_target="tpu_custom_call" | custom-call | flops 100000000 | bytes 2696704 | tf_op jit(solution)/shard_map/pallas_call | solution.py:441
  58.1 2.7 %collective-permute-done.21.rest_1_ = f32[16,64]{1,0:T(8,128)S(1)} collective-permute-done((f32[16,64]{1,0:T(8,128)S(1)}, f32[16,64]{1,0:T(8,128)S(1)}, u32[]{:S(2)}, u32[]{:S(2)}) %collective-permute-start.21) | collective-permute-done | bytes 4128 | tf_op jit(solution)/shard_map/ppermute | solution.py:463
  60.8 1.6 %shard_map.98 = f32[5,120,512]{2,1,0:T(8,128)} custom-call(s32[1]{0:T(128)} %bitcast.me, s32[3,512]{1,0:T(4,128)S(1)} %copy-done.2, f32[5,5,512]{2,1,0:T(8,128)S(1)} %copy-done.1, f32[8,512]{1,0:T(8,128)S(1)} %shard_map.83.heights, f32[16,512]{1,0:T(8,128)S(1)} %get-tuple-element.39.kappas, f32[16,512]{1,0:T(8,128)S(1)} %get-tuple-element.49.old_aux, ...), custom_call_target="tpu_custom_call" | custom-call | flops 1000000 | bytes 2625028 | tf_op jit(solution)/shard_map/pallas_call | solution.py:441
  (27 shorter events, 0.1 us)
Async XLA Ops:
  0.0 14.7 %copy-start = (f32[5,120,512]{2,1,0:T(8,128)S(1)}, f32[5,120,512]{2,1,0:T(8,128)}, u32[]{:S(2)}) copy-start(f32[5,120,512]{2,1,0:T(8,128)} %state.5) | copy-start | bytes 3686404
  0.0 12.4 %copy-start.3 = (f32[216,120]{1,0:T(8,128)S(1)}, f32[216,120]{1,0:T(8,128)}, u32[]{:S(2)}) copy-start(f32[216,120]{1,0:T(8,128)} %basis.1) | copy-start | bytes 311044
  0.0 12.4 %copy-start.4 = (f32[120,216]{0,1:T(8,128)S(1)}, f32[120,216]{0,1:T(8,128)}, u32[]{:S(2)}) copy-start(f32[120,216]{0,1:T(8,128)} %param.11) | copy-start | bytes 311044
  2.4 16.9 %copy-start.2 = (s32[3,512]{1,0:T(4,128)S(1)}, s32[3,512]{1,0:T(4,128)}, u32[]{:S(2)}) copy-start(s32[3,512]{1,0:T(4,128)} %tents.7) | copy-start | bytes 18436
  2.4 17.2 %copy-start.1 = (f32[5,5,512]{2,1,0:T(8,128)S(1)}, f32[5,5,512]{2,1,0:T(8,128)}, u32[]{:S(2)}) copy-start(f32[5,5,512]{2,1,0:T(8,128)} %coef.19) | copy-start | bytes 153604
  2.5 12.6 %collective-permute-start = (f32[48,64]{1,0:T(8,128)S(1)}, f32[48,64]{1,0:T(8,128)S(1)}, u32[]{:S(2)}, u32[]{:S(2)}) collective-permute-start(f32[48,64]{1,0:T(8,128)S(1)} %get-tuple-element.32), channel_id=1, source_target_pairs={{0,8},{8,0},{16,24},{24,16},{32,40},{40,32},{48,56},{56,48},{64,72... | collective-permute-start | bytes 36872 | tf_op jit(solution)/shard_map/ppermute | solution.py:463
  4.7 10.4 %collective-permute-start.1 = (f32[48,64]{1,0:T(8,128)S(1)}, f32[48,64]{1,0:T(8,128)S(1)}, u32[]{:S(2)}, u32[]{:S(2)}) collective-permute-start(f32[48,64]{1,0:T(8,128)S(1)} %get-tuple-element.33), channel_id=1, source_target_pairs={{0,120},{8,16},{16,8},{24,32},{32,24},{40,48},{48,40},{56,64},{64,... | collective-permute-start | bytes 36872 | tf_op jit(solution)/shard_map/ppermute | solution.py:463
  10.0 5.1 %collective-permute-start.2 = (f32[48,64]{1,0:T(8,128)S(1)}, f32[48,64]{1,0:T(8,128)S(1)}, u32[]{:S(2)}, u32[]{:S(2)}) collective-permute-start(f32[48,64]{1,0:T(8,128)S(1)} %get-tuple-element.34), channel_id=1, source_target_pairs={{0,1},{1,0},{2,3},{3,2},{4,5},{5,4},{6,7},{7,6},{8,9},{9,8},{10,11... | collective-permute-start | bytes 36872 | tf_op jit(solution)/shard_map/ppermute | solution.py:463
  11.3 3.8 %collective-permute-start.3 = (f32[48,64]{1,0:T(8,128)S(1)}, f32[48,64]{1,0:T(8,128)S(1)}, u32[]{:S(2)}, u32[]{:S(2)}) collective-permute-start(f32[48,64]{1,0:T(8,128)S(1)} %get-tuple-element.35), channel_id=1, source_target_pairs={{0,7},{1,2},{2,1},{3,4},{4,3},{5,6},{6,5},{7,0},{8,15},{9,10},{10,... | collective-permute-start | bytes 36872 | tf_op jit(solution)/shard_map/ppermute | solution.py:463
  15.1 8.8 %collective-permute-start.7 = (f32[16,64]{1,0:T(8,128)S(1)}, f32[16,64]{1,0:T(8,128)S(1)}, u32[]{:S(2)}, u32[]{:S(2)}) collective-permute-start(f32[16,64]{1,0:T(8,128)S(1)} %shard_map.86.rest_4_), channel_id=1, source_target_pairs={{0,7},{1,2},{2,1},{3,4},{4,3},{5,6},{6,5},{7,0},{8,15},{9,10},{10,... | collective-permute-start | bytes 12296 | tf_op jit(solution)/shard_map/ppermute | solution.py:463
  15.9 8.1 %collective-permute-start.6 = (f32[16,64]{1,0:T(8,128)S(1)}, f32[16,64]{1,0:T(8,128)S(1)}, u32[]{:S(2)}, u32[]{:S(2)}) collective-permute-start(f32[16,64]{1,0:T(8,128)S(1)} %shard_map.86.rest_4_), channel_id=1, source_target_pairs={{0,1},{1,0},{2,3},{3,2},{4,5},{5,4},{6,7},{7,6},{8,9},{9,8},{10,11... | collective-permute-start | bytes 12296 | tf_op jit(solution)/shard_map/ppermute | solution.py:463
  18.7 5.8 %collective-permute-start.5 = (f32[16,64]{1,0:T(8,128)S(1)}, f32[16,64]{1,0:T(8,128)S(1)}, u32[]{:S(2)}, u32[]{:S(2)}) collective-permute-start(f32[16,64]{1,0:T(8,128)S(1)} %shard_map.86.rest_4_), channel_id=1, source_target_pairs={{0,120},{8,16},{16,8},{24,32},{32,24},{40,48},{48,40},{56,64},{64,... | collective-permute-start | bytes 12296 | tf_op jit(solution)/shard_map/ppermute | solution.py:463
  19.4 5.2 %collective-permute-start.4 = (f32[16,64]{1,0:T(8,128)S(1)}, f32[16,64]{1,0:T(8,128)S(1)}, u32[]{:S(2)}, u32[]{:S(2)}) collective-permute-start(f32[16,64]{1,0:T(8,128)S(1)} %shard_map.86.rest_4_), channel_id=1, source_target_pairs={{0,8},{8,0},{16,24},{24,16},{32,40},{40,32},{48,56},{56,48},{64,72... | collective-permute-start | bytes 12296 | tf_op jit(solution)/shard_map/ppermute | solution.py:463
  25.4 7.6 %collective-permute-start.8 = (f32[48,64]{1,0:T(8,128)S(1)}, f32[48,64]{1,0:T(8,128)S(1)}, u32[]{:S(2)}, u32[]{:S(2)}) collective-permute-start(f32[48,64]{1,0:T(8,128)S(1)} %get-tuple-element.45), channel_id=1, source_target_pairs={{0,8},{8,0},{16,24},{24,16},{32,40},{40,32},{48,56},{56,48},{64,72... | collective-permute-start | bytes 36872 | tf_op jit(solution)/shard_map/ppermute | solution.py:463
  26.4 6.7 %collective-permute-start.9 = (f32[48,64]{1,0:T(8,128)S(1)}, f32[48,64]{1,0:T(8,128)S(1)}, u32[]{:S(2)}, u32[]{:S(2)}) collective-permute-start(f32[48,64]{1,0:T(8,128)S(1)} %get-tuple-element.46), channel_id=1, source_target_pairs={{0,120},{8,16},{16,8},{24,32},{32,24},{40,48},{48,40},{56,64},{64,... | collective-permute-start | bytes 36872 | tf_op jit(solution)/shard_map/ppermute | solution.py:463
  30.6 2.5 %collective-permute-start.10 = (f32[48,64]{1,0:T(8,128)S(1)}, f32[48,64]{1,0:T(8,128)S(1)}, u32[]{:S(2)}, u32[]{:S(2)}) collective-permute-start(f32[48,64]{1,0:T(8,128)S(1)} %get-tuple-element.47), channel_id=1, source_target_pairs={{0,1},{1,0},{2,3},{3,2},{4,5},{5,4},{6,7},{7,6},{8,9},{9,8},{10,11... | collective-permute-start | bytes 36872 | tf_op jit(solution)/shard_map/ppermute | solution.py:463
  31.7 3.5 %collective-permute-start.11 = (f32[48,64]{1,0:T(8,128)S(1)}, f32[48,64]{1,0:T(8,128)S(1)}, u32[]{:S(2)}, u32[]{:S(2)}) collective-permute-start(f32[48,64]{1,0:T(8,128)S(1)} %get-tuple-element.48), channel_id=1, source_target_pairs={{0,7},{1,2},{2,1},{3,4},{4,3},{5,6},{6,5},{7,0},{8,15},{9,10},{10,... | collective-permute-start | bytes 36872 | tf_op jit(solution)/shard_map/ppermute | solution.py:463
  35.3 5.7 %collective-permute-start.15 = (f32[16,64]{1,0:T(8,128)S(1)}, f32[16,64]{1,0:T(8,128)S(1)}, u32[]{:S(2)}, u32[]{:S(2)}) collective-permute-start(f32[16,64]{1,0:T(8,128)S(1)} %shard_map.88.rest_4_), channel_id=1, source_target_pairs={{0,7},{1,2},{2,1},{3,4},{4,3},{5,6},{6,5},{7,0},{8,15},{9,10},{10,... | collective-permute-start | bytes 12296 | tf_op jit(solution)/shard_map/ppermute | solution.py:463
  36.1 4.8 %collective-permute-start.14 = (f32[16,64]{1,0:T(8,128)S(1)}, f32[16,64]{1,0:T(8,128)S(1)}, u32[]{:S(2)}, u32[]{:S(2)}) collective-permute-start(f32[16,64]{1,0:T(8,128)S(1)} %shard_map.88.rest_4_), channel_id=1, source_target_pairs={{0,1},{1,0},{2,3},{3,2},{4,5},{5,4},{6,7},{7,6},{8,9},{9,8},{10,11... | collective-permute-start | bytes 12296 | tf_op jit(solution)/shard_map/ppermute | solution.py:463
  38.0 5.8 %collective-permute-start.13 = (f32[16,64]{1,0:T(8,128)S(1)}, f32[16,64]{1,0:T(8,128)S(1)}, u32[]{:S(2)}, u32[]{:S(2)}) collective-permute-start(f32[16,64]{1,0:T(8,128)S(1)} %shard_map.88.rest_4_), channel_id=1, source_target_pairs={{0,120},{8,16},{16,8},{24,32},{32,24},{40,48},{48,40},{56,64},{64,... | collective-permute-start | bytes 12296 | tf_op jit(solution)/shard_map/ppermute | solution.py:463
  39.6 4.3 %collective-permute-start.12 = (f32[16,64]{1,0:T(8,128)S(1)}, f32[16,64]{1,0:T(8,128)S(1)}, u32[]{:S(2)}, u32[]{:S(2)}) collective-permute-start(f32[16,64]{1,0:T(8,128)S(1)} %shard_map.88.rest_4_), channel_id=1, source_target_pairs={{0,8},{8,0},{16,24},{24,16},{32,40},{40,32},{48,56},{56,48},{64,72... | collective-permute-start | bytes 12296 | tf_op jit(solution)/shard_map/ppermute | solution.py:463
  44.7 4.7 %collective-permute-start.16 = (f32[48,64]{1,0:T(8,128)S(1)}, f32[48,64]{1,0:T(8,128)S(1)}, u32[]{:S(2)}, u32[]{:S(2)}) collective-permute-start(f32[48,64]{1,0:T(8,128)S(1)} %get-tuple-element.55), channel_id=1, source_target_pairs={{0,8},{8,0},{16,24},{24,16},{32,40},{40,32},{48,56},{56,48},{64,72... | collective-permute-start | bytes 36872 | tf_op jit(solution)/shard_map/ppermute | solution.py:463
  44.8 6.1 %collective-permute-start.17 = (f32[48,64]{1,0:T(8,128)S(1)}, f32[48,64]{1,0:T(8,128)S(1)}, u32[]{:S(2)}, u32[]{:S(2)}) collective-permute-start(f32[48,64]{1,0:T(8,128)S(1)} %get-tuple-element.56), channel_id=1, source_target_pairs={{0,120},{8,16},{16,8},{24,32},{32,24},{40,48},{48,40},{56,64},{64,... | collective-permute-start | bytes 36872 | tf_op jit(solution)/shard_map/ppermute | solution.py:463
  46.6 4.2 %collective-permute-start.18 = (f32[48,64]{1,0:T(8,128)S(1)}, f32[48,64]{1,0:T(8,128)S(1)}, u32[]{:S(2)}, u32[]{:S(2)}) collective-permute-start(f32[48,64]{1,0:T(8,128)S(1)} %get-tuple-element.57), channel_id=1, source_target_pairs={{0,1},{1,0},{2,3},{3,2},{4,5},{5,4},{6,7},{7,6},{8,9},{9,8},{10,11... | collective-permute-start | bytes 36872 | tf_op jit(solution)/shard_map/ppermute | solution.py:463
  48.1 3.5 %collective-permute-start.19 = (f32[48,64]{1,0:T(8,128)S(1)}, f32[48,64]{1,0:T(8,128)S(1)}, u32[]{:S(2)}, u32[]{:S(2)}) collective-permute-start(f32[48,64]{1,0:T(8,128)S(1)} %get-tuple-element.58), channel_id=1, source_target_pairs={{0,7},{1,2},{2,1},{3,4},{4,3},{5,6},{6,5},{7,0},{8,15},{9,10},{10,... | collective-permute-start | bytes 36872 | tf_op jit(solution)/shard_map/ppermute | solution.py:463
  51.6 6.5 %collective-permute-start.23 = (f32[16,64]{1,0:T(8,128)S(1)}, f32[16,64]{1,0:T(8,128)S(1)}, u32[]{:S(2)}, u32[]{:S(2)}) collective-permute-start(f32[16,64]{1,0:T(8,128)S(1)} %shard_map.97.rest_4_), channel_id=1, source_target_pairs={{0,7},{1,2},{2,1},{3,4},{4,3},{5,6},{6,5},{7,0},{8,15},{9,10},{10,... | collective-permute-start | bytes 12296 | tf_op jit(solution)/shard_map/ppermute | solution.py:463
  52.7 5.4 %collective-permute-start.22 = (f32[16,64]{1,0:T(8,128)S(1)}, f32[16,64]{1,0:T(8,128)S(1)}, u32[]{:S(2)}, u32[]{:S(2)}) collective-permute-start(f32[16,64]{1,0:T(8,128)S(1)} %shard_map.97.rest_4_), channel_id=1, source_target_pairs={{0,1},{1,0},{2,3},{3,2},{4,5},{5,4},{6,7},{7,6},{8,9},{9,8},{10,11... | collective-permute-start | bytes 12296 | tf_op jit(solution)/shard_map/ppermute | solution.py:463
  55.0 5.8 %collective-permute-start.21 = (f32[16,64]{1,0:T(8,128)S(1)}, f32[16,64]{1,0:T(8,128)S(1)}, u32[]{:S(2)}, u32[]{:S(2)}) collective-permute-start(f32[16,64]{1,0:T(8,128)S(1)} %shard_map.97.rest_4_), channel_id=1, source_target_pairs={{0,120},{8,16},{16,8},{24,32},{32,24},{40,48},{48,40},{56,64},{64,... | collective-permute-start | bytes 12296 | tf_op jit(solution)/shard_map/ppermute | solution.py:463
  57.4 3.4 %collective-permute-start.20 = (f32[16,64]{1,0:T(8,128)S(1)}, f32[16,64]{1,0:T(8,128)S(1)}, u32[]{:S(2)}, u32[]{:S(2)}) collective-permute-start(f32[16,64]{1,0:T(8,128)S(1)} %shard_map.97.rest_4_), channel_id=1, source_target_pairs={{0,8},{8,0},{16,24},{24,16},{32,40},{40,32},{48,56},{56,48},{64,72... | collective-permute-start | bytes 12296 | tf_op jit(solution)/shard_map/ppermute | solution.py:463

commit v2 on v1

--- a/solution.py
+++ b/solution.py
@@ -24,12 +24,6 @@
 
 def exact_dot(left, right):
     return jnp.dot(left, right, precision=HIGHEST, preferred_element_type=F32)
-
-
-def dot_rows(left, right):
-    return lax.dot_general(
-        left, right, (((1,), (1,)), ((), ())), precision=HIGHEST, preferred_element_type=F32
-    )
 
 
 def partners(index, size):
@@ -95,17 +89,20 @@
         both, member, (((1,), (1,)), ((), ())), preferred_element_type=F32
     )
     sums = sums[:ROWS] + sums[ROWS:]
-    tent_dev = messages[0].shape[1]
+    rows, tent_dev = messages[0].shape[0], messages[0].shape[1] // 2
     for slot in range(SLOTS):
-        messages[slot][...] = sums[:, slot * tent_dev : (slot + 1) * tent_dev]
+        columns = slice(slot * tent_dev, (slot + 1) * tent_dev)
+        messages[slot][:, :tent_dev] = sums[:rows, columns]
+        messages[slot][:, tent_dev:] = sums[rows:, columns]
         if heights is not None:
-            messages[slot][41:44, :] = heights[...]
+            messages[slot][41 - rows : 44 - rows, tent_dev:] = heights[...]
 
 
 def opening_kernel(shape, me, basis_in, test_in, trace_in, lift_in, state_in, coef_in, *rest):
     heights_in, tents_in, rows3, lift_row, aux, *rest = rest
     messages = rest[:SLOTS]
-    vals, basis, test, trace, lift, state, coef, heights, tents, wide, found, sems = rest[SLOTS:]
+    basis, test, state, coef, tents, *rest = rest[SLOTS:]
+    vals, trace, lift, heights, wide, found, sems = rest
     sources = (test_in, trace_in, basis_in, lift_in, tents_in, state_in, coef_in, heights_in)
     targets = (test, trace, basis, lift, tents, state, coef, heights)
     copies = [
@@ -154,7 +151,10 @@
     tent_sums(coef, member, traces, aux, vals, messages, heights, kappa)
 
 
-def powers_kernel(basis, test, rows3, lift, stack, rstack, lcols, kappas, rows, lrows):
+def powers_kernel(basis, test, rows3, lift, stack, rstack, lcols, kappas, rows, left, right):
+    count = basis.shape[1]
+    first, second = slice(8, 8 + count), slice(8 + count, 8 + 2 * count)
+    extra = right.shape[1]
     s1 = lax.dot_general(
         test[...],
         basis[...],
@@ -162,28 +162,44 @@
         precision=HIGHEST,
         preferred_element_type=F32,
     )
-    count = s1.shape[0]
-    s2 = exact_dot(s1, s1)
-    s3 = exact_dot(s2, s1)
-    s4 = exact_dot(s2, s2)
     stack[...] = jnp.zeros_like(stack)
     rstack[...] = jnp.zeros_like(rstack)
-    half = stack.shape[1] // 2
     rows[...] = jnp.zeros_like(rows)
-    lrows[...] = jnp.zeros_like(lrows)
-    rows[0:2, :] = rows3[0:2, :]
-    rows[2:4, :] = exact_dot(rows3[0:2, :], s2)
-    rows[4:8, :] = exact_dot(rows[0:4, :], s4)
-    rows[8:9, :] = exact_dot(rows[4:5, :], s4)
-    lrows[0:1, :] = lift[...]
-    lrows[1:2, :] = dot_rows(lift[...], s1)
-    lrows[2:4, :] = dot_rows(lrows[0:2, :], s2)
-    lrows[4:8, :] = dot_rows(lrows[0:4, :], s4)
-    lrows[8:9, :] = dot_rows(lrows[4:5, :], s4)
-    lcols[...] = lrows[...].T
+    left[...] = jnp.zeros_like(left)
+    right[...] = jnp.zeros_like(right)
+    lcols[...] = jnp.zeros_like(lcols)
+    rows[8:9, :] = lift[...]
+    lcols[:, 0:8] = rows[8:16, :].T
+    rows[0:3, :] = rows3[0:3, :]
+    left[0:8, :] = rows[0:8, :]
+    left[first, :] = s1
+    right[:, 0:count] = s1
+    right[:, count:extra] = lcols[:, 0:8]
+    product = exact_dot(left[0 : 8 + count, :], right[...])
+    s2 = product[first, 0:count]
+    rows[3:4, :] = product[2:3, 0:count]
+    lcols[:, 1:2] = product[first, count : count + 1]
+    left[0:8, :] = rows[0:8, :]
+    left[second, :] = s2
+    right[:, 0:count] = s2
+    right[:, count:extra] = lcols[:, 0:8]
+    product = exact_dot(left[0 : 8 + 2 * count, :], right[...])
+    s3 = product[first, 0:count]
+    s4 = product[second, 0:count]
+    rows[4:6, :] = product[2:4, 0:count]
+    lcols[:, 2:4] = product[second, count : count + 2]
+    left[0:4, :] = rows[2:6, :]
+    left[first, :] = s4
+    right[:, 0:count] = s4
+    right[:, count:extra] = lcols[:, 0:8]
+    product = exact_dot(left[0 : 8 + count, :], right[...])
+    rows[6:9, :] = product[0:3, 0:count]
+    lcols[:, 4:8] = product[first, count : count + 4]
+    lcols[:, 8:9] = jnp.sum(product[first, 0:count] * lift[...], axis=1, keepdims=True)
     kappas[...] = jnp.broadcast_to(
         jnp.sum(rows[...] * lift[...], axis=1, keepdims=True), kappas.shape
     )
+    half = rstack.shape[1] // 2
     row_high, row_low = split(rows[...])
     for side in range(2):
         columns = slice(side * half, side * half + count)
@@ -215,6 +231,7 @@
     total = own[...]
     for ref in received:
         total = total + ref[...]
+    total = jnp.concatenate([total[:, : out.shape[1]], total[:, out.shape[1] :]], axis=0)
     mean = total / jnp.maximum(total[40:41], 1.0)
     first = mean[0:5]
     out[...] = jnp.zeros_like(out)
@@ -226,7 +243,7 @@
 
 
 def gather(tables, table, member):
-    tent_dev = tables[0].shape[1]
+    tent_dev = table.shape[1] // SLOTS
     for slot in range(SLOTS):
         table[:, slot * tent_dev : (slot + 1) * tent_dev] = tables[slot]
     high, low = split(table[...])
@@ -237,12 +254,29 @@
     return found[:count] + found[count:]
 
 
-def heights_kernel(shape, me, tents, *rest):
-    *messages, out, table = rest
-    for level in range(tents.shape[0]):
-        member = members(tents[level : level + 1, :], me[0], shape)
-        found = gather([m[32:48, :] for m in messages], table, member)
+def members_kernel(shape, me, tents, *outs):
+    for level, out in enumerate(outs):
+        out[...] = members(tents[level : level + 1, :], me[0], shape)
+
+
+def heights_kernel(messages, memberships, out, table):
+    out[...] = jnp.zeros_like(out)
+    half = messages[0].shape[1] // 2
+    for level, member in enumerate(memberships):
+        found = gather([m[8:24, half:] for m in messages], table, member[...])
         out[level : level + 1, :] = found[9 + level : 10 + level]
+
+
+def drift_kernel(level, count, coef, heights, proj, out):
+    fields = coef.shape[0]
+    height = heights[level : level + 1, :]
+    state = mix(coef, [proj[f, 3 : 3 + count, :] for f in range(fields)])
+    state = [proj[f, 2 : 2 + count, :] + height / 3.0 * state[f] for f in range(fields)]
+    state = mix(coef, state)
+    state = [proj[f, 1 : 1 + count, :] + height / 2.0 * state[f] for f in range(fields)]
+    state = mix(coef, state)
+    for f in range(fields):
+        out[f, 0:count, :] = proj[f, 0:count, :] + height * state[f]
 
 
 def lift_weights(coef, height, means, aux, kappas):
@@ -253,8 +287,9 @@
     second = [
         means[5 + f : 6 + f] - aux[5 + f : 6 + f, :] - kappa0 * first[f] for f in range(fields)
     ]
-    moved_first = mix(coef, first)
-    moved_second = mix(coef, second)
+    moved = mix(coef, [jnp.concatenate([first[f], second[f]], axis=0) for f in range(fields)])
+    moved_first = [m[0:1] for m in moved]
+    moved_second = [m[1:2] for m in moved]
     moved_twice = mix(coef, moved_first)
     half = height * height / 2.0
     sixth = height * height * height / 6.0
@@ -276,90 +311,116 @@
     return weights
 
 
-def element_kernel(shape, level, count, me, tents, coef, heights, kappas, old_aux, proj, *rest):
+def element_kernel(level, count, coef, heights, kappas, old_aux, drift, member, following, *rest):
     tables = rest[:SLOTS]
     weights_out, aux, *messages = rest[SLOTS : 2 * SLOTS + 2]
     proj_out = rest[2 * SLOTS + 2] if count > 3 else None
     vals, table = rest[-2:]
     fields = coef.shape[0]
-    member = members(tents[level : level + 1, :], me[0], shape)
-    means = gather([t[...] for t in tables], table, member)
+    means = gather([t[...] for t in tables], table, member[...])
     height = heights[level : level + 1, :]
     weights = lift_weights(coef, height, means, old_aux, kappas)
     weights_out[...] = jnp.zeros_like(weights_out)
+    fresh = []
     for f in range(fields):
         for k in range(3):
             weights_out[f, k : k + 1, :] = weights[f][k]
-    state = mix(coef, [proj[f, 3 : 3 + count, :] for f in range(fields)])
-    state = [proj[f, 2 : 2 + count, :] + height / 3.0 * state[f] for f in range(fields)]
-    state = mix(coef, state)
-    state = [proj[f, 1 : 1 + count, :] + height / 2.0 * state[f] for f in range(fields)]
-    state = mix(coef, state)
-    fresh = []
-    for f in range(fields):
-        value = proj[f, 0:count, :] + height * state[f]
+        value = drift[f, 0:count, :]
         for k in range(3):
             value = value + kappas[k : k + count, :] * weights[f][k]
         fresh.append(value)
         if proj_out is not None:
             proj_out[f, 0:count, :] = value
-    following = members(tents[level + 1 : level + 2, :], me[0], shape)
-    tent_sums(coef, following, [v[0:3] for v in fresh], aux, vals, messages, None, kappas[1:2, :])
-
-
-def level_kernel(level, offset, state, coef, heights, stack, out, packed, powers):
-    fields, basis, width = out.shape
-    half = packed.shape[0] // 2
-    base = offset if state.shape[2] > width else 0
+    tent_sums(
+        coef,
+        following[...],
+        [v[0:3] for v in fresh],
+        aux,
+        vals,
+        messages,
+        None,
+        kappas[1:2, :],
+    )
+
+
+def poly_kernel(steps, resumed, state, coef, heights, stack, *rest):
+    rest = list(rest)
+    current = rest.pop(0) if resumed else None
+    moves = any(mixed is not None for mixed, _ in steps)
+    out = rest.pop(0) if moves else None
+    left = rest.pop(0) if steps[-1][1] is not None else None
+    packed, powers, factors = rest
+    fields, basis, n_elem = state.shape
+    width = n_elem // HALVES
+    half_rows = packed.shape[1] // 2
+    written = set()
     packed[...] = jnp.zeros_like(packed)
-    for f in range(fields):
-        high, low = split(state[f, :, base : base + width])
-        packed[0:basis, :] = high
-        packed[half : half + basis, :] = low
-        product = jnp.dot(stack[...], packed[...], preferred_element_type=F32)
-        powers[f] = product[: 3 * half] + product[3 * half :]
-
-    def lanes(tile, carry):
-        near = pl.multiple_of(tile * 128, 128)
-        at = pl.multiple_of(offset + near, 128)
-        place = pl.multiple_of(base + near, 128)
-        height = heights[level : level + 1, pl.ds(at, 128)]
-        factor = [
-            [
-                jnp.broadcast_to(height * coef[g, f : f + 1, pl.ds(at, 128)], (8, 128))
-                for f in range(fields)
-            ]
-            for g in range(fields)
-        ]
-
-        def combine(start, values):
-            mixed = []
-            for g in range(fields):
-                total = start[g]
+
+    def multiply(f, half, target):
+        source = out if half in written else state
+        high, low = split(source[f, :, half * width : (half + 1) * width])
+        slot = f % 2
+        packed[slot, 0:basis, :] = high
+        packed[slot, half_rows : half_rows + basis, :] = low
+        product = jnp.dot(stack[...], packed[slot], preferred_element_type=F32)
+        target[f] = product[: 3 * half_rows] + product[3 * half_rows :]
+
+    def set_factors(level, half):
+        at = slice(half * width, (half + 1) * width)
+        height = heights[level : level + 1, at]
+        for g in range(fields):
+            for f in range(fields):
+                factors[g * fields + f] = jnp.broadcast_to(
+                    height * coef[g, f : f + 1, at], (8, width)
+                )
+
+    def mix_lines(half, groups, values):
+        base = out if half in written else state
+        for tile in range(width // 128):
+            near = slice(tile * 128, (tile + 1) * 128)
+            at = slice(half * width + tile * 128, half * width + (tile + 1) * 128)
+            factor = [factors[k, :, near] for k in range(fields * fields)]
+
+            def combine(start, values):
+                mixed = []
+                for g in range(fields):
+                    total = start[g]
+                    for f in range(fields):
+                        total = total + factor[g * fields + f] * values[f]
+                    mixed.append(total)
+                return mixed
+
+            for group in groups:
+                lines = slice(group * 8, group * 8 + 8)
+
+                def power(k):
+                    rows = slice(k * half_rows + group * 8, k * half_rows + group * 8 + 8)
+                    return [values[f, rows, near] for f in range(fields)]
+
+                value = combine(power(1), power(2))
+                value = combine(power(0), value)
+                value = combine([base[f, lines, at] for f in range(fields)], value)
                 for f in range(fields):
-                    total = total + factor[g][f] * values[f]
-                mixed.append(total)
-            return mixed
-
-        def lines(group, inner):
-            top = pl.multiple_of(group * 8, 8)
-
-            def power(k):
-                return [
-                    powers[f, pl.ds(k * half + top, 8), pl.ds(near, 128)] for f in range(fields)
-                ]
-
-            value = combine(power(1), power(2))
-            value = combine(power(0), value)
-            start = [state[f, pl.ds(top, 8), pl.ds(place, 128)] for f in range(fields)]
-            value = combine(start, value)
-            for f in range(fields):
-                out[f, pl.ds(top, 8), pl.ds(near, 128)] = value[f]
-            return inner
-
-        return lax.fori_loop(0, basis // 8, lines, carry, unroll=3)
-
-    lax.fori_loop(0, width // 128, lanes, 0)
+                    out[f, lines, at] = value[f]
+
+    groups = basis // 8 // fields
+    for index, (mixed, multiplied) in enumerate(steps):
+        last = index == len(steps) - 1
+        target = left if last else powers.at[index % 2]
+        if mixed is not None:
+            set_factors(*mixed)
+        for f in range(fields):
+            if multiplied is not None:
+                multiply(f, multiplied[1], target)
+            if mixed is not None:
+                mix_lines(mixed[1], range(f * groups, (f + 1) * groups), current)
+        if mixed is not None:
+            written.add(mixed[1])
+        current = target
+    for half in range(HALVES if moves else 0):
+        if half not in written:
+            at = slice(half * width, (half + 1) * width)
+            out[:, :, at] = state[:, :, at]
 
 
 def advance(coef, height, held, count):
@@ -372,10 +433,8 @@
     return [held[f, 8 : 8 + count, :] + height * value[f] for f in range(fields)]
 
 
-def lift_kernel(coef, heights, weights0, weights1, lcols, *rest):
-    *blocks, out, held = rest
-    fields, _, n_elem = out.shape
-    width = n_elem // len(blocks)
+def lift_kernel(coef, heights, weights0, weights1, lcols, state, out, held):
+    fields, _, _ = out.shape
     held[...] = jnp.zeros_like(held)
     for f in range(fields):
         held[f, 8:11, :] = weights0[f, 0:3, :]
@@ -390,18 +449,14 @@
         held[f, 8:17, :] = value[f]
         right_high, right_low = split(held[f, 8:24, :])
         right = jnp.concatenate([right_high, right_low, right_high], axis=0)
-        added = jnp.dot(left, right, preferred_element_type=F32)
-        for k, block in enumerate(blocks):
-            at = slice(k * width, (k + 1) * width)
-            out[f, :, at] = block[f] + added[:, at]
-
-
-def closing_kernel(shape, level, me, tents, coef, heights, kappas, old_aux, lcols, state, *rest):
+        out[f] = state[f] + jnp.dot(left, right, preferred_element_type=F32)
+
+
+def closing_kernel(level, coef, heights, kappas, old_aux, lcols, state, member, *rest):
     tables = rest[:SLOTS]
     out, table, held, wide, sems = rest[SLOTS:]
     fields, basis, n_elem = state.shape
-    member = members(tents[level : level + 1, :], me[0], shape)
-    means = gather([t[...] for t in tables], table, member)
+    means = gather([t[...] for t in tables], table, member[...])
     height = heights[level : level + 1, :]
     weights = lift_weights(coef, height, means, old_aux, kappas)
     for k in range(3):
@@ -473,6 +528,14 @@
     return received
 
 
+PARTS = ((0, 1), (1, 3), (3, 4), (4, 6), (6, 7))
+
+
+def poly_steps(levels):
+    blocks = [(level, half) for level in range(levels) for half in range(HALVES)]
+    return list(zip([None] + blocks, blocks + [None]))
+
+
 def slab(state, coef, basis_quad, test_deriv, trace_vec, lift_vec, tent_height, elem_tent):
     size_first = lax.axis_size("gx")
     size_second = lax.axis_size("gy")
@@ -480,14 +543,21 @@
     levels, tent_dev = tent_height.shape
     shape = (size_first, size_second, tent_dev)
     me = (lax.axis_index("gx") * size_second + lax.axis_index("gy")).reshape(1)
-    message = [shaped(ROWS, tent_dev)] * SLOTS
+    message = [shaped(ROWS // 2, 2 * tent_dev)] * SLOTS
     aux_shape = shaped(BACK, n_elem)
     vals = pltpu.VMEM((ROWS, n_elem), F32)
     table = pltpu.VMEM((BACK, SLOTS * tent_dev), F32)
 
+    kept = [
+        shaped(*basis_quad.shape),
+        shaped(*test_deriv.shape[::-1]),
+        shaped(*state.shape),
+        shaped(*coef.shape),
+        shaped(*elem_tent.shape, dtype=jnp.int32),
+    ]
     rows3, lift, aux, *out = call(
         functools.partial(opening_kernel, shape),
-        [shaped(8, basis), shaped(1, basis), aux_shape] + message,
+        [shaped(8, basis), shaped(1, basis), aux_shape] + message + kept,
         (
             me,
             *(
@@ -506,14 +576,9 @@
         ),
         [
             vals,
-            pltpu.VMEM(basis_quad.shape, F32),
-            pltpu.VMEM(test_deriv.shape[::-1], F32),
             pltpu.VMEM(trace_vec.shape, F32),
             pltpu.VMEM(lift_vec.shape, F32),
-            pltpu.VMEM(state.shape, F32),
-            pltpu.VMEM(coef.shape, F32),
             pltpu.VMEM(tent_height.shape, F32),
-            pltpu.VMEM(elem_tent.shape, jnp.int32),
             pltpu.VMEM((3, basis, 128), F32),
             pltpu.VMEM((fields, 8, n_elem), F32),
             pltpu.SemaphoreType.DMA((8,)),
@@ -521,6 +586,8 @@
         1,
         space=pltpu.HBM,
     )
+    basis_near, test_near, state, coef, elem_tent = out[SLOTS:]
+    out = out[:SLOTS]
     stack, rstack, lcols, kappas = call(
         powers_kernel,
         [
@@ -529,8 +596,12 @@
             shaped(basis, 16),
             shaped(16, n_elem),
         ],
-        (basis_quad, test_deriv.T, rows3, lift),
-        [pltpu.VMEM((16, basis), F32), pltpu.VMEM((16, basis), F32)],
+        (basis_near, test_near, rows3, lift),
+        [
+            pltpu.VMEM((16, basis), F32),
+            pltpu.VMEM((8 + 2 * basis, basis), F32),
+            pltpu.VMEM((basis, basis + 8), F32),
+        ],
         flops=100000000,
     )
     proj = call(
@@ -540,65 +611,103 @@
         [pltpu.VMEM((256, 256), BF16)],
         flops=300000000,
     )
-    blocks = [state] * HALVES
     width = n_elem // HALVES
     weights = []
     heights = None
-
-    def advance_block(level, half):
-        blocks[half] = call(
-            functools.partial(level_kernel, level, half * width),
-            shaped(fields, basis, width),
-            (blocks[half], coef, heights, stack),
-            [pltpu.VMEM((256, width), BF16), pltpu.VMEM((fields, 384, width), F32)],
-            flops=1000000000,
+    steps = poly_steps(levels)
+    values = state
+    held = []
+
+    def advance_state(values, held, part):
+        chosen = PARTS[part]
+        resumed = chosen[0] > 0
+        mine = steps[chosen[0] : chosen[1]]
+        half_powers = shaped(fields, 384, width)
+        moves = any(mixed is not None for mixed, _ in mine)
+        outs = [shaped(fields, basis, n_elem)] if moves else []
+        if mine[-1][1] is not None:
+            outs.append(half_powers)
+        held = call(
+            functools.partial(poly_kernel, mine, resumed),
+            outs,
+            (values, coef, heights, stack, *held),
+            [
+                pltpu.VMEM((2, 256, width), BF16),
+                pltpu.VMEM((2, fields, 384, width), F32),
+                pltpu.VMEM((fields * fields, 8, width), F32),
+            ],
+            flops=3000000000,
         )
+        if moves:
+            values, *held = held
+        return values, held
 
     for level in range(levels):
         received = exchange(out[:4])
         means = call(owner_kernel, shaped(BACK, tent_dev), (kappas, out[4], *received))
         back = exchange([means] * 4)
         if level == 0:
+            memberships = call(
+                functools.partial(members_kernel, shape),
+                [shaped(SLOTS * tent_dev, n_elem, dtype=BF16)] * levels,
+                (me, elem_tent),
+                (),
+                1,
+            )
             heights = call(
-                functools.partial(heights_kernel, shape),
+                lambda *refs: heights_kernel(refs[:5], refs[5 : 5 + levels], *refs[5 + levels :]),
                 shaped(8, n_elem),
-                (me, elem_tent, *received, out[4]),
+                (*received, out[4], *memberships),
                 [table],
-                1,
                 flops=10000000,
             )
-        for half in range(HALVES):
-            advance_block(level, half)
+        if level < levels - 1:
+            count = 6 - 3 * level
+            drift = call(
+                functools.partial(drift_kernel, level, count),
+                shaped(fields, 8, n_elem),
+                (coef, heights, proj),
+            )
         if level < levels - 1:
             more = [shaped(fields, 8, n_elem)] if level < levels - 2 else []
             weight, aux, *out = call(
-                functools.partial(element_kernel, shape, level, 6 - 3 * level),
+                functools.partial(element_kernel, level, count),
                 [shaped(fields, 8, n_elem), aux_shape] + message + more,
-                (me, elem_tent, coef, heights, kappas, aux, proj, *back, means),
+                (
+                    coef,
+                    heights,
+                    kappas,
+                    aux,
+                    drift,
+                    memberships[level],
+                    memberships[level + 1],
+                    *back,
+                    means,
+                ),
                 [vals, table],
-                1,
             )
             weights.append(weight)
             if more:
                 proj = out.pop()
+    for part in range(len(PARTS)):
+        values, held = advance_state(values, held, part)
     values = call(
         lift_kernel,
         shaped(fields, basis, n_elem),
-        (coef, heights, weights[0], weights[1], lcols, *blocks),
+        (coef, heights, weights[0], weights[1], lcols, values),
         [pltpu.VMEM((fields, 24, n_elem), F32)],
         flops=100000000,
     )
     return call(
-        functools.partial(closing_kernel, shape, levels - 1),
+        functools.partial(closing_kernel, levels - 1),
         shaped(fields, basis, n_elem),
-        (me, elem_tent, coef, heights, kappas, aux, lcols, values, *back, means),
+        (coef, heights, kappas, aux, lcols, values, memberships[levels - 1], *back, means),
         [
             table,
             pltpu.VMEM(state.shape, F32),
             pltpu.VMEM((3, basis, 128), F32),
             pltpu.SemaphoreType.DMA((fields,)),
         ],
-        1,
         out_space=pltpu.HBM,
     )
 

time: 62.7 us -> 60.8 us (0.970)
  Pallas kernels: 17.9 us -> 15.9 us
  starting transfers between devices: 33.8 us -> 32.8 us
  waiting for transfers between devices: 10.5 us -> 11.5 us
    pallas_call x17 -> x19, Pallas kernels: 17.9 us -> 15.9 us  [call(): pl.pallas_call(kernel, out_shape=shapes, in_specs=specs, out_specs=[pl.Bl...]
    ppermute x24, waiting for transfers between devices: 10.5 us -> 11.5 us  [swap(): return lax.ppermute(x, axis, pairs)]
    ppermute x24, starting transfers between devices: 33.8 us -> 32.8 us  [swap(): return lax.ppermute(x, axis, pairs)]
  transfers between devices with their start and end apart: 24 -> 24, of which waited for: 6 -> 6; matrix products, arithmetic and copies ran while one was open for 0% -> 0% of each run, Pallas kernels for 19% -> 17%
where the time goes in v2:
time: 60.8 us; the launch traced here: 60.6 us
  starting transfers between devices  32.8 us (54%)
  Pallas kernels  15.9 us (26%)
  waiting for transfers between devices  11.5 us (19%)
    ppermute x24, starting transfers between devices, swap(): return lax.ppermute(x, axis, pairs)  32.8 us
    pallas_call x19, Pallas kernels, call(): pl.pallas_call(kernel, out_shape=shapes, in_specs=specs, out_specs=[pl.Bl...  15.9 us
    ppermute x24, waiting for transfers between devices, swap(): return lax.ppermute(x, axis, pairs)  11.5 us
  transfers between devices with their start and end apart: 24, of which 6 were waited for; matrix products, arithmetic and copies ran while one was open for 0% of the time, Pallas kernels for 17%

profile of v2, /device:TPU:1, one launch (start us, length us, event | category | flops | bytes accessed | tf_op | source)
XLA Modules:
  0.0 60.6 jit_solution(17845779850182034901)
XLA Ops:
  0.0 2.2 %shard_map.82 = (f32[8,120]{1,0:T(8,128)S(1)}, f32[1,120]{1,0:T(1,128)S(1)}, f32[16,512]{1,0:T(8,128)S(1)}, f32[24,128]{1,0:T(8,128)S(1)}, f32[24,128]{1,0:T(8,1...) custom-call(s32[1]{0:T(128)} %bitcast.me, ...), custom_call_target="tpu_custom_call" | custom-call | flops 1000000 | bytes 3087268 | tf_op jit(solution)/shard_map/pallas_call | solution.py:496
  2.2 2.2 %collective-permute-start = (f32[24,128]{1,0:T(8,128)S(1)}, f32[24,128]{1,0:T(8,128)S(1)}, u32[]{:S(2)}, u32[]{:S(2)}) collective-permute-start(f32[24,128]{1,0:T(8,128)S(1)} %get-tuple-element.47), channel_id=1, source_target_pairs={{0,8},{8,0},{16,24},{24,16},{32,40},{40,32},{48,56},{56,48},{64,72... | collective-permute-start | bytes 36872 | tf_op jit(solution)/shard_map/ppermute | solution.py:518
  4.4 5.4 %collective-permute-start.1 = (f32[24,128]{1,0:T(8,128)S(1)}, f32[24,128]{1,0:T(8,128)S(1)}, u32[]{:S(2)}, u32[]{:S(2)}) collective-permute-start(f32[24,128]{1,0:T(8,128)S(1)} %get-tuple-element.48), channel_id=1, source_target_pairs={{0,120},{8,16},{16,8},{24,32},{32,24},{40,48},{48,40},{56,64},{64,... | collective-permute-start | bytes 36872 | tf_op jit(solution)/shard_map/ppermute | solution.py:518
  9.8 1.2 %collective-permute-start.2 = (f32[24,128]{1,0:T(8,128)S(1)}, f32[24,128]{1,0:T(8,128)S(1)}, u32[]{:S(2)}, u32[]{:S(2)}) collective-permute-start(f32[24,128]{1,0:T(8,128)S(1)} %get-tuple-element.49), channel_id=1, source_target_pairs={{0,1},{1,0},{2,3},{3,2},{4,5},{5,4},{6,7},{7,6},{8,9},{9,8},{10,11... | collective-permute-start | bytes 36872 | tf_op jit(solution)/shard_map/ppermute | solution.py:518
  11.0 1.1 %collective-permute-start.3 = (f32[24,128]{1,0:T(8,128)S(1)}, f32[24,128]{1,0:T(8,128)S(1)}, u32[]{:S(2)}, u32[]{:S(2)}) collective-permute-start(f32[24,128]{1,0:T(8,128)S(1)} %get-tuple-element.50), channel_id=1, source_target_pairs={{0,7},{1,2},{2,1},{3,4},{4,3},{5,6},{6,5},{7,0},{8,15},{9,10},{10,... | collective-permute-start | bytes 36872 | tf_op jit(solution)/shard_map/ppermute | solution.py:518
  12.1 1.8 %shard_map.85 = (bf16[768,256]{1,0:T(8,128)(2,1)S(1)}, bf16[32,256]{1,0:T(8,128)(2,1)S(1)}, f32[120,16]{1,0:T(8,128)S(1)}, f32[16,512]{1,0:T(8,128)S(1)}) custom-call(f32[216,120]{1,0:T(8,128)S(1)} %get-tuple-element.56.basis, f32[216,120]{1,0:T(8,128)S(1)} %get-tuple-element.57.test, f32[8,120]{1,0:T(8,128)S(1)} %get-tuple-element.58.rows3, ...), custom_call_target="tpu_custom_call" | custom-call | flops 100000000 | bytes 1071328 | tf_op jit(solution)/shard_map/pallas_call | solution.py:496
  14.0 0.3 shard_map.86.proj
  14.3 0.2 shard_map.83
  14.5 0.0 collective-permute-done.1.refs_1_.rest_1_
  14.5 0.0 collective-permute-done.2.refs_2_.rest_2_
  14.6 0.1 shard_map.88.rest_4_
  14.7 0.8 %collective-permute-start.7 = (f32[16,64]{1,0:T(8,128)S(1)}, f32[16,64]{1,0:T(8,128)S(1)}, u32[]{:S(2)}, u32[]{:S(2)}) collective-permute-start(f32[16,64]{1,0:T(8,128)S(1)} %shard_map.88.rest_4_), channel_id=1, source_target_pairs={{0,7},{1,2},{2,1},{3,4},{4,3},{5,6},{6,5},{7,0},{8,15},{9,10},{10,... | collective-permute-start | bytes 12296 | tf_op jit(solution)/shard_map/ppermute | solution.py:518
  15.4 3.0 %collective-permute-start.6 = (f32[16,64]{1,0:T(8,128)S(1)}, f32[16,64]{1,0:T(8,128)S(1)}, u32[]{:S(2)}, u32[]{:S(2)}) collective-permute-start(f32[16,64]{1,0:T(8,128)S(1)} %shard_map.88.rest_4_), channel_id=1, source_target_pairs={{0,1},{1,0},{2,3},{3,2},{4,5},{5,4},{6,7},{7,6},{8,9},{9,8},{10,11... | collective-permute-start | bytes 12296 | tf_op jit(solution)/shard_map/ppermute | solution.py:518
  18.4 0.6 %collective-permute-start.5 = (f32[16,64]{1,0:T(8,128)S(1)}, f32[16,64]{1,0:T(8,128)S(1)}, u32[]{:S(2)}, u32[]{:S(2)}) collective-permute-start(f32[16,64]{1,0:T(8,128)S(1)} %shard_map.88.rest_4_), channel_id=1, source_target_pairs={{0,120},{8,16},{16,8},{24,32},{32,24},{40,48},{48,40},{56,64},{64,... | collective-permute-start | bytes 12296 | tf_op jit(solution)/shard_map/ppermute | solution.py:518
  19.1 0.3 shard_map.84.heights
  19.4 0.7 %shard_map.93.rest_0_ = f32[5,384,256]{2,1,0:T(8,128)S(1)} custom-call(f32[5,120,512]{2,1,0:T(8,128)S(1)} %get-tuple-element.63.state, f32[5,5,512]{2,1,0:T(8,128)S(1)} %get-tuple-element.46.coef, f32[8,512]{1,0:T(8,128)S(1)} %shard_map.84.heights, bf16[768,256]{1,0:T(8,128)(2,1)S(1)} %get-tuple-element.75.stack), custom_call_target="tpu_custom_call" | custom-call | flops 3000000000 | bytes 4048896 | tf_op jit(solution)/shard_map/pallas_call | solution.py:496
  20.1 2.0 %shard_map.94 = (f32[5,120,512]{2,1,0:T(8,128)S(1)}, f32[5,384,256]{2,1,0:T(8,128)S(1)}) custom-call(f32[5,120,512]{2,1,0:T(8,128)S(1)} %get-tuple-element.63.state, f32[5,5,512]{2,1,0:T(8,128)S(1)} %get-tuple-element.46.coef, f32[8,512]{1,0:T(8,128)S(1)} %shard_map.84.heights, bf16[768,256]{1,0:T(8,128)(2,1)S(1)} %get-tuple-element.75.stack, ...), custom_call_target="tpu_custom_call" | custom-call | flops 3000000000 | bytes 7243776 | tf_op jit(solution)/shard_map/pallas_call | solution.py:496
  22.1 0.1 shard_map.87.drift
  22.3 2.0 %collective-permute-done.5.rest_1_ = f32[16,64]{1,0:T(8,128)S(1)} collective-permute-done((f32[16,64]{1,0:T(8,128)S(1)}, f32[16,64]{1,0:T(8,128)S(1)}, u32[]{:S(2)}, u32[]{:S(2)}) %collective-permute-start.5) | collective-permute-done | bytes 4128 | tf_op jit(solution)/shard_map/ppermute | solution.py:518
  24.2 0.0 collective-permute-done.4.rest_0_
  24.3 0.8 %shard_map.89 = (f32[5,8,512]{2,1,0:T(8,128)S(1)}, f32[16,512]{1,0:T(8,128)S(1)}, f32[24,128]{1,0:T(8,128)S(1)}, f32[24,128]{1,0:T(8,128)S(1)}, f32[24,128]{1,0:...) custom-call(f32[5,5,512]{2,1,0:T(8,128)S(1)} %get-tuple-element.46.coef, ...), custom_call_target="tpu_custom_call" | custom-call | flops 1000000 | bytes 1804288 | tf_op jit(solution)/shard_map/pallas_call | solution.py:496
  25.0 0.1 collective-permute-start.8
  25.1 3.7 %collective-permute-start.9 = (f32[24,128]{1,0:T(8,128)S(1)}, f32[24,128]{1,0:T(8,128)S(1)}, u32[]{:S(2)}, u32[]{:S(2)}) collective-permute-start(f32[24,128]{1,0:T(8,128)S(1)} %get-tuple-element.68), channel_id=1, source_target_pairs={{0,120},{8,16},{16,8},{24,32},{32,24},{40,48},{48,40},{56,64},{64,... | collective-permute-start | bytes 36872 | tf_op jit(solution)/shard_map/ppermute | solution.py:518
  28.8 1.1 %collective-permute-start.10 = (f32[24,128]{1,0:T(8,128)S(1)}, f32[24,128]{1,0:T(8,128)S(1)}, u32[]{:S(2)}, u32[]{:S(2)}) collective-permute-start(f32[24,128]{1,0:T(8,128)S(1)} %get-tuple-element.69), channel_id=1, source_target_pairs={{0,1},{1,0},{2,3},{3,2},{4,5},{5,4},{6,7},{7,6},{8,9},{9,8},{10,11... | collective-permute-start | bytes 36872 | tf_op jit(solution)/shard_map/ppermute | solution.py:518
  29.9 1.2 %shard_map.95 = (f32[5,120,512]{2,1,0:T(8,128)S(1)}, f32[5,384,256]{2,1,0:T(8,128)S(1)}) custom-call(f32[5,120,512]{2,1,0:T(8,128)S(1)} %get-tuple-element.76.state, f32[5,5,512]{2,1,0:T(8,128)S(1)} %get-tuple-element.46.coef, f32[8,512]{1,0:T(8,128)S(1)} %shard_map.84.heights, bf16[768,256]{1,0:T(8,128)(2,1)S(1)} %get-tuple-element.75.stack, ...), custom_call_target="tpu_custom_call" | custom-call | flops 3000000000 | bytes 7243776 | tf_op jit(solution)/shard_map/pallas_call | solution.py:496
  31.2 2.2 %collective-permute-done.11.rest_3_ = f32[24,128]{1,0:T(8,128)S(1)} collective-permute-done((f32[24,128]{1,0:T(8,128)S(1)}, f32[24,128]{1,0:T(8,128)S(1)}, u32[]{:S(2)}, u32[]{:S(2)}) %collective-permute-start.11) | collective-permute-done | bytes 12320 | tf_op jit(solution)/shard_map/ppermute | solution.py:518
  33.3 0.1 shard_map.91.rest_4_
  33.4 0.9 %collective-permute-start.15 = (f32[16,64]{1,0:T(8,128)S(1)}, f32[16,64]{1,0:T(8,128)S(1)}, u32[]{:S(2)}, u32[]{:S(2)}) collective-permute-start(f32[16,64]{1,0:T(8,128)S(1)} %shard_map.91.rest_4_), channel_id=1, source_target_pairs={{0,7},{1,2},{2,1},{3,4},{4,3},{5,6},{6,5},{7,0},{8,15},{9,10},{10,... | collective-permute-start | bytes 12296 | tf_op jit(solution)/shard_map/ppermute | solution.py:518
  34.3 1.7 %collective-permute-start.14 = (f32[16,64]{1,0:T(8,128)S(1)}, f32[16,64]{1,0:T(8,128)S(1)}, u32[]{:S(2)}, u32[]{:S(2)}) collective-permute-start(f32[16,64]{1,0:T(8,128)S(1)} %shard_map.91.rest_4_), channel_id=1, source_target_pairs={{0,1},{1,0},{2,3},{3,2},{4,5},{5,4},{6,7},{7,6},{8,9},{9,8},{10,11... | collective-permute-start | bytes 12296 | tf_op jit(solution)/shard_map/ppermute | solution.py:518
  36.0 1.8 %collective-permute-start.13 = (f32[16,64]{1,0:T(8,128)S(1)}, f32[16,64]{1,0:T(8,128)S(1)}, u32[]{:S(2)}, u32[]{:S(2)}) collective-permute-start(f32[16,64]{1,0:T(8,128)S(1)} %shard_map.91.rest_4_), channel_id=1, source_target_pairs={{0,120},{8,16},{16,8},{24,32},{32,24},{40,48},{48,40},{56,64},{64,... | collective-permute-start | bytes 12296 | tf_op jit(solution)/shard_map/ppermute | solution.py:518
  37.8 0.0 collective-permute-start.12
  37.8 2.0 %shard_map.96 = (f32[5,120,512]{2,1,0:T(8,128)S(1)}, f32[5,384,256]{2,1,0:T(8,128)S(1)}) custom-call(f32[5,120,512]{2,1,0:T(8,128)S(1)} %get-tuple-element.78.state, f32[5,5,512]{2,1,0:T(8,128)S(1)} %get-tuple-element.46.coef, f32[8,512]{1,0:T(8,128)S(1)} %shard_map.84.heights, bf16[768,256]{1,0:T(8,128)(2,1)S(1)} %get-tuple-element.75.stack, ...), custom_call_target="tpu_custom_call" | custom-call | flops 3000000000 | bytes 7243776 | tf_op jit(solution)/shard_map/pallas_call | solution.py:496
  39.8 0.1 shard_map.90.drift
  40.0 1.8 %collective-permute-done.13.rest_1_ = f32[16,64]{1,0:T(8,128)S(1)} collective-permute-done((f32[16,64]{1,0:T(8,128)S(1)}, f32[16,64]{1,0:T(8,128)S(1)}, u32[]{:S(2)}, u32[]{:S(2)}) %collective-permute-start.13) | collective-permute-done | bytes 4128 | tf_op jit(solution)/shard_map/ppermute | solution.py:518
  41.8 0.8 %shard_map.92 = (f32[5,8,512]{2,1,0:T(8,128)S(1)}, f32[16,512]{1,0:T(8,128)S(1)}, f32[24,128]{1,0:T(8,128)S(1)}, f32[24,128]{1,0:T(8,128)S(1)}, f32[24,128]{1,0:...) custom-call(f32[5,5,512]{2,1,0:T(8,128)S(1)} %get-tuple-element.46.coef, f32[8,512]{1,0:T(8,128)S(1)} %shard_map.84.heights, ...), custom_call_target="tpu_custom_call" | custom-call | flops 1000000 | bytes 1722368 | tf_op jit(solution)/shard_map/pallas_call | solution.py:496
  42.6 0.1 collective-permute-start.16
  42.7 2.6 %collective-permute-start.17 = (f32[24,128]{1,0:T(8,128)S(1)}, f32[24,128]{1,0:T(8,128)S(1)}, u32[]{:S(2)}, u32[]{:S(2)}) collective-permute-start(f32[24,128]{1,0:T(8,128)S(1)} %get-tuple-element.84), channel_id=1, source_target_pairs={{0,120},{8,16},{16,8},{24,32},{32,24},{40,48},{48,40},{56,64},{64,... | collective-permute-start | bytes 36872 | tf_op jit(solution)/shard_map/ppermute | solution.py:518
  45.3 1.1 %collective-permute-start.18 = (f32[24,128]{1,0:T(8,128)S(1)}, f32[24,128]{1,0:T(8,128)S(1)}, u32[]{:S(2)}, u32[]{:S(2)}) collective-permute-start(f32[24,128]{1,0:T(8,128)S(1)} %get-tuple-element.85), channel_id=1, source_target_pairs={{0,1},{1,0},{2,3},{3,2},{4,5},{5,4},{6,7},{7,6},{8,9},{9,8},{10,11... | collective-permute-start | bytes 36872 | tf_op jit(solution)/shard_map/ppermute | solution.py:518
  46.4 0.6 %shard_map.97.state = f32[5,120,512]{2,1,0:T(8,128)S(1)} custom-call(f32[5,120,512]{2,1,0:T(8,128)S(1)} %get-tuple-element.80.state, f32[5,5,512]{2,1,0:T(8,128)S(1)} %get-tuple-element.46.coef, f32[8,512]{1,0:T(8,128)S(1)} %shard_map.84.heights, bf16[768,256]{1,0:T(8,128)(2,1)S(1)} %get-tuple-element.75.stack, f32[5,384,256]{2,1,0:T(8,128)S(1)} %get-tuple-element.81.rest_0_), custom_call_target="tpu_custom_call" | custom-call | flops 3000000000 | bytes 5277696 | tf_op jit(solution)/shard_map/pallas_call | solution.py:496
  47.1 1.5 %collective-permute-done.17.rest_1_ = f32[24,128]{1,0:T(8,128)S(1)} collective-permute-done((f32[24,128]{1,0:T(8,128)S(1)}, f32[24,128]{1,0:T(8,128)S(1)}, u32[]{:S(2)}, u32[]{:S(2)}) %collective-permute-start.17) | collective-permute-done | bytes 12320 | tf_op jit(solution)/shard_map/ppermute | solution.py:518
  48.6 1.2 %collective-permute-done.19.rest_3_ = f32[24,128]{1,0:T(8,128)S(1)} collective-permute-done((f32[24,128]{1,0:T(8,128)S(1)}, f32[24,128]{1,0:T(8,128)S(1)}, u32[]{:S(2)}, u32[]{:S(2)}) %collective-permute-start.19) | collective-permute-done | bytes 12320 | tf_op jit(solution)/shard_map/ppermute | solution.py:518
  49.8 0.1 shard_map.99.rest_4_
  49.9 0.8 %collective-permute-start.23 = (f32[16,64]{1,0:T(8,128)S(1)}, f32[16,64]{1,0:T(8,128)S(1)}, u32[]{:S(2)}, u32[]{:S(2)}) collective-permute-start(f32[16,64]{1,0:T(8,128)S(1)} %shard_map.99.rest_4_), channel_id=1, source_target_pairs={{0,7},{1,2},{2,1},{3,4},{4,3},{5,6},{6,5},{7,0},{8,15},{9,10},{10,... | collective-permute-start | bytes 12296 | tf_op jit(solution)/shard_map/ppermute | solution.py:518
  50.7 2.3 %collective-permute-start.22 = (f32[16,64]{1,0:T(8,128)S(1)}, f32[16,64]{1,0:T(8,128)S(1)}, u32[]{:S(2)}, u32[]{:S(2)}) collective-permute-start(f32[16,64]{1,0:T(8,128)S(1)} %shard_map.99.rest_4_), channel_id=1, source_target_pairs={{0,1},{1,0},{2,3},{3,2},{4,5},{5,4},{6,7},{7,6},{8,9},{9,8},{10,11... | collective-permute-start | bytes 12296 | tf_op jit(solution)/shard_map/ppermute | solution.py:518
  53.0 2.4 %collective-permute-start.21 = (f32[16,64]{1,0:T(8,128)S(1)}, f32[16,64]{1,0:T(8,128)S(1)}, u32[]{:S(2)}, u32[]{:S(2)}) collective-permute-start(f32[16,64]{1,0:T(8,128)S(1)} %shard_map.99.rest_4_), channel_id=1, source_target_pairs={{0,120},{8,16},{16,8},{24,32},{32,24},{40,48},{48,40},{56,64},{64,... | collective-permute-start | bytes 12296 | tf_op jit(solution)/shard_map/ppermute | solution.py:518
  55.4 0.7 %shard_map.98.state = f32[5,120,512]{2,1,0:T(8,128)S(1)} custom-call(f32[5,5,512]{2,1,0:T(8,128)S(1)} %get-tuple-element.46.coef, f32[8,512]{1,0:T(8,128)S(1)} %shard_map.84.heights, f32[5,8,512]{2,1,0:T(8,128)S(1)} %get-tuple-element.73.weights0, f32[5,8,512]{2,1,0:T(8,128)S(1)} %get-tuple-element.74.weights1, f32[120,16]{1,0:T(8,128)S(1)} %get-tuple-element.72.lcols, ...), custom_call_target="tpu_custom_call" | custom-call | flops 100000000 | bytes 2696704 | tf_op jit(solution)/shard_map/pallas_call | solution.py:496
  56.1 2.7 %collective-permute-done.21.rest_1_ = f32[16,64]{1,0:T(8,128)S(1)} collective-permute-done((f32[16,64]{1,0:T(8,128)S(1)}, f32[16,64]{1,0:T(8,128)S(1)}, u32[]{:S(2)}, u32[]{:S(2)}) %collective-permute-start.21) | collective-permute-done | bytes 4128 | tf_op jit(solution)/shard_map/ppermute | solution.py:518
  58.8 1.6 %shard_map.100 = f32[5,120,512]{2,1,0:T(8,128)} custom-call(f32[5,5,512]{2,1,0:T(8,128)S(1)} %get-tuple-element.46.coef, f32[8,512]{1,0:T(8,128)S(1)} %shard_map.84.heights, f32[16,512]{1,0:T(8,128)S(1)} %get-tuple-element.60.kappas, f32[16,512]{1,0:T(8,128)S(1)} %get-tuple-element.71.old_aux, f32[120,16]{1,0:T(8,128)S(1)} %get-tuple-element.72.lcols, ...), custom_call_target="tpu_custom_call" | custom-call | flops 1000000 | bytes 3274240 | tf_op jit(solution)/shard_map/pallas_call | solution.py:496
  (19 shorter events, 0.0 us)
Async XLA Ops:
  2.2 12.3 %collective-permute-start = (f32[24,128]{1,0:T(8,128)S(1)}, f32[24,128]{1,0:T(8,128)S(1)}, u32[]{:S(2)}, u32[]{:S(2)}) collective-permute-start(f32[24,128]{1,0:T(8,128)S(1)} %get-tuple-element.47), channel_id=1, source_target_pairs={{0,8},{8,0},{16,24},{24,16},{32,40},{40,32},{48,56},{56,48},{64,72... | collective-permute-start | bytes 36872 | tf_op jit(solution)/shard_map/ppermute | solution.py:518
  4.4 10.1 %collective-permute-start.1 = (f32[24,128]{1,0:T(8,128)S(1)}, f32[24,128]{1,0:T(8,128)S(1)}, u32[]{:S(2)}, u32[]{:S(2)}) collective-permute-start(f32[24,128]{1,0:T(8,128)S(1)} %get-tuple-element.48), channel_id=1, source_target_pairs={{0,120},{8,16},{16,8},{24,32},{32,24},{40,48},{48,40},{56,64},{64,... | collective-permute-start | bytes 36872 | tf_op jit(solution)/shard_map/ppermute | solution.py:518
  9.8 4.7 %collective-permute-start.2 = (f32[24,128]{1,0:T(8,128)S(1)}, f32[24,128]{1,0:T(8,128)S(1)}, u32[]{:S(2)}, u32[]{:S(2)}) collective-permute-start(f32[24,128]{1,0:T(8,128)S(1)} %get-tuple-element.49), channel_id=1, source_target_pairs={{0,1},{1,0},{2,3},{3,2},{4,5},{5,4},{6,7},{7,6},{8,9},{9,8},{10,11... | collective-permute-start | bytes 36872 | tf_op jit(solution)/shard_map/ppermute | solution.py:518
  11.0 3.5 %collective-permute-start.3 = (f32[24,128]{1,0:T(8,128)S(1)}, f32[24,128]{1,0:T(8,128)S(1)}, u32[]{:S(2)}, u32[]{:S(2)}) collective-permute-start(f32[24,128]{1,0:T(8,128)S(1)} %get-tuple-element.50), channel_id=1, source_target_pairs={{0,7},{1,2},{2,1},{3,4},{4,3},{5,6},{6,5},{7,0},{8,15},{9,10},{10,... | collective-permute-start | bytes 36872 | tf_op jit(solution)/shard_map/ppermute | solution.py:518
  14.7 7.6 %collective-permute-start.7 = (f32[16,64]{1,0:T(8,128)S(1)}, f32[16,64]{1,0:T(8,128)S(1)}, u32[]{:S(2)}, u32[]{:S(2)}) collective-permute-start(f32[16,64]{1,0:T(8,128)S(1)} %shard_map.88.rest_4_), channel_id=1, source_target_pairs={{0,7},{1,2},{2,1},{3,4},{4,3},{5,6},{6,5},{7,0},{8,15},{9,10},{10,... | collective-permute-start | bytes 12296 | tf_op jit(solution)/shard_map/ppermute | solution.py:518
  15.4 6.8 %collective-permute-start.6 = (f32[16,64]{1,0:T(8,128)S(1)}, f32[16,64]{1,0:T(8,128)S(1)}, u32[]{:S(2)}, u32[]{:S(2)}) collective-permute-start(f32[16,64]{1,0:T(8,128)S(1)} %shard_map.88.rest_4_), channel_id=1, source_target_pairs={{0,1},{1,0},{2,3},{3,2},{4,5},{5,4},{6,7},{7,6},{8,9},{9,8},{10,11... | collective-permute-start | bytes 12296 | tf_op jit(solution)/shard_map/ppermute | solution.py:518
  18.4 5.8 %collective-permute-start.5 = (f32[16,64]{1,0:T(8,128)S(1)}, f32[16,64]{1,0:T(8,128)S(1)}, u32[]{:S(2)}, u32[]{:S(2)}) collective-permute-start(f32[16,64]{1,0:T(8,128)S(1)} %shard_map.88.rest_4_), channel_id=1, source_target_pairs={{0,120},{8,16},{16,8},{24,32},{32,24},{40,48},{48,40},{56,64},{64,... | collective-permute-start | bytes 12296 | tf_op jit(solution)/shard_map/ppermute | solution.py:518
  19.1 5.2 %collective-permute-start.4 = (f32[16,64]{1,0:T(8,128)S(1)}, f32[16,64]{1,0:T(8,128)S(1)}, u32[]{:S(2)}, u32[]{:S(2)}) collective-permute-start(f32[16,64]{1,0:T(8,128)S(1)} %shard_map.88.rest_4_), channel_id=1, source_target_pairs={{0,8},{8,0},{16,24},{24,16},{32,40},{40,32},{48,56},{56,48},{64,72... | collective-permute-start | bytes 12296 | tf_op jit(solution)/shard_map/ppermute | solution.py:518
  25.0 6.1 %collective-permute-start.8 = (f32[24,128]{1,0:T(8,128)S(1)}, f32[24,128]{1,0:T(8,128)S(1)}, u32[]{:S(2)}, u32[]{:S(2)}) collective-permute-start(f32[24,128]{1,0:T(8,128)S(1)} %get-tuple-element.67), channel_id=1, source_target_pairs={{0,8},{8,0},{16,24},{24,16},{32,40},{40,32},{48,56},{56,48},{64,72... | collective-permute-start | bytes 36872 | tf_op jit(solution)/shard_map/ppermute | solution.py:518
  25.1 6.0 %collective-permute-start.9 = (f32[24,128]{1,0:T(8,128)S(1)}, f32[24,128]{1,0:T(8,128)S(1)}, u32[]{:S(2)}, u32[]{:S(2)}) collective-permute-start(f32[24,128]{1,0:T(8,128)S(1)} %get-tuple-element.68), channel_id=1, source_target_pairs={{0,120},{8,16},{16,8},{24,32},{32,24},{40,48},{48,40},{56,64},{64,... | collective-permute-start | bytes 36872 | tf_op jit(solution)/shard_map/ppermute | solution.py:518
  28.8 2.4 %collective-permute-start.10 = (f32[24,128]{1,0:T(8,128)S(1)}, f32[24,128]{1,0:T(8,128)S(1)}, u32[]{:S(2)}, u32[]{:S(2)}) collective-permute-start(f32[24,128]{1,0:T(8,128)S(1)} %get-tuple-element.69), channel_id=1, source_target_pairs={{0,1},{1,0},{2,3},{3,2},{4,5},{5,4},{6,7},{7,6},{8,9},{9,8},{10,11... | collective-permute-start | bytes 36872 | tf_op jit(solution)/shard_map/ppermute | solution.py:518
  29.9 3.4 %collective-permute-start.11 = (f32[24,128]{1,0:T(8,128)S(1)}, f32[24,128]{1,0:T(8,128)S(1)}, u32[]{:S(2)}, u32[]{:S(2)}) collective-permute-start(f32[24,128]{1,0:T(8,128)S(1)} %get-tuple-element.70), channel_id=1, source_target_pairs={{0,7},{1,2},{2,1},{3,4},{4,3},{5,6},{6,5},{7,0},{8,15},{9,10},{10,... | collective-permute-start | bytes 36872 | tf_op jit(solution)/shard_map/ppermute | solution.py:518
  33.4 6.5 %collective-permute-start.15 = (f32[16,64]{1,0:T(8,128)S(1)}, f32[16,64]{1,0:T(8,128)S(1)}, u32[]{:S(2)}, u32[]{:S(2)}) collective-permute-start(f32[16,64]{1,0:T(8,128)S(1)} %shard_map.91.rest_4_), channel_id=1, source_target_pairs={{0,7},{1,2},{2,1},{3,4},{4,3},{5,6},{6,5},{7,0},{8,15},{9,10},{10,... | collective-permute-start | bytes 12296 | tf_op jit(solution)/shard_map/ppermute | solution.py:518
  34.3 5.7 %collective-permute-start.14 = (f32[16,64]{1,0:T(8,128)S(1)}, f32[16,64]{1,0:T(8,128)S(1)}, u32[]{:S(2)}, u32[]{:S(2)}) collective-permute-start(f32[16,64]{1,0:T(8,128)S(1)} %shard_map.91.rest_4_), channel_id=1, source_target_pairs={{0,1},{1,0},{2,3},{3,2},{4,5},{5,4},{6,7},{7,6},{8,9},{9,8},{10,11... | collective-permute-start | bytes 12296 | tf_op jit(solution)/shard_map/ppermute | solution.py:518
  36.0 5.8 %collective-permute-start.13 = (f32[16,64]{1,0:T(8,128)S(1)}, f32[16,64]{1,0:T(8,128)S(1)}, u32[]{:S(2)}, u32[]{:S(2)}) collective-permute-start(f32[16,64]{1,0:T(8,128)S(1)} %shard_map.91.rest_4_), channel_id=1, source_target_pairs={{0,120},{8,16},{16,8},{24,32},{32,24},{40,48},{48,40},{56,64},{64,... | collective-permute-start | bytes 12296 | tf_op jit(solution)/shard_map/ppermute | solution.py:518
  37.8 4.0 %collective-permute-start.12 = (f32[16,64]{1,0:T(8,128)S(1)}, f32[16,64]{1,0:T(8,128)S(1)}, u32[]{:S(2)}, u32[]{:S(2)}) collective-permute-start(f32[16,64]{1,0:T(8,128)S(1)} %shard_map.91.rest_4_), channel_id=1, source_target_pairs={{0,8},{8,0},{16,24},{24,16},{32,40},{40,32},{48,56},{56,48},{64,72... | collective-permute-start | bytes 12296 | tf_op jit(solution)/shard_map/ppermute | solution.py:518
  42.6 4.5 %collective-permute-start.16 = (f32[24,128]{1,0:T(8,128)S(1)}, f32[24,128]{1,0:T(8,128)S(1)}, u32[]{:S(2)}, u32[]{:S(2)}) collective-permute-start(f32[24,128]{1,0:T(8,128)S(1)} %get-tuple-element.83), channel_id=1, source_target_pairs={{0,8},{8,0},{16,24},{24,16},{32,40},{40,32},{48,56},{56,48},{64,72... | collective-permute-start | bytes 36872 | tf_op jit(solution)/shard_map/ppermute | solution.py:518
  42.7 5.9 %collective-permute-start.17 = (f32[24,128]{1,0:T(8,128)S(1)}, f32[24,128]{1,0:T(8,128)S(1)}, u32[]{:S(2)}, u32[]{:S(2)}) collective-permute-start(f32[24,128]{1,0:T(8,128)S(1)} %get-tuple-element.84), channel_id=1, source_target_pairs={{0,120},{8,16},{16,8},{24,32},{32,24},{40,48},{48,40},{56,64},{64,... | collective-permute-start | bytes 36872 | tf_op jit(solution)/shard_map/ppermute | solution.py:518
  45.3 3.3 %collective-permute-start.18 = (f32[24,128]{1,0:T(8,128)S(1)}, f32[24,128]{1,0:T(8,128)S(1)}, u32[]{:S(2)}, u32[]{:S(2)}) collective-permute-start(f32[24,128]{1,0:T(8,128)S(1)} %get-tuple-element.85), channel_id=1, source_target_pairs={{0,1},{1,0},{2,3},{3,2},{4,5},{5,4},{6,7},{7,6},{8,9},{9,8},{10,11... | collective-permute-start | bytes 36872 | tf_op jit(solution)/shard_map/ppermute | solution.py:518
  46.4 3.4 %collective-permute-start.19 = (f32[24,128]{1,0:T(8,128)S(1)}, f32[24,128]{1,0:T(8,128)S(1)}, u32[]{:S(2)}, u32[]{:S(2)}) collective-permute-start(f32[24,128]{1,0:T(8,128)S(1)} %get-tuple-element.86), channel_id=1, source_target_pairs={{0,7},{1,2},{2,1},{3,4},{4,3},{5,6},{6,5},{7,0},{8,15},{9,10},{10,... | collective-permute-start | bytes 36872 | tf_op jit(solution)/shard_map/ppermute | solution.py:518
  49.9 6.2 %collective-permute-start.23 = (f32[16,64]{1,0:T(8,128)S(1)}, f32[16,64]{1,0:T(8,128)S(1)}, u32[]{:S(2)}, u32[]{:S(2)}) collective-permute-start(f32[16,64]{1,0:T(8,128)S(1)} %shard_map.99.rest_4_), channel_id=1, source_target_pairs={{0,7},{1,2},{2,1},{3,4},{4,3},{5,6},{6,5},{7,0},{8,15},{9,10},{10,... | collective-permute-start | bytes 12296 | tf_op jit(solution)/shard_map/ppermute | solution.py:518
  50.7 5.4 %collective-permute-start.22 = (f32[16,64]{1,0:T(8,128)S(1)}, f32[16,64]{1,0:T(8,128)S(1)}, u32[]{:S(2)}, u32[]{:S(2)}) collective-permute-start(f32[16,64]{1,0:T(8,128)S(1)} %shard_map.99.rest_4_), channel_id=1, source_target_pairs={{0,1},{1,0},{2,3},{3,2},{4,5},{5,4},{6,7},{7,6},{8,9},{9,8},{10,11... | collective-permute-start | bytes 12296 | tf_op jit(solution)/shard_map/ppermute | solution.py:518
  53.0 5.8 %collective-permute-start.21 = (f32[16,64]{1,0:T(8,128)S(1)}, f32[16,64]{1,0:T(8,128)S(1)}, u32[]{:S(2)}, u32[]{:S(2)}) collective-permute-start(f32[16,64]{1,0:T(8,128)S(1)} %shard_map.99.rest_4_), channel_id=1, source_target_pairs={{0,120},{8,16},{16,8},{24,32},{32,24},{40,48},{48,40},{56,64},{64,... | collective-permute-start | bytes 12296 | tf_op jit(solution)/shard_map/ppermute | solution.py:518
  55.4 3.4 %collective-permute-start.20 = (f32[16,64]{1,0:T(8,128)S(1)}, f32[16,64]{1,0:T(8,128)S(1)}, u32[]{:S(2)}, u32[]{:S(2)}) collective-permute-start(f32[16,64]{1,0:T(8,128)S(1)} %shard_map.99.rest_4_), channel_id=1, source_target_pairs={{0,8},{8,0},{16,24},{24,16},{32,40},{40,32},{48,56},{56,48},{64,72... | collective-permute-start | bytes 12296 | tf_op jit(solution)/shard_map/ppermute | solution.py:518

commit v3 on v2

--- a/solution.py
+++ b/solution.py
@@ -454,21 +454,24 @@
 
 def closing_kernel(level, coef, heights, kappas, old_aux, lcols, state, member, *rest):
     tables = rest[:SLOTS]
-    out, table, held, wide, sems = rest[SLOTS:]
+    out, table, held, wide, scales, sems = rest[SLOTS:]
     fields, basis, n_elem = state.shape
     means = gather([t[...] for t in tables], table, member[...])
     height = heights[level : level + 1, :]
     weights = lift_weights(coef, height, means, old_aux, kappas)
     for k in range(3):
         wide[k] = jnp.broadcast_to(lcols[:, k : k + 1], (basis, 128))
-    copies = []
-    for f in range(fields):
+    for f in range(fields):
+        for k in range(3):
+            scales[f, k : k + 1, :] = weights[f][k]
+
+    def field(f, carry):
         for pair in range(n_elem // 256):
             lanes = [
                 slice(pair * 256 + part * 128, pair * 256 + part * 128 + 128) for part in range(2)
             ]
             scale = [
-                [jnp.broadcast_to(weights[f][k][:, at], (8, 128)) for k in range(3)]
+                [jnp.broadcast_to(scales[f, k : k + 1, at], (8, 128)) for k in range(3)]
                 for at in lanes
             ]
             for group in range(basis // 8):
@@ -479,10 +482,12 @@
                     for k in range(3):
                         value = value + vector[k] * scale[part][k]
                     held[f, lines, lanes[part]] = value
-        copies.append(pltpu.make_async_copy(held.at[f], out.at[f], sems.at[f]))
-        copies[-1].start()
-    for copy in copies:
-        copy.wait()
+        pltpu.make_async_copy(held.at[f], out.at[f], sems.at[f]).start()
+        return carry
+
+    lax.fori_loop(0, fields, field, 0)
+    for f in range(fields):
+        pltpu.make_async_copy(held.at[f], out.at[f], sems.at[f]).wait()
 
 
 def call(kernel, outs, args, scratch=(), scalars=0, flops=1000000, space=pltpu.VMEM, out_space=pltpu.VMEM, limit=40):
@@ -706,6 +711,7 @@
             table,
             pltpu.VMEM(state.shape, F32),
             pltpu.VMEM((3, basis, 128), F32),
+            pltpu.VMEM((fields, 8, n_elem), F32),
             pltpu.SemaphoreType.DMA((fields,)),
         ],
         out_space=pltpu.HBM,

time: 60.8 us -> 60.6 us (level)
  no operation moved by 1% of the time
where the time goes in v3:
time: 60.6 us; the launch traced here: 60.4 us
  starting transfers between devices  32.8 us (54%)
  Pallas kernels  15.7 us (26%)
  waiting for transfers between devices  11.5 us (19%)
    ppermute x24, starting transfers between devices, swap(): return lax.ppermute(x, axis, pairs)  32.8 us
    pallas_call x19, Pallas kernels, call(): pl.pallas_call(kernel, out_shape=shapes, in_specs=specs, out_specs=[pl.Bl...  15.7 us
    ppermute x24, waiting for transfers between devices, swap(): return lax.ppermute(x, axis, pairs)  11.5 us
  transfers between devices with their start and end apart: 24, of which 6 were waited for; matrix products, arithmetic and copies ran while one was open for 0% of the time, Pallas kernels for 17%

profile of v3, /device:TPU:1, one launch (start us, length us, event | category | flops | bytes accessed | tf_op | source)
XLA Modules:
  0.0 60.4 jit_solution(1384755779397962763)
XLA Ops:
  0.0 2.2 %shard_map.82 = (f32[8,120]{1,0:T(8,128)S(1)}, f32[1,120]{1,0:T(1,128)S(1)}, f32[16,512]{1,0:T(8,128)S(1)}, f32[24,128]{1,0:T(8,128)S(1)}, f32[24,128]{1,0:T(8,1...) custom-call(s32[1]{0:T(128)} %bitcast.me, ...), custom_call_target="tpu_custom_call" | custom-call | flops 1000000 | bytes 3087268 | tf_op jit(solution)/shard_map/pallas_call | solution.py:501
  2.2 2.2 %collective-permute-start = (f32[24,128]{1,0:T(8,128)S(1)}, f32[24,128]{1,0:T(8,128)S(1)}, u32[]{:S(2)}, u32[]{:S(2)}) collective-permute-start(f32[24,128]{1,0:T(8,128)S(1)} %get-tuple-element.47), channel_id=1, source_target_pairs={{0,8},{8,0},{16,24},{24,16},{32,40},{40,32},{48,56},{56,48},{64,72... | collective-permute-start | bytes 36872 | tf_op jit(solution)/shard_map/ppermute | solution.py:523
  4.4 5.4 %collective-permute-start.1 = (f32[24,128]{1,0:T(8,128)S(1)}, f32[24,128]{1,0:T(8,128)S(1)}, u32[]{:S(2)}, u32[]{:S(2)}) collective-permute-start(f32[24,128]{1,0:T(8,128)S(1)} %get-tuple-element.48), channel_id=1, source_target_pairs={{0,120},{8,16},{16,8},{24,32},{32,24},{40,48},{48,40},{56,64},{64,... | collective-permute-start | bytes 36872 | tf_op jit(solution)/shard_map/ppermute | solution.py:523
  9.8 1.2 %collective-permute-start.2 = (f32[24,128]{1,0:T(8,128)S(1)}, f32[24,128]{1,0:T(8,128)S(1)}, u32[]{:S(2)}, u32[]{:S(2)}) collective-permute-start(f32[24,128]{1,0:T(8,128)S(1)} %get-tuple-element.49), channel_id=1, source_target_pairs={{0,1},{1,0},{2,3},{3,2},{4,5},{5,4},{6,7},{7,6},{8,9},{9,8},{10,11... | collective-permute-start | bytes 36872 | tf_op jit(solution)/shard_map/ppermute | solution.py:523
  11.0 1.1 %collective-permute-start.3 = (f32[24,128]{1,0:T(8,128)S(1)}, f32[24,128]{1,0:T(8,128)S(1)}, u32[]{:S(2)}, u32[]{:S(2)}) collective-permute-start(f32[24,128]{1,0:T(8,128)S(1)} %get-tuple-element.50), channel_id=1, source_target_pairs={{0,7},{1,2},{2,1},{3,4},{4,3},{5,6},{6,5},{7,0},{8,15},{9,10},{10,... | collective-permute-start | bytes 36872 | tf_op jit(solution)/shard_map/ppermute | solution.py:523
  12.1 1.8 %shard_map.85 = (bf16[768,256]{1,0:T(8,128)(2,1)S(1)}, bf16[32,256]{1,0:T(8,128)(2,1)S(1)}, f32[120,16]{1,0:T(8,128)S(1)}, f32[16,512]{1,0:T(8,128)S(1)}) custom-call(f32[216,120]{1,0:T(8,128)S(1)} %get-tuple-element.56.basis, f32[216,120]{1,0:T(8,128)S(1)} %get-tuple-element.57.test, f32[8,120]{1,0:T(8,128)S(1)} %get-tuple-element.58.rows3, ...), custom_call_target="tpu_custom_call" | custom-call | flops 100000000 | bytes 1071328 | tf_op jit(solution)/shard_map/pallas_call | solution.py:501
  14.0 0.3 shard_map.86.proj
  14.3 0.2 shard_map.83
  14.5 0.0 collective-permute-done.1.refs_1_.rest_1_
  14.5 0.0 collective-permute-done.2.refs_2_.rest_2_
  14.6 0.1 shard_map.88.rest_4_
  14.7 0.8 %collective-permute-start.7 = (f32[16,64]{1,0:T(8,128)S(1)}, f32[16,64]{1,0:T(8,128)S(1)}, u32[]{:S(2)}, u32[]{:S(2)}) collective-permute-start(f32[16,64]{1,0:T(8,128)S(1)} %shard_map.88.rest_4_), channel_id=1, source_target_pairs={{0,7},{1,2},{2,1},{3,4},{4,3},{5,6},{6,5},{7,0},{8,15},{9,10},{10,... | collective-permute-start | bytes 12296 | tf_op jit(solution)/shard_map/ppermute | solution.py:523
  15.4 3.0 %collective-permute-start.6 = (f32[16,64]{1,0:T(8,128)S(1)}, f32[16,64]{1,0:T(8,128)S(1)}, u32[]{:S(2)}, u32[]{:S(2)}) collective-permute-start(f32[16,64]{1,0:T(8,128)S(1)} %shard_map.88.rest_4_), channel_id=1, source_target_pairs={{0,1},{1,0},{2,3},{3,2},{4,5},{5,4},{6,7},{7,6},{8,9},{9,8},{10,11... | collective-permute-start | bytes 12296 | tf_op jit(solution)/shard_map/ppermute | solution.py:523
  18.4 0.6 %collective-permute-start.5 = (f32[16,64]{1,0:T(8,128)S(1)}, f32[16,64]{1,0:T(8,128)S(1)}, u32[]{:S(2)}, u32[]{:S(2)}) collective-permute-start(f32[16,64]{1,0:T(8,128)S(1)} %shard_map.88.rest_4_), channel_id=1, source_target_pairs={{0,120},{8,16},{16,8},{24,32},{32,24},{40,48},{48,40},{56,64},{64,... | collective-permute-start | bytes 12296 | tf_op jit(solution)/shard_map/ppermute | solution.py:523
  19.1 0.3 shard_map.84.heights
  19.4 0.7 %shard_map.93.rest_0_ = f32[5,384,256]{2,1,0:T(8,128)S(1)} custom-call(f32[5,120,512]{2,1,0:T(8,128)S(1)} %get-tuple-element.63.state, f32[5,5,512]{2,1,0:T(8,128)S(1)} %get-tuple-element.46.coef, f32[8,512]{1,0:T(8,128)S(1)} %shard_map.84.heights, bf16[768,256]{1,0:T(8,128)(2,1)S(1)} %get-tuple-element.75.stack), custom_call_target="tpu_custom_call" | custom-call | flops 3000000000 | bytes 4048896 | tf_op jit(solution)/shard_map/pallas_call | solution.py:501
  20.1 2.0 %shard_map.94 = (f32[5,120,512]{2,1,0:T(8,128)S(1)}, f32[5,384,256]{2,1,0:T(8,128)S(1)}) custom-call(f32[5,120,512]{2,1,0:T(8,128)S(1)} %get-tuple-element.63.state, f32[5,5,512]{2,1,0:T(8,128)S(1)} %get-tuple-element.46.coef, f32[8,512]{1,0:T(8,128)S(1)} %shard_map.84.heights, bf16[768,256]{1,0:T(8,128)(2,1)S(1)} %get-tuple-element.75.stack, ...), custom_call_target="tpu_custom_call" | custom-call | flops 3000000000 | bytes 7243776 | tf_op jit(solution)/shard_map/pallas_call | solution.py:501
  22.1 0.1 shard_map.87.drift
  22.3 2.0 %collective-permute-done.5.rest_1_ = f32[16,64]{1,0:T(8,128)S(1)} collective-permute-done((f32[16,64]{1,0:T(8,128)S(1)}, f32[16,64]{1,0:T(8,128)S(1)}, u32[]{:S(2)}, u32[]{:S(2)}) %collective-permute-start.5) | collective-permute-done | bytes 4128 | tf_op jit(solution)/shard_map/ppermute | solution.py:523
  24.2 0.0 collective-permute-done.4.rest_0_
  24.3 0.8 %shard_map.89 = (f32[5,8,512]{2,1,0:T(8,128)S(1)}, f32[16,512]{1,0:T(8,128)S(1)}, f32[24,128]{1,0:T(8,128)S(1)}, f32[24,128]{1,0:T(8,128)S(1)}, f32[24,128]{1,0:...) custom-call(f32[5,5,512]{2,1,0:T(8,128)S(1)} %get-tuple-element.46.coef, ...), custom_call_target="tpu_custom_call" | custom-call | flops 1000000 | bytes 1804288 | tf_op jit(solution)/shard_map/pallas_call | solution.py:501
  25.0 0.1 collective-permute-start.8
  25.1 3.7 %collective-permute-start.9 = (f32[24,128]{1,0:T(8,128)S(1)}, f32[24,128]{1,0:T(8,128)S(1)}, u32[]{:S(2)}, u32[]{:S(2)}) collective-permute-start(f32[24,128]{1,0:T(8,128)S(1)} %get-tuple-element.68), channel_id=1, source_target_pairs={{0,120},{8,16},{16,8},{24,32},{32,24},{40,48},{48,40},{56,64},{64,... | collective-permute-start | bytes 36872 | tf_op jit(solution)/shard_map/ppermute | solution.py:523
  28.8 1.1 %collective-permute-start.10 = (f32[24,128]{1,0:T(8,128)S(1)}, f32[24,128]{1,0:T(8,128)S(1)}, u32[]{:S(2)}, u32[]{:S(2)}) collective-permute-start(f32[24,128]{1,0:T(8,128)S(1)} %get-tuple-element.69), channel_id=1, source_target_pairs={{0,1},{1,0},{2,3},{3,2},{4,5},{5,4},{6,7},{7,6},{8,9},{9,8},{10,11... | collective-permute-start | bytes 36872 | tf_op jit(solution)/shard_map/ppermute | solution.py:523
  29.9 1.2 %shard_map.95 = (f32[5,120,512]{2,1,0:T(8,128)S(1)}, f32[5,384,256]{2,1,0:T(8,128)S(1)}) custom-call(f32[5,120,512]{2,1,0:T(8,128)S(1)} %get-tuple-element.76.state, f32[5,5,512]{2,1,0:T(8,128)S(1)} %get-tuple-element.46.coef, f32[8,512]{1,0:T(8,128)S(1)} %shard_map.84.heights, bf16[768,256]{1,0:T(8,128)(2,1)S(1)} %get-tuple-element.75.stack, ...), custom_call_target="tpu_custom_call" | custom-call | flops 3000000000 | bytes 7243776 | tf_op jit(solution)/shard_map/pallas_call | solution.py:501
  31.2 2.2 %collective-permute-done.11.rest_3_ = f32[24,128]{1,0:T(8,128)S(1)} collective-permute-done((f32[24,128]{1,0:T(8,128)S(1)}, f32[24,128]{1,0:T(8,128)S(1)}, u32[]{:S(2)}, u32[]{:S(2)}) %collective-permute-start.11) | collective-permute-done | bytes 12320 | tf_op jit(solution)/shard_map/ppermute | solution.py:523
  33.3 0.1 shard_map.91.rest_4_
  33.4 0.9 %collective-permute-start.15 = (f32[16,64]{1,0:T(8,128)S(1)}, f32[16,64]{1,0:T(8,128)S(1)}, u32[]{:S(2)}, u32[]{:S(2)}) collective-permute-start(f32[16,64]{1,0:T(8,128)S(1)} %shard_map.91.rest_4_), channel_id=1, source_target_pairs={{0,7},{1,2},{2,1},{3,4},{4,3},{5,6},{6,5},{7,0},{8,15},{9,10},{10,... | collective-permute-start | bytes 12296 | tf_op jit(solution)/shard_map/ppermute | solution.py:523
  34.3 1.7 %collective-permute-start.14 = (f32[16,64]{1,0:T(8,128)S(1)}, f32[16,64]{1,0:T(8,128)S(1)}, u32[]{:S(2)}, u32[]{:S(2)}) collective-permute-start(f32[16,64]{1,0:T(8,128)S(1)} %shard_map.91.rest_4_), channel_id=1, source_target_pairs={{0,1},{1,0},{2,3},{3,2},{4,5},{5,4},{6,7},{7,6},{8,9},{9,8},{10,11... | collective-permute-start | bytes 12296 | tf_op jit(solution)/shard_map/ppermute | solution.py:523
  36.0 1.8 %collective-permute-start.13 = (f32[16,64]{1,0:T(8,128)S(1)}, f32[16,64]{1,0:T(8,128)S(1)}, u32[]{:S(2)}, u32[]{:S(2)}) collective-permute-start(f32[16,64]{1,0:T(8,128)S(1)} %shard_map.91.rest_4_), channel_id=1, source_target_pairs={{0,120},{8,16},{16,8},{24,32},{32,24},{40,48},{48,40},{56,64},{64,... | collective-permute-start | bytes 12296 | tf_op jit(solution)/shard_map/ppermute | solution.py:523
  37.8 0.0 collective-permute-start.12
  37.8 2.0 %shard_map.96 = (f32[5,120,512]{2,1,0:T(8,128)S(1)}, f32[5,384,256]{2,1,0:T(8,128)S(1)}) custom-call(f32[5,120,512]{2,1,0:T(8,128)S(1)} %get-tuple-element.78.state, f32[5,5,512]{2,1,0:T(8,128)S(1)} %get-tuple-element.46.coef, f32[8,512]{1,0:T(8,128)S(1)} %shard_map.84.heights, bf16[768,256]{1,0:T(8,128)(2,1)S(1)} %get-tuple-element.75.stack, ...), custom_call_target="tpu_custom_call" | custom-call | flops 3000000000 | bytes 7243776 | tf_op jit(solution)/shard_map/pallas_call | solution.py:501
  39.8 0.1 shard_map.90.drift
  40.0 1.8 %collective-permute-done.13.rest_1_ = f32[16,64]{1,0:T(8,128)S(1)} collective-permute-done((f32[16,64]{1,0:T(8,128)S(1)}, f32[16,64]{1,0:T(8,128)S(1)}, u32[]{:S(2)}, u32[]{:S(2)}) %collective-permute-start.13) | collective-permute-done | bytes 4128 | tf_op jit(solution)/shard_map/ppermute | solution.py:523
  41.8 0.8 %shard_map.92 = (f32[5,8,512]{2,1,0:T(8,128)S(1)}, f32[16,512]{1,0:T(8,128)S(1)}, f32[24,128]{1,0:T(8,128)S(1)}, f32[24,128]{1,0:T(8,128)S(1)}, f32[24,128]{1,0:...) custom-call(f32[5,5,512]{2,1,0:T(8,128)S(1)} %get-tuple-element.46.coef, f32[8,512]{1,0:T(8,128)S(1)} %shard_map.84.heights, ...), custom_call_target="tpu_custom_call" | custom-call | flops 1000000 | bytes 1722368 | tf_op jit(solution)/shard_map/pallas_call | solution.py:501
  42.6 0.1 collective-permute-start.16
  42.7 2.6 %collective-permute-start.17 = (f32[24,128]{1,0:T(8,128)S(1)}, f32[24,128]{1,0:T(8,128)S(1)}, u32[]{:S(2)}, u32[]{:S(2)}) collective-permute-start(f32[24,128]{1,0:T(8,128)S(1)} %get-tuple-element.84), channel_id=1, source_target_pairs={{0,120},{8,16},{16,8},{24,32},{32,24},{40,48},{48,40},{56,64},{64,... | collective-permute-start | bytes 36872 | tf_op jit(solution)/shard_map/ppermute | solution.py:523
  45.3 1.1 %collective-permute-start.18 = (f32[24,128]{1,0:T(8,128)S(1)}, f32[24,128]{1,0:T(8,128)S(1)}, u32[]{:S(2)}, u32[]{:S(2)}) collective-permute-start(f32[24,128]{1,0:T(8,128)S(1)} %get-tuple-element.85), channel_id=1, source_target_pairs={{0,1},{1,0},{2,3},{3,2},{4,5},{5,4},{6,7},{7,6},{8,9},{9,8},{10,11... | collective-permute-start | bytes 36872 | tf_op jit(solution)/shard_map/ppermute | solution.py:523
  46.4 0.6 %shard_map.97.state = f32[5,120,512]{2,1,0:T(8,128)S(1)} custom-call(f32[5,120,512]{2,1,0:T(8,128)S(1)} %get-tuple-element.80.state, f32[5,5,512]{2,1,0:T(8,128)S(1)} %get-tuple-element.46.coef, f32[8,512]{1,0:T(8,128)S(1)} %shard_map.84.heights, bf16[768,256]{1,0:T(8,128)(2,1)S(1)} %get-tuple-element.75.stack, f32[5,384,256]{2,1,0:T(8,128)S(1)} %get-tuple-element.81.rest_0_), custom_call_target="tpu_custom_call" | custom-call | flops 3000000000 | bytes 5277696 | tf_op jit(solution)/shard_map/pallas_call | solution.py:501
  47.1 1.5 %collective-permute-done.17.rest_1_ = f32[24,128]{1,0:T(8,128)S(1)} collective-permute-done((f32[24,128]{1,0:T(8,128)S(1)}, f32[24,128]{1,0:T(8,128)S(1)}, u32[]{:S(2)}, u32[]{:S(2)}) %collective-permute-start.17) | collective-permute-done | bytes 12320 | tf_op jit(solution)/shard_map/ppermute | solution.py:523
  48.6 1.2 %collective-permute-done.19.rest_3_ = f32[24,128]{1,0:T(8,128)S(1)} collective-permute-done((f32[24,128]{1,0:T(8,128)S(1)}, f32[24,128]{1,0:T(8,128)S(1)}, u32[]{:S(2)}, u32[]{:S(2)}) %collective-permute-start.19) | collective-permute-done | bytes 12320 | tf_op jit(solution)/shard_map/ppermute | solution.py:523
  49.8 0.1 shard_map.99.rest_4_
  49.9 0.8 %collective-permute-start.23 = (f32[16,64]{1,0:T(8,128)S(1)}, f32[16,64]{1,0:T(8,128)S(1)}, u32[]{:S(2)}, u32[]{:S(2)}) collective-permute-start(f32[16,64]{1,0:T(8,128)S(1)} %shard_map.99.rest_4_), channel_id=1, source_target_pairs={{0,7},{1,2},{2,1},{3,4},{4,3},{5,6},{6,5},{7,0},{8,15},{9,10},{10,... | collective-permute-start | bytes 12296 | tf_op jit(solution)/shard_map/ppermute | solution.py:523
  50.7 2.3 %collective-permute-start.22 = (f32[16,64]{1,0:T(8,128)S(1)}, f32[16,64]{1,0:T(8,128)S(1)}, u32[]{:S(2)}, u32[]{:S(2)}) collective-permute-start(f32[16,64]{1,0:T(8,128)S(1)} %shard_map.99.rest_4_), channel_id=1, source_target_pairs={{0,1},{1,0},{2,3},{3,2},{4,5},{5,4},{6,7},{7,6},{8,9},{9,8},{10,11... | collective-permute-start | bytes 12296 | tf_op jit(solution)/shard_map/ppermute | solution.py:523
  53.0 2.4 %collective-permute-start.21 = (f32[16,64]{1,0:T(8,128)S(1)}, f32[16,64]{1,0:T(8,128)S(1)}, u32[]{:S(2)}, u32[]{:S(2)}) collective-permute-start(f32[16,64]{1,0:T(8,128)S(1)} %shard_map.99.rest_4_), channel_id=1, source_target_pairs={{0,120},{8,16},{16,8},{24,32},{32,24},{40,48},{48,40},{56,64},{64,... | collective-permute-start | bytes 12296 | tf_op jit(solution)/shard_map/ppermute | solution.py:523
  55.4 0.7 %shard_map.98.state = f32[5,120,512]{2,1,0:T(8,128)S(1)} custom-call(f32[5,5,512]{2,1,0:T(8,128)S(1)} %get-tuple-element.46.coef, f32[8,512]{1,0:T(8,128)S(1)} %shard_map.84.heights, f32[5,8,512]{2,1,0:T(8,128)S(1)} %get-tuple-element.73.weights0, f32[5,8,512]{2,1,0:T(8,128)S(1)} %get-tuple-element.74.weights1, f32[120,16]{1,0:T(8,128)S(1)} %get-tuple-element.72.lcols, ...), custom_call_target="tpu_custom_call" | custom-call | flops 100000000 | bytes 2696704 | tf_op jit(solution)/shard_map/pallas_call | solution.py:501
  56.1 2.7 %collective-permute-done.21.rest_1_ = f32[16,64]{1,0:T(8,128)S(1)} collective-permute-done((f32[16,64]{1,0:T(8,128)S(1)}, f32[16,64]{1,0:T(8,128)S(1)}, u32[]{:S(2)}, u32[]{:S(2)}) %collective-permute-start.21) | collective-permute-done | bytes 4128 | tf_op jit(solution)/shard_map/ppermute | solution.py:523
  58.8 1.4 %shard_map.100 = f32[5,120,512]{2,1,0:T(8,128)} custom-call(f32[5,5,512]{2,1,0:T(8,128)S(1)} %get-tuple-element.46.coef, f32[8,512]{1,0:T(8,128)S(1)} %shard_map.84.heights, f32[16,512]{1,0:T(8,128)S(1)} %get-tuple-element.60.kappas, f32[16,512]{1,0:T(8,128)S(1)} %get-tuple-element.71.old_aux, f32[120,16]{1,0:T(8,128)S(1)} %get-tuple-element.72.lcols, ...), custom_call_target="tpu_custom_call" | custom-call | flops 1000000 | bytes 3274240 | tf_op jit(solution)/shard_map/pallas_call | solution.py:501
  (19 shorter events, 0.0 us)
Async XLA Ops:
  2.2 12.3 %collective-permute-start = (f32[24,128]{1,0:T(8,128)S(1)}, f32[24,128]{1,0:T(8,128)S(1)}, u32[]{:S(2)}, u32[]{:S(2)}) collective-permute-start(f32[24,128]{1,0:T(8,128)S(1)} %get-tuple-element.47), channel_id=1, source_target_pairs={{0,8},{8,0},{16,24},{24,16},{32,40},{40,32},{48,56},{56,48},{64,72... | collective-permute-start | bytes 36872 | tf_op jit(solution)/shard_map/ppermute | solution.py:523
  4.4 10.1 %collective-permute-start.1 = (f32[24,128]{1,0:T(8,128)S(1)}, f32[24,128]{1,0:T(8,128)S(1)}, u32[]{:S(2)}, u32[]{:S(2)}) collective-permute-start(f32[24,128]{1,0:T(8,128)S(1)} %get-tuple-element.48), channel_id=1, source_target_pairs={{0,120},{8,16},{16,8},{24,32},{32,24},{40,48},{48,40},{56,64},{64,... | collective-permute-start | bytes 36872 | tf_op jit(solution)/shard_map/ppermute | solution.py:523
  9.8 4.7 %collective-permute-start.2 = (f32[24,128]{1,0:T(8,128)S(1)}, f32[24,128]{1,0:T(8,128)S(1)}, u32[]{:S(2)}, u32[]{:S(2)}) collective-permute-start(f32[24,128]{1,0:T(8,128)S(1)} %get-tuple-element.49), channel_id=1, source_target_pairs={{0,1},{1,0},{2,3},{3,2},{4,5},{5,4},{6,7},{7,6},{8,9},{9,8},{10,11... | collective-permute-start | bytes 36872 | tf_op jit(solution)/shard_map/ppermute | solution.py:523
  11.0 3.5 %collective-permute-start.3 = (f32[24,128]{1,0:T(8,128)S(1)}, f32[24,128]{1,0:T(8,128)S(1)}, u32[]{:S(2)}, u32[]{:S(2)}) collective-permute-start(f32[24,128]{1,0:T(8,128)S(1)} %get-tuple-element.50), channel_id=1, source_target_pairs={{0,7},{1,2},{2,1},{3,4},{4,3},{5,6},{6,5},{7,0},{8,15},{9,10},{10,... | collective-permute-start | bytes 36872 | tf_op jit(solution)/shard_map/ppermute | solution.py:523
  14.7 7.6 %collective-permute-start.7 = (f32[16,64]{1,0:T(8,128)S(1)}, f32[16,64]{1,0:T(8,128)S(1)}, u32[]{:S(2)}, u32[]{:S(2)}) collective-permute-start(f32[16,64]{1,0:T(8,128)S(1)} %shard_map.88.rest_4_), channel_id=1, source_target_pairs={{0,7},{1,2},{2,1},{3,4},{4,3},{5,6},{6,5},{7,0},{8,15},{9,10},{10,... | collective-permute-start | bytes 12296 | tf_op jit(solution)/shard_map/ppermute | solution.py:523
  15.4 6.8 %collective-permute-start.6 = (f32[16,64]{1,0:T(8,128)S(1)}, f32[16,64]{1,0:T(8,128)S(1)}, u32[]{:S(2)}, u32[]{:S(2)}) collective-permute-start(f32[16,64]{1,0:T(8,128)S(1)} %shard_map.88.rest_4_), channel_id=1, source_target_pairs={{0,1},{1,0},{2,3},{3,2},{4,5},{5,4},{6,7},{7,6},{8,9},{9,8},{10,11... | collective-permute-start | bytes 12296 | tf_op jit(solution)/shard_map/ppermute | solution.py:523
  18.4 5.8 %collective-permute-start.5 = (f32[16,64]{1,0:T(8,128)S(1)}, f32[16,64]{1,0:T(8,128)S(1)}, u32[]{:S(2)}, u32[]{:S(2)}) collective-permute-start(f32[16,64]{1,0:T(8,128)S(1)} %shard_map.88.rest_4_), channel_id=1, source_target_pairs={{0,120},{8,16},{16,8},{24,32},{32,24},{40,48},{48,40},{56,64},{64,... | collective-permute-start | bytes 12296 | tf_op jit(solution)/shard_map/ppermute | solution.py:523
  19.1 5.2 %collective-permute-start.4 = (f32[16,64]{1,0:T(8,128)S(1)}, f32[16,64]{1,0:T(8,128)S(1)}, u32[]{:S(2)}, u32[]{:S(2)}) collective-permute-start(f32[16,64]{1,0:T(8,128)S(1)} %shard_map.88.rest_4_), channel_id=1, source_target_pairs={{0,8},{8,0},{16,24},{24,16},{32,40},{40,32},{48,56},{56,48},{64,72... | collective-permute-start | bytes 12296 | tf_op jit(solution)/shard_map/ppermute | solution.py:523
  25.0 6.1 %collective-permute-start.8 = (f32[24,128]{1,0:T(8,128)S(1)}, f32[24,128]{1,0:T(8,128)S(1)}, u32[]{:S(2)}, u32[]{:S(2)}) collective-permute-start(f32[24,128]{1,0:T(8,128)S(1)} %get-tuple-element.67), channel_id=1, source_target_pairs={{0,8},{8,0},{16,24},{24,16},{32,40},{40,32},{48,56},{56,48},{64,72... | collective-permute-start | bytes 36872 | tf_op jit(solution)/shard_map/ppermute | solution.py:523
  25.1 6.0 %collective-permute-start.9 = (f32[24,128]{1,0:T(8,128)S(1)}, f32[24,128]{1,0:T(8,128)S(1)}, u32[]{:S(2)}, u32[]{:S(2)}) collective-permute-start(f32[24,128]{1,0:T(8,128)S(1)} %get-tuple-element.68), channel_id=1, source_target_pairs={{0,120},{8,16},{16,8},{24,32},{32,24},{40,48},{48,40},{56,64},{64,... | collective-permute-start | bytes 36872 | tf_op jit(solution)/shard_map/ppermute | solution.py:523
  28.8 2.4 %collective-permute-start.10 = (f32[24,128]{1,0:T(8,128)S(1)}, f32[24,128]{1,0:T(8,128)S(1)}, u32[]{:S(2)}, u32[]{:S(2)}) collective-permute-start(f32[24,128]{1,0:T(8,128)S(1)} %get-tuple-element.69), channel_id=1, source_target_pairs={{0,1},{1,0},{2,3},{3,2},{4,5},{5,4},{6,7},{7,6},{8,9},{9,8},{10,11... | collective-permute-start | bytes 36872 | tf_op jit(solution)/shard_map/ppermute | solution.py:523
  29.9 3.4 %collective-permute-start.11 = (f32[24,128]{1,0:T(8,128)S(1)}, f32[24,128]{1,0:T(8,128)S(1)}, u32[]{:S(2)}, u32[]{:S(2)}) collective-permute-start(f32[24,128]{1,0:T(8,128)S(1)} %get-tuple-element.70), channel_id=1, source_target_pairs={{0,7},{1,2},{2,1},{3,4},{4,3},{5,6},{6,5},{7,0},{8,15},{9,10},{10,... | collective-permute-start | bytes 36872 | tf_op jit(solution)/shard_map/ppermute | solution.py:523
  33.4 6.5 %collective-permute-start.15 = (f32[16,64]{1,0:T(8,128)S(1)}, f32[16,64]{1,0:T(8,128)S(1)}, u32[]{:S(2)}, u32[]{:S(2)}) collective-permute-start(f32[16,64]{1,0:T(8,128)S(1)} %shard_map.91.rest_4_), channel_id=1, source_target_pairs={{0,7},{1,2},{2,1},{3,4},{4,3},{5,6},{6,5},{7,0},{8,15},{9,10},{10,... | collective-permute-start | bytes 12296 | tf_op jit(solution)/shard_map/ppermute | solution.py:523
  34.3 5.7 %collective-permute-start.14 = (f32[16,64]{1,0:T(8,128)S(1)}, f32[16,64]{1,0:T(8,128)S(1)}, u32[]{:S(2)}, u32[]{:S(2)}) collective-permute-start(f32[16,64]{1,0:T(8,128)S(1)} %shard_map.91.rest_4_), channel_id=1, source_target_pairs={{0,1},{1,0},{2,3},{3,2},{4,5},{5,4},{6,7},{7,6},{8,9},{9,8},{10,11... | collective-permute-start | bytes 12296 | tf_op jit(solution)/shard_map/ppermute | solution.py:523
  36.0 5.8 %collective-permute-start.13 = (f32[16,64]{1,0:T(8,128)S(1)}, f32[16,64]{1,0:T(8,128)S(1)}, u32[]{:S(2)}, u32[]{:S(2)}) collective-permute-start(f32[16,64]{1,0:T(8,128)S(1)} %shard_map.91.rest_4_), channel_id=1, source_target_pairs={{0,120},{8,16},{16,8},{24,32},{32,24},{40,48},{48,40},{56,64},{64,... | collective-permute-start | bytes 12296 | tf_op jit(solution)/shard_map/ppermute | solution.py:523
  37.8 4.0 %collective-permute-start.12 = (f32[16,64]{1,0:T(8,128)S(1)}, f32[16,64]{1,0:T(8,128)S(1)}, u32[]{:S(2)}, u32[]{:S(2)}) collective-permute-start(f32[16,64]{1,0:T(8,128)S(1)} %shard_map.91.rest_4_), channel_id=1, source_target_pairs={{0,8},{8,0},{16,24},{24,16},{32,40},{40,32},{48,56},{56,48},{64,72... | collective-permute-start | bytes 12296 | tf_op jit(solution)/shard_map/ppermute | solution.py:523
  42.6 4.5 %collective-permute-start.16 = (f32[24,128]{1,0:T(8,128)S(1)}, f32[24,128]{1,0:T(8,128)S(1)}, u32[]{:S(2)}, u32[]{:S(2)}) collective-permute-start(f32[24,128]{1,0:T(8,128)S(1)} %get-tuple-element.83), channel_id=1, source_target_pairs={{0,8},{8,0},{16,24},{24,16},{32,40},{40,32},{48,56},{56,48},{64,72... | collective-permute-start | bytes 36872 | tf_op jit(solution)/shard_map/ppermute | solution.py:523
  42.7 5.9 %collective-permute-start.17 = (f32[24,128]{1,0:T(8,128)S(1)}, f32[24,128]{1,0:T(8,128)S(1)}, u32[]{:S(2)}, u32[]{:S(2)}) collective-permute-start(f32[24,128]{1,0:T(8,128)S(1)} %get-tuple-element.84), channel_id=1, source_target_pairs={{0,120},{8,16},{16,8},{24,32},{32,24},{40,48},{48,40},{56,64},{64,... | collective-permute-start | bytes 36872 | tf_op jit(solution)/shard_map/ppermute | solution.py:523
  45.3 3.3 %collective-permute-start.18 = (f32[24,128]{1,0:T(8,128)S(1)}, f32[24,128]{1,0:T(8,128)S(1)}, u32[]{:S(2)}, u32[]{:S(2)}) collective-permute-start(f32[24,128]{1,0:T(8,128)S(1)} %get-tuple-element.85), channel_id=1, source_target_pairs={{0,1},{1,0},{2,3},{3,2},{4,5},{5,4},{6,7},{7,6},{8,9},{9,8},{10,11... | collective-permute-start | bytes 36872 | tf_op jit(solution)/shard_map/ppermute | solution.py:523
  46.4 3.4 %collective-permute-start.19 = (f32[24,128]{1,0:T(8,128)S(1)}, f32[24,128]{1,0:T(8,128)S(1)}, u32[]{:S(2)}, u32[]{:S(2)}) collective-permute-start(f32[24,128]{1,0:T(8,128)S(1)} %get-tuple-element.86), channel_id=1, source_target_pairs={{0,7},{1,2},{2,1},{3,4},{4,3},{5,6},{6,5},{7,0},{8,15},{9,10},{10,... | collective-permute-start | bytes 36872 | tf_op jit(solution)/shard_map/ppermute | solution.py:523
  49.9 6.2 %collective-permute-start.23 = (f32[16,64]{1,0:T(8,128)S(1)}, f32[16,64]{1,0:T(8,128)S(1)}, u32[]{:S(2)}, u32[]{:S(2)}) collective-permute-start(f32[16,64]{1,0:T(8,128)S(1)} %shard_map.99.rest_4_), channel_id=1, source_target_pairs={{0,7},{1,2},{2,1},{3,4},{4,3},{5,6},{6,5},{7,0},{8,15},{9,10},{10,... | collective-permute-start | bytes 12296 | tf_op jit(solution)/shard_map/ppermute | solution.py:523
  50.7 5.4 %collective-permute-start.22 = (f32[16,64]{1,0:T(8,128)S(1)}, f32[16,64]{1,0:T(8,128)S(1)}, u32[]{:S(2)}, u32[]{:S(2)}) collective-permute-start(f32[16,64]{1,0:T(8,128)S(1)} %shard_map.99.rest_4_), channel_id=1, source_target_pairs={{0,1},{1,0},{2,3},{3,2},{4,5},{5,4},{6,7},{7,6},{8,9},{9,8},{10,11... | collective-permute-start | bytes 12296 | tf_op jit(solution)/shard_map/ppermute | solution.py:523
  53.0 5.8 %collective-permute-start.21 = (f32[16,64]{1,0:T(8,128)S(1)}, f32[16,64]{1,0:T(8,128)S(1)}, u32[]{:S(2)}, u32[]{:S(2)}) collective-permute-start(f32[16,64]{1,0:T(8,128)S(1)} %shard_map.99.rest_4_), channel_id=1, source_target_pairs={{0,120},{8,16},{16,8},{24,32},{32,24},{40,48},{48,40},{56,64},{64,... | collective-permute-start | bytes 12296 | tf_op jit(solution)/shard_map/ppermute | solution.py:523
  55.4 3.4 %collective-permute-start.20 = (f32[16,64]{1,0:T(8,128)S(1)}, f32[16,64]{1,0:T(8,128)S(1)}, u32[]{:S(2)}, u32[]{:S(2)}) collective-permute-start(f32[16,64]{1,0:T(8,128)S(1)} %shard_map.99.rest_4_), channel_id=1, source_target_pairs={{0,8},{8,0},{16,24},{24,16},{32,40},{40,32},{48,56},{56,48},{64,72... | collective-permute-start | bytes 12296 | tf_op jit(solution)/shard_map/ppermute | solution.py:523

commit v4 on v3

--- a/solution.py
+++ b/solution.py
@@ -433,8 +433,10 @@
     return [held[f, 8 : 8 + count, :] + height * value[f] for f in range(fields)]
 
 
-def lift_kernel(coef, heights, weights0, weights1, lcols, state, out, held):
-    fields, _, _ = out.shape
+def lift_kernel(coef, heights, weights0, weights1, lcols, state, out, wide, held):
+    fields, basis, _ = out.shape
+    for k in range(3):
+        wide[k] = jnp.broadcast_to(lcols[:, k : k + 1], (basis, 128))
     held[...] = jnp.zeros_like(held)
     for f in range(fields):
         held[f, 8:11, :] = weights0[f, 0:3, :]
@@ -452,15 +454,13 @@
         out[f] = state[f] + jnp.dot(left, right, preferred_element_type=F32)
 
 
-def closing_kernel(level, coef, heights, kappas, old_aux, lcols, state, member, *rest):
+def closing_kernel(level, coef, heights, kappas, old_aux, wide, state, member, *rest):
     tables = rest[:SLOTS]
-    out, table, held, wide, scales, sems = rest[SLOTS:]
+    out, table, held, scales, sems = rest[SLOTS:]
     fields, basis, n_elem = state.shape
     means = gather([t[...] for t in tables], table, member[...])
     height = heights[level : level + 1, :]
     weights = lift_weights(coef, height, means, old_aux, kappas)
-    for k in range(3):
-        wide[k] = jnp.broadcast_to(lcols[:, k : k + 1], (basis, 128))
     for f in range(fields):
         for k in range(3):
             scales[f, k : k + 1, :] = weights[f][k]
@@ -696,9 +696,9 @@
                 proj = out.pop()
     for part in range(len(PARTS)):
         values, held = advance_state(values, held, part)
-    values = call(
+    values, wide = call(
         lift_kernel,
-        shaped(fields, basis, n_elem),
+        [shaped(fields, basis, n_elem), shaped(3, basis, 128)],
         (coef, heights, weights[0], weights[1], lcols, values),
         [pltpu.VMEM((fields, 24, n_elem), F32)],
         flops=100000000,
@@ -706,11 +706,10 @@
     return call(
         functools.partial(closing_kernel, levels - 1),
         shaped(fields, basis, n_elem),
-        (coef, heights, kappas, aux, lcols, values, memberships[levels - 1], *back, means),
+        (coef, heights, kappas, aux, wide, values, memberships[levels - 1], *back, means),
         [
             table,
             pltpu.VMEM(state.shape, F32),
-            pltpu.VMEM((3, basis, 128), F32),
             pltpu.VMEM((fields, 8, n_elem), F32),
             pltpu.SemaphoreType.DMA((fields,)),
         ],

time: 60.6 us -> 60.6 us (level)
  no operation moved by 1% of the time
where the time goes in v4:
time: 60.6 us; the launch traced here: 60.4 us
  starting transfers between devices  32.8 us (54%)
  Pallas kernels  15.7 us (26%)
  waiting for transfers between devices  11.4 us (19%)
    ppermute x24, starting transfers between devices, swap(): return lax.ppermute(x, axis, pairs)  32.8 us
    pallas_call x19, Pallas kernels, call(): pl.pallas_call(kernel, out_shape=shapes, in_specs=specs, out_specs=[pl.Bl...  15.7 us
    ppermute x24, waiting for transfers between devices, swap(): return lax.ppermute(x, axis, pairs)  11.4 us
  transfers between devices with their start and end apart: 24, of which 6 were waited for; matrix products, arithmetic and copies ran while one was open for 0% of the time, Pallas kernels for 17%

profile of v4, /device:TPU:1, one launch (start us, length us, event | category | flops | bytes accessed | tf_op | source)
XLA Modules:
  0.0 60.4 jit_solution(5134471512804374802)
XLA Ops:
  0.0 2.2 %shard_map.82 = (f32[8,120]{1,0:T(8,128)S(1)}, f32[1,120]{1,0:T(1,128)S(1)}, f32[16,512]{1,0:T(8,128)S(1)}, f32[24,128]{1,0:T(8,128)S(1)}, f32[24,128]{1,0:T(8,1...) custom-call(s32[1]{0:T(128)} %bitcast.me, ...), custom_call_target="tpu_custom_call" | custom-call | flops 1000000 | bytes 3087268 | tf_op jit(solution)/shard_map/pallas_call | solution.py:501
  2.2 2.2 %collective-permute-start = (f32[24,128]{1,0:T(8,128)S(1)}, f32[24,128]{1,0:T(8,128)S(1)}, u32[]{:S(2)}, u32[]{:S(2)}) collective-permute-start(f32[24,128]{1,0:T(8,128)S(1)} %get-tuple-element.49), channel_id=1, source_target_pairs={{0,8},{8,0},{16,24},{24,16},{32,40},{40,32},{48,56},{56,48},{64,72... | collective-permute-start | bytes 36872 | tf_op jit(solution)/shard_map/ppermute | solution.py:523
  4.4 5.4 %collective-permute-start.1 = (f32[24,128]{1,0:T(8,128)S(1)}, f32[24,128]{1,0:T(8,128)S(1)}, u32[]{:S(2)}, u32[]{:S(2)}) collective-permute-start(f32[24,128]{1,0:T(8,128)S(1)} %get-tuple-element.50), channel_id=1, source_target_pairs={{0,120},{8,16},{16,8},{24,32},{32,24},{40,48},{48,40},{56,64},{64,... | collective-permute-start | bytes 36872 | tf_op jit(solution)/shard_map/ppermute | solution.py:523
  9.8 1.2 %collective-permute-start.2 = (f32[24,128]{1,0:T(8,128)S(1)}, f32[24,128]{1,0:T(8,128)S(1)}, u32[]{:S(2)}, u32[]{:S(2)}) collective-permute-start(f32[24,128]{1,0:T(8,128)S(1)} %get-tuple-element.51), channel_id=1, source_target_pairs={{0,1},{1,0},{2,3},{3,2},{4,5},{5,4},{6,7},{7,6},{8,9},{9,8},{10,11... | collective-permute-start | bytes 36872 | tf_op jit(solution)/shard_map/ppermute | solution.py:523
  11.0 1.1 %collective-permute-start.3 = (f32[24,128]{1,0:T(8,128)S(1)}, f32[24,128]{1,0:T(8,128)S(1)}, u32[]{:S(2)}, u32[]{:S(2)}) collective-permute-start(f32[24,128]{1,0:T(8,128)S(1)} %get-tuple-element.52), channel_id=1, source_target_pairs={{0,7},{1,2},{2,1},{3,4},{4,3},{5,6},{6,5},{7,0},{8,15},{9,10},{10,... | collective-permute-start | bytes 36872 | tf_op jit(solution)/shard_map/ppermute | solution.py:523
  12.1 1.8 %shard_map.85 = (bf16[768,256]{1,0:T(8,128)(2,1)S(1)}, bf16[32,256]{1,0:T(8,128)(2,1)S(1)}, f32[120,16]{1,0:T(8,128)S(1)}, f32[16,512]{1,0:T(8,128)S(1)}) custom-call(f32[216,120]{1,0:T(8,128)S(1)} %get-tuple-element.58.basis, f32[216,120]{1,0:T(8,128)S(1)} %get-tuple-element.59.test, f32[8,120]{1,0:T(8,128)S(1)} %get-tuple-element.60.rows3, ...), custom_call_target="tpu_custom_call" | custom-call | flops 100000000 | bytes 1071328 | tf_op jit(solution)/shard_map/pallas_call | solution.py:501
  14.0 0.3 shard_map.86.proj
  14.3 0.2 shard_map.83
  14.5 0.0 collective-permute-done.1.refs_1_.rest_1_
  14.5 0.0 collective-permute-done.2.refs_2_.rest_2_
  14.6 0.1 shard_map.88.rest_4_
  14.7 0.8 %collective-permute-start.7 = (f32[16,64]{1,0:T(8,128)S(1)}, f32[16,64]{1,0:T(8,128)S(1)}, u32[]{:S(2)}, u32[]{:S(2)}) collective-permute-start(f32[16,64]{1,0:T(8,128)S(1)} %shard_map.88.rest_4_), channel_id=1, source_target_pairs={{0,7},{1,2},{2,1},{3,4},{4,3},{5,6},{6,5},{7,0},{8,15},{9,10},{10,... | collective-permute-start | bytes 12296 | tf_op jit(solution)/shard_map/ppermute | solution.py:523
  15.4 3.0 %collective-permute-start.6 = (f32[16,64]{1,0:T(8,128)S(1)}, f32[16,64]{1,0:T(8,128)S(1)}, u32[]{:S(2)}, u32[]{:S(2)}) collective-permute-start(f32[16,64]{1,0:T(8,128)S(1)} %shard_map.88.rest_4_), channel_id=1, source_target_pairs={{0,1},{1,0},{2,3},{3,2},{4,5},{5,4},{6,7},{7,6},{8,9},{9,8},{10,11... | collective-permute-start | bytes 12296 | tf_op jit(solution)/shard_map/ppermute | solution.py:523
  18.4 0.6 %collective-permute-start.5 = (f32[16,64]{1,0:T(8,128)S(1)}, f32[16,64]{1,0:T(8,128)S(1)}, u32[]{:S(2)}, u32[]{:S(2)}) collective-permute-start(f32[16,64]{1,0:T(8,128)S(1)} %shard_map.88.rest_4_), channel_id=1, source_target_pairs={{0,120},{8,16},{16,8},{24,32},{32,24},{40,48},{48,40},{56,64},{64,... | collective-permute-start | bytes 12296 | tf_op jit(solution)/shard_map/ppermute | solution.py:523
  19.1 0.3 shard_map.84.heights
  19.4 0.7 %shard_map.93.rest_0_ = f32[5,384,256]{2,1,0:T(8,128)S(1)} custom-call(f32[5,120,512]{2,1,0:T(8,128)S(1)} %get-tuple-element.65.state, f32[5,5,512]{2,1,0:T(8,128)S(1)} %get-tuple-element.48.coef, f32[8,512]{1,0:T(8,128)S(1)} %shard_map.84.heights, bf16[768,256]{1,0:T(8,128)(2,1)S(1)} %get-tuple-element.77.stack), custom_call_target="tpu_custom_call" | custom-call | flops 3000000000 | bytes 4048896 | tf_op jit(solution)/shard_map/pallas_call | solution.py:501
  20.1 2.0 %shard_map.94 = (f32[5,120,512]{2,1,0:T(8,128)S(1)}, f32[5,384,256]{2,1,0:T(8,128)S(1)}) custom-call(f32[5,120,512]{2,1,0:T(8,128)S(1)} %get-tuple-element.65.state, f32[5,5,512]{2,1,0:T(8,128)S(1)} %get-tuple-element.48.coef, f32[8,512]{1,0:T(8,128)S(1)} %shard_map.84.heights, bf16[768,256]{1,0:T(8,128)(2,1)S(1)} %get-tuple-element.77.stack, ...), custom_call_target="tpu_custom_call" | custom-call | flops 3000000000 | bytes 7243776 | tf_op jit(solution)/shard_map/pallas_call | solution.py:501
  22.1 0.1 shard_map.87.drift
  22.3 2.0 %collective-permute-done.5.rest_1_ = f32[16,64]{1,0:T(8,128)S(1)} collective-permute-done((f32[16,64]{1,0:T(8,128)S(1)}, f32[16,64]{1,0:T(8,128)S(1)}, u32[]{:S(2)}, u32[]{:S(2)}) %collective-permute-start.5) | collective-permute-done | bytes 4128 | tf_op jit(solution)/shard_map/ppermute | solution.py:523
  24.2 0.0 collective-permute-done.4.rest_0_
  24.3 0.8 %shard_map.89 = (f32[5,8,512]{2,1,0:T(8,128)S(1)}, f32[16,512]{1,0:T(8,128)S(1)}, f32[24,128]{1,0:T(8,128)S(1)}, f32[24,128]{1,0:T(8,128)S(1)}, f32[24,128]{1,0:...) custom-call(f32[5,5,512]{2,1,0:T(8,128)S(1)} %get-tuple-element.48.coef, ...), custom_call_target="tpu_custom_call" | custom-call | flops 1000000 | bytes 1804288 | tf_op jit(solution)/shard_map/pallas_call | solution.py:501
  25.0 0.1 collective-permute-start.8
  25.1 3.7 %collective-permute-start.9 = (f32[24,128]{1,0:T(8,128)S(1)}, f32[24,128]{1,0:T(8,128)S(1)}, u32[]{:S(2)}, u32[]{:S(2)}) collective-permute-start(f32[24,128]{1,0:T(8,128)S(1)} %get-tuple-element.70), channel_id=1, source_target_pairs={{0,120},{8,16},{16,8},{24,32},{32,24},{40,48},{48,40},{56,64},{64,... | collective-permute-start | bytes 36872 | tf_op jit(solution)/shard_map/ppermute | solution.py:523
  28.8 1.1 %collective-permute-start.10 = (f32[24,128]{1,0:T(8,128)S(1)}, f32[24,128]{1,0:T(8,128)S(1)}, u32[]{:S(2)}, u32[]{:S(2)}) collective-permute-start(f32[24,128]{1,0:T(8,128)S(1)} %get-tuple-element.71), channel_id=1, source_target_pairs={{0,1},{1,0},{2,3},{3,2},{4,5},{5,4},{6,7},{7,6},{8,9},{9,8},{10,11... | collective-permute-start | bytes 36872 | tf_op jit(solution)/shard_map/ppermute | solution.py:523
  29.9 1.2 %shard_map.95 = (f32[5,120,512]{2,1,0:T(8,128)S(1)}, f32[5,384,256]{2,1,0:T(8,128)S(1)}) custom-call(f32[5,120,512]{2,1,0:T(8,128)S(1)} %get-tuple-element.78.state, f32[5,5,512]{2,1,0:T(8,128)S(1)} %get-tuple-element.48.coef, f32[8,512]{1,0:T(8,128)S(1)} %shard_map.84.heights, bf16[768,256]{1,0:T(8,128)(2,1)S(1)} %get-tuple-element.77.stack, ...), custom_call_target="tpu_custom_call" | custom-call | flops 3000000000 | bytes 7243776 | tf_op jit(solution)/shard_map/pallas_call | solution.py:501
  31.2 2.2 %collective-permute-done.11.rest_3_ = f32[24,128]{1,0:T(8,128)S(1)} collective-permute-done((f32[24,128]{1,0:T(8,128)S(1)}, f32[24,128]{1,0:T(8,128)S(1)}, u32[]{:S(2)}, u32[]{:S(2)}) %collective-permute-start.11) | collective-permute-done | bytes 12320 | tf_op jit(solution)/shard_map/ppermute | solution.py:523
  33.3 0.1 shard_map.91.rest_4_
  33.4 0.9 %collective-permute-start.15 = (f32[16,64]{1,0:T(8,128)S(1)}, f32[16,64]{1,0:T(8,128)S(1)}, u32[]{:S(2)}, u32[]{:S(2)}) collective-permute-start(f32[16,64]{1,0:T(8,128)S(1)} %shard_map.91.rest_4_), channel_id=1, source_target_pairs={{0,7},{1,2},{2,1},{3,4},{4,3},{5,6},{6,5},{7,0},{8,15},{9,10},{10,... | collective-permute-start | bytes 12296 | tf_op jit(solution)/shard_map/ppermute | solution.py:523
  34.3 1.7 %collective-permute-start.14 = (f32[16,64]{1,0:T(8,128)S(1)}, f32[16,64]{1,0:T(8,128)S(1)}, u32[]{:S(2)}, u32[]{:S(2)}) collective-permute-start(f32[16,64]{1,0:T(8,128)S(1)} %shard_map.91.rest_4_), channel_id=1, source_target_pairs={{0,1},{1,0},{2,3},{3,2},{4,5},{5,4},{6,7},{7,6},{8,9},{9,8},{10,11... | collective-permute-start | bytes 12296 | tf_op jit(solution)/shard_map/ppermute | solution.py:523
  36.0 1.8 %collective-permute-start.13 = (f32[16,64]{1,0:T(8,128)S(1)}, f32[16,64]{1,0:T(8,128)S(1)}, u32[]{:S(2)}, u32[]{:S(2)}) collective-permute-start(f32[16,64]{1,0:T(8,128)S(1)} %shard_map.91.rest_4_), channel_id=1, source_target_pairs={{0,120},{8,16},{16,8},{24,32},{32,24},{40,48},{48,40},{56,64},{64,... | collective-permute-start | bytes 12296 | tf_op jit(solution)/shard_map/ppermute | solution.py:523
  37.8 0.0 collective-permute-start.12
  37.8 2.0 %shard_map.96 = (f32[5,120,512]{2,1,0:T(8,128)S(1)}, f32[5,384,256]{2,1,0:T(8,128)S(1)}) custom-call(f32[5,120,512]{2,1,0:T(8,128)S(1)} %get-tuple-element.80.state, f32[5,5,512]{2,1,0:T(8,128)S(1)} %get-tuple-element.48.coef, f32[8,512]{1,0:T(8,128)S(1)} %shard_map.84.heights, bf16[768,256]{1,0:T(8,128)(2,1)S(1)} %get-tuple-element.77.stack, ...), custom_call_target="tpu_custom_call" | custom-call | flops 3000000000 | bytes 7243776 | tf_op jit(solution)/shard_map/pallas_call | solution.py:501
  39.8 0.1 shard_map.90.drift
  40.0 1.8 %collective-permute-done.13.rest_1_ = f32[16,64]{1,0:T(8,128)S(1)} collective-permute-done((f32[16,64]{1,0:T(8,128)S(1)}, f32[16,64]{1,0:T(8,128)S(1)}, u32[]{:S(2)}, u32[]{:S(2)}) %collective-permute-start.13) | collective-permute-done | bytes 4128 | tf_op jit(solution)/shard_map/ppermute | solution.py:523
  41.8 0.8 %shard_map.92 = (f32[5,8,512]{2,1,0:T(8,128)S(1)}, f32[16,512]{1,0:T(8,128)S(1)}, f32[24,128]{1,0:T(8,128)S(1)}, f32[24,128]{1,0:T(8,128)S(1)}, f32[24,128]{1,0:...) custom-call(f32[5,5,512]{2,1,0:T(8,128)S(1)} %get-tuple-element.48.coef, f32[8,512]{1,0:T(8,128)S(1)} %shard_map.84.heights, ...), custom_call_target="tpu_custom_call" | custom-call | flops 1000000 | bytes 1722368 | tf_op jit(solution)/shard_map/pallas_call | solution.py:501
  42.6 0.1 collective-permute-start.16
  42.7 2.6 %collective-permute-start.17 = (f32[24,128]{1,0:T(8,128)S(1)}, f32[24,128]{1,0:T(8,128)S(1)}, u32[]{:S(2)}, u32[]{:S(2)}) collective-permute-start(f32[24,128]{1,0:T(8,128)S(1)} %get-tuple-element.88), channel_id=1, source_target_pairs={{0,120},{8,16},{16,8},{24,32},{32,24},{40,48},{48,40},{56,64},{64,... | collective-permute-start | bytes 36872 | tf_op jit(solution)/shard_map/ppermute | solution.py:523
  45.3 1.1 %collective-permute-start.18 = (f32[24,128]{1,0:T(8,128)S(1)}, f32[24,128]{1,0:T(8,128)S(1)}, u32[]{:S(2)}, u32[]{:S(2)}) collective-permute-start(f32[24,128]{1,0:T(8,128)S(1)} %get-tuple-element.89), channel_id=1, source_target_pairs={{0,1},{1,0},{2,3},{3,2},{4,5},{5,4},{6,7},{7,6},{8,9},{9,8},{10,11... | collective-permute-start | bytes 36872 | tf_op jit(solution)/shard_map/ppermute | solution.py:523
  46.4 0.7 %shard_map.97.state = f32[5,120,512]{2,1,0:T(8,128)S(1)} custom-call(f32[5,120,512]{2,1,0:T(8,128)S(1)} %get-tuple-element.82.state, f32[5,5,512]{2,1,0:T(8,128)S(1)} %get-tuple-element.48.coef, f32[8,512]{1,0:T(8,128)S(1)} %shard_map.84.heights, bf16[768,256]{1,0:T(8,128)(2,1)S(1)} %get-tuple-element.77.stack, f32[5,384,256]{2,1,0:T(8,128)S(1)} %get-tuple-element.83.rest_0_), custom_call_target="tpu_custom_call" | custom-call | flops 3000000000 | bytes 5277696 | tf_op jit(solution)/shard_map/pallas_call | solution.py:501
  47.1 1.5 %collective-permute-done.17.rest_1_ = f32[24,128]{1,0:T(8,128)S(1)} collective-permute-done((f32[24,128]{1,0:T(8,128)S(1)}, f32[24,128]{1,0:T(8,128)S(1)}, u32[]{:S(2)}, u32[]{:S(2)}) %collective-permute-start.17) | collective-permute-done | bytes 12320 | tf_op jit(solution)/shard_map/ppermute | solution.py:523
  48.6 1.2 %collective-permute-done.19.rest_3_ = f32[24,128]{1,0:T(8,128)S(1)} collective-permute-done((f32[24,128]{1,0:T(8,128)S(1)}, f32[24,128]{1,0:T(8,128)S(1)}, u32[]{:S(2)}, u32[]{:S(2)}) %collective-permute-start.19) | collective-permute-done | bytes 12320 | tf_op jit(solution)/shard_map/ppermute | solution.py:523
  49.8 0.1 shard_map.99.rest_4_
  49.9 0.8 %collective-permute-start.23 = (f32[16,64]{1,0:T(8,128)S(1)}, f32[16,64]{1,0:T(8,128)S(1)}, u32[]{:S(2)}, u32[]{:S(2)}) collective-permute-start(f32[16,64]{1,0:T(8,128)S(1)} %shard_map.99.rest_4_), channel_id=1, source_target_pairs={{0,7},{1,2},{2,1},{3,4},{4,3},{5,6},{6,5},{7,0},{8,15},{9,10},{10,... | collective-permute-start | bytes 12296 | tf_op jit(solution)/shard_map/ppermute | solution.py:523
  50.7 2.3 %collective-permute-start.22 = (f32[16,64]{1,0:T(8,128)S(1)}, f32[16,64]{1,0:T(8,128)S(1)}, u32[]{:S(2)}, u32[]{:S(2)}) collective-permute-start(f32[16,64]{1,0:T(8,128)S(1)} %shard_map.99.rest_4_), channel_id=1, source_target_pairs={{0,1},{1,0},{2,3},{3,2},{4,5},{5,4},{6,7},{7,6},{8,9},{9,8},{10,11... | collective-permute-start | bytes 12296 | tf_op jit(solution)/shard_map/ppermute | solution.py:523
  53.0 2.4 %collective-permute-start.21 = (f32[16,64]{1,0:T(8,128)S(1)}, f32[16,64]{1,0:T(8,128)S(1)}, u32[]{:S(2)}, u32[]{:S(2)}) collective-permute-start(f32[16,64]{1,0:T(8,128)S(1)} %shard_map.99.rest_4_), channel_id=1, source_target_pairs={{0,120},{8,16},{16,8},{24,32},{32,24},{40,48},{48,40},{56,64},{64,... | collective-permute-start | bytes 12296 | tf_op jit(solution)/shard_map/ppermute | solution.py:523
  55.4 0.7 %shard_map.98 = (f32[5,120,512]{2,1,0:T(8,128)S(1)}, f32[3,120,128]{2,1,0:T(8,128)S(1)}) custom-call(f32[5,5,512]{2,1,0:T(8,128)S(1)} %get-tuple-element.48.coef, f32[8,512]{1,0:T(8,128)S(1)} %shard_map.84.heights, f32[5,8,512]{2,1,0:T(8,128)S(1)} %get-tuple-element.74.weights0, f32[5,8,512]{2,1,0:T(8,128)S(1)} %get-tuple-element.75.weights1, ...), custom_call_target="tpu_custom_call" | custom-call | flops 100000000 | bytes 2881024 | tf_op jit(solution)/shard_map/pallas_call | solution.py:501
  56.1 2.7 %collective-permute-done.21.rest_1_ = f32[16,64]{1,0:T(8,128)S(1)} collective-permute-done((f32[16,64]{1,0:T(8,128)S(1)}, f32[16,64]{1,0:T(8,128)S(1)}, u32[]{:S(2)}, u32[]{:S(2)}) %collective-permute-start.21) | collective-permute-done | bytes 4128 | tf_op jit(solution)/shard_map/ppermute | solution.py:523
  58.8 1.4 %shard_map.100 = f32[5,120,512]{2,1,0:T(8,128)} custom-call(f32[5,5,512]{2,1,0:T(8,128)S(1)} %get-tuple-element.48.coef, f32[8,512]{1,0:T(8,128)S(1)} %shard_map.84.heights, f32[16,512]{1,0:T(8,128)S(1)} %get-tuple-element.62.kappas, f32[16,512]{1,0:T(8,128)S(1)} %get-tuple-element.73.old_aux, f32[3,120,128]{2,1,0:T(8,128)S(1)} %get-tuple-element.84.wide, ...), custom_call_target="tpu_custom_call" | custom-call | flops 1000000 | bytes 3450880 | tf_op jit(solution)/shard_map/pallas_call | solution.py:501
  (19 shorter events, 0.0 us)
Async XLA Ops:
  2.2 12.3 %collective-permute-start = (f32[24,128]{1,0:T(8,128)S(1)}, f32[24,128]{1,0:T(8,128)S(1)}, u32[]{:S(2)}, u32[]{:S(2)}) collective-permute-start(f32[24,128]{1,0:T(8,128)S(1)} %get-tuple-element.49), channel_id=1, source_target_pairs={{0,8},{8,0},{16,24},{24,16},{32,40},{40,32},{48,56},{56,48},{64,72... | collective-permute-start | bytes 36872 | tf_op jit(solution)/shard_map/ppermute | solution.py:523
  4.4 10.1 %collective-permute-start.1 = (f32[24,128]{1,0:T(8,128)S(1)}, f32[24,128]{1,0:T(8,128)S(1)}, u32[]{:S(2)}, u32[]{:S(2)}) collective-permute-start(f32[24,128]{1,0:T(8,128)S(1)} %get-tuple-element.50), channel_id=1, source_target_pairs={{0,120},{8,16},{16,8},{24,32},{32,24},{40,48},{48,40},{56,64},{64,... | collective-permute-start | bytes 36872 | tf_op jit(solution)/shard_map/ppermute | solution.py:523
  9.8 4.7 %collective-permute-start.2 = (f32[24,128]{1,0:T(8,128)S(1)}, f32[24,128]{1,0:T(8,128)S(1)}, u32[]{:S(2)}, u32[]{:S(2)}) collective-permute-start(f32[24,128]{1,0:T(8,128)S(1)} %get-tuple-element.51), channel_id=1, source_target_pairs={{0,1},{1,0},{2,3},{3,2},{4,5},{5,4},{6,7},{7,6},{8,9},{9,8},{10,11... | collective-permute-start | bytes 36872 | tf_op jit(solution)/shard_map/ppermute | solution.py:523
  11.0 3.5 %collective-permute-start.3 = (f32[24,128]{1,0:T(8,128)S(1)}, f32[24,128]{1,0:T(8,128)S(1)}, u32[]{:S(2)}, u32[]{:S(2)}) collective-permute-start(f32[24,128]{1,0:T(8,128)S(1)} %get-tuple-element.52), channel_id=1, source_target_pairs={{0,7},{1,2},{2,1},{3,4},{4,3},{5,6},{6,5},{7,0},{8,15},{9,10},{10,... | collective-permute-start | bytes 36872 | tf_op jit(solution)/shard_map/ppermute | solution.py:523
  14.7 7.6 %collective-permute-start.7 = (f32[16,64]{1,0:T(8,128)S(1)}, f32[16,64]{1,0:T(8,128)S(1)}, u32[]{:S(2)}, u32[]{:S(2)}) collective-permute-start(f32[16,64]{1,0:T(8,128)S(1)} %shard_map.88.rest_4_), channel_id=1, source_target_pairs={{0,7},{1,2},{2,1},{3,4},{4,3},{5,6},{6,5},{7,0},{8,15},{9,10},{10,... | collective-permute-start | bytes 12296 | tf_op jit(solution)/shard_map/ppermute | solution.py:523
  15.4 6.8 %collective-permute-start.6 = (f32[16,64]{1,0:T(8,128)S(1)}, f32[16,64]{1,0:T(8,128)S(1)}, u32[]{:S(2)}, u32[]{:S(2)}) collective-permute-start(f32[16,64]{1,0:T(8,128)S(1)} %shard_map.88.rest_4_), channel_id=1, source_target_pairs={{0,1},{1,0},{2,3},{3,2},{4,5},{5,4},{6,7},{7,6},{8,9},{9,8},{10,11... | collective-permute-start | bytes 12296 | tf_op jit(solution)/shard_map/ppermute | solution.py:523
  18.4 5.8 %collective-permute-start.5 = (f32[16,64]{1,0:T(8,128)S(1)}, f32[16,64]{1,0:T(8,128)S(1)}, u32[]{:S(2)}, u32[]{:S(2)}) collective-permute-start(f32[16,64]{1,0:T(8,128)S(1)} %shard_map.88.rest_4_), channel_id=1, source_target_pairs={{0,120},{8,16},{16,8},{24,32},{32,24},{40,48},{48,40},{56,64},{64,... | collective-permute-start | bytes 12296 | tf_op jit(solution)/shard_map/ppermute | solution.py:523
  19.1 5.2 %collective-permute-start.4 = (f32[16,64]{1,0:T(8,128)S(1)}, f32[16,64]{1,0:T(8,128)S(1)}, u32[]{:S(2)}, u32[]{:S(2)}) collective-permute-start(f32[16,64]{1,0:T(8,128)S(1)} %shard_map.88.rest_4_), channel_id=1, source_target_pairs={{0,8},{8,0},{16,24},{24,16},{32,40},{40,32},{48,56},{56,48},{64,72... | collective-permute-start | bytes 12296 | tf_op jit(solution)/shard_map/ppermute | solution.py:523
  25.0 6.1 %collective-permute-start.8 = (f32[24,128]{1,0:T(8,128)S(1)}, f32[24,128]{1,0:T(8,128)S(1)}, u32[]{:S(2)}, u32[]{:S(2)}) collective-permute-start(f32[24,128]{1,0:T(8,128)S(1)} %get-tuple-element.69), channel_id=1, source_target_pairs={{0,8},{8,0},{16,24},{24,16},{32,40},{40,32},{48,56},{56,48},{64,72... | collective-permute-start | bytes 36872 | tf_op jit(solution)/shard_map/ppermute | solution.py:523
  25.1 6.0 %collective-permute-start.9 = (f32[24,128]{1,0:T(8,128)S(1)}, f32[24,128]{1,0:T(8,128)S(1)}, u32[]{:S(2)}, u32[]{:S(2)}) collective-permute-start(f32[24,128]{1,0:T(8,128)S(1)} %get-tuple-element.70), channel_id=1, source_target_pairs={{0,120},{8,16},{16,8},{24,32},{32,24},{40,48},{48,40},{56,64},{64,... | collective-permute-start | bytes 36872 | tf_op jit(solution)/shard_map/ppermute | solution.py:523
  28.8 2.4 %collective-permute-start.10 = (f32[24,128]{1,0:T(8,128)S(1)}, f32[24,128]{1,0:T(8,128)S(1)}, u32[]{:S(2)}, u32[]{:S(2)}) collective-permute-start(f32[24,128]{1,0:T(8,128)S(1)} %get-tuple-element.71), channel_id=1, source_target_pairs={{0,1},{1,0},{2,3},{3,2},{4,5},{5,4},{6,7},{7,6},{8,9},{9,8},{10,11... | collective-permute-start | bytes 36872 | tf_op jit(solution)/shard_map/ppermute | solution.py:523
  29.9 3.4 %collective-permute-start.11 = (f32[24,128]{1,0:T(8,128)S(1)}, f32[24,128]{1,0:T(8,128)S(1)}, u32[]{:S(2)}, u32[]{:S(2)}) collective-permute-start(f32[24,128]{1,0:T(8,128)S(1)} %get-tuple-element.72), channel_id=1, source_target_pairs={{0,7},{1,2},{2,1},{3,4},{4,3},{5,6},{6,5},{7,0},{8,15},{9,10},{10,... | collective-permute-start | bytes 36872 | tf_op jit(solution)/shard_map/ppermute | solution.py:523
  33.4 6.5 %collective-permute-start.15 = (f32[16,64]{1,0:T(8,128)S(1)}, f32[16,64]{1,0:T(8,128)S(1)}, u32[]{:S(2)}, u32[]{:S(2)}) collective-permute-start(f32[16,64]{1,0:T(8,128)S(1)} %shard_map.91.rest_4_), channel_id=1, source_target_pairs={{0,7},{1,2},{2,1},{3,4},{4,3},{5,6},{6,5},{7,0},{8,15},{9,10},{10,... | collective-permute-start | bytes 12296 | tf_op jit(solution)/shard_map/ppermute | solution.py:523
  34.3 5.7 %collective-permute-start.14 = (f32[16,64]{1,0:T(8,128)S(1)}, f32[16,64]{1,0:T(8,128)S(1)}, u32[]{:S(2)}, u32[]{:S(2)}) collective-permute-start(f32[16,64]{1,0:T(8,128)S(1)} %shard_map.91.rest_4_), channel_id=1, source_target_pairs={{0,1},{1,0},{2,3},{3,2},{4,5},{5,4},{6,7},{7,6},{8,9},{9,8},{10,11... | collective-permute-start | bytes 12296 | tf_op jit(solution)/shard_map/ppermute | solution.py:523
  36.0 5.8 %collective-permute-start.13 = (f32[16,64]{1,0:T(8,128)S(1)}, f32[16,64]{1,0:T(8,128)S(1)}, u32[]{:S(2)}, u32[]{:S(2)}) collective-permute-start(f32[16,64]{1,0:T(8,128)S(1)} %shard_map.91.rest_4_), channel_id=1, source_target_pairs={{0,120},{8,16},{16,8},{24,32},{32,24},{40,48},{48,40},{56,64},{64,... | collective-permute-start | bytes 12296 | tf_op jit(solution)/shard_map/ppermute | solution.py:523
  37.8 4.0 %collective-permute-start.12 = (f32[16,64]{1,0:T(8,128)S(1)}, f32[16,64]{1,0:T(8,128)S(1)}, u32[]{:S(2)}, u32[]{:S(2)}) collective-permute-start(f32[16,64]{1,0:T(8,128)S(1)} %shard_map.91.rest_4_), channel_id=1, source_target_pairs={{0,8},{8,0},{16,24},{24,16},{32,40},{40,32},{48,56},{56,48},{64,72... | collective-permute-start | bytes 12296 | tf_op jit(solution)/shard_map/ppermute | solution.py:523
  42.6 4.5 %collective-permute-start.16 = (f32[24,128]{1,0:T(8,128)S(1)}, f32[24,128]{1,0:T(8,128)S(1)}, u32[]{:S(2)}, u32[]{:S(2)}) collective-permute-start(f32[24,128]{1,0:T(8,128)S(1)} %get-tuple-element.87), channel_id=1, source_target_pairs={{0,8},{8,0},{16,24},{24,16},{32,40},{40,32},{48,56},{56,48},{64,72... | collective-permute-start | bytes 36872 | tf_op jit(solution)/shard_map/ppermute | solution.py:523
  42.7 5.9 %collective-permute-start.17 = (f32[24,128]{1,0:T(8,128)S(1)}, f32[24,128]{1,0:T(8,128)S(1)}, u32[]{:S(2)}, u32[]{:S(2)}) collective-permute-start(f32[24,128]{1,0:T(8,128)S(1)} %get-tuple-element.88), channel_id=1, source_target_pairs={{0,120},{8,16},{16,8},{24,32},{32,24},{40,48},{48,40},{56,64},{64,... | collective-permute-start | bytes 36872 | tf_op jit(solution)/shard_map/ppermute | solution.py:523
  45.3 3.3 %collective-permute-start.18 = (f32[24,128]{1,0:T(8,128)S(1)}, f32[24,128]{1,0:T(8,128)S(1)}, u32[]{:S(2)}, u32[]{:S(2)}) collective-permute-start(f32[24,128]{1,0:T(8,128)S(1)} %get-tuple-element.89), channel_id=1, source_target_pairs={{0,1},{1,0},{2,3},{3,2},{4,5},{5,4},{6,7},{7,6},{8,9},{9,8},{10,11... | collective-permute-start | bytes 36872 | tf_op jit(solution)/shard_map/ppermute | solution.py:523
  46.4 3.4 %collective-permute-start.19 = (f32[24,128]{1,0:T(8,128)S(1)}, f32[24,128]{1,0:T(8,128)S(1)}, u32[]{:S(2)}, u32[]{:S(2)}) collective-permute-start(f32[24,128]{1,0:T(8,128)S(1)} %get-tuple-element.90), channel_id=1, source_target_pairs={{0,7},{1,2},{2,1},{3,4},{4,3},{5,6},{6,5},{7,0},{8,15},{9,10},{10,... | collective-permute-start | bytes 36872 | tf_op jit(solution)/shard_map/ppermute | solution.py:523
  49.9 6.2 %collective-permute-start.23 = (f32[16,64]{1,0:T(8,128)S(1)}, f32[16,64]{1,0:T(8,128)S(1)}, u32[]{:S(2)}, u32[]{:S(2)}) collective-permute-start(f32[16,64]{1,0:T(8,128)S(1)} %shard_map.99.rest_4_), channel_id=1, source_target_pairs={{0,7},{1,2},{2,1},{3,4},{4,3},{5,6},{6,5},{7,0},{8,15},{9,10},{10,... | collective-permute-start | bytes 12296 | tf_op jit(solution)/shard_map/ppermute | solution.py:523
  50.7 5.4 %collective-permute-start.22 = (f32[16,64]{1,0:T(8,128)S(1)}, f32[16,64]{1,0:T(8,128)S(1)}, u32[]{:S(2)}, u32[]{:S(2)}) collective-permute-start(f32[16,64]{1,0:T(8,128)S(1)} %shard_map.99.rest_4_), channel_id=1, source_target_pairs={{0,1},{1,0},{2,3},{3,2},{4,5},{5,4},{6,7},{7,6},{8,9},{9,8},{10,11... | collective-permute-start | bytes 12296 | tf_op jit(solution)/shard_map/ppermute | solution.py:523
  53.0 5.8 %collective-permute-start.21 = (f32[16,64]{1,0:T(8,128)S(1)}, f32[16,64]{1,0:T(8,128)S(1)}, u32[]{:S(2)}, u32[]{:S(2)}) collective-permute-start(f32[16,64]{1,0:T(8,128)S(1)} %shard_map.99.rest_4_), channel_id=1, source_target_pairs={{0,120},{8,16},{16,8},{24,32},{32,24},{40,48},{48,40},{56,64},{64,... | collective-permute-start | bytes 12296 | tf_op jit(solution)/shard_map/ppermute | solution.py:523
  55.4 3.4 %collective-permute-start.20 = (f32[16,64]{1,0:T(8,128)S(1)}, f32[16,64]{1,0:T(8,128)S(1)}, u32[]{:S(2)}, u32[]{:S(2)}) collective-permute-start(f32[16,64]{1,0:T(8,128)S(1)} %shard_map.99.rest_4_), channel_id=1, source_target_pairs={{0,8},{8,0},{16,24},{24,16},{32,40},{40,32},{48,56},{56,48},{64,72... | collective-permute-start | bytes 12296 | tf_op jit(solution)/shard_map/ppermute | solution.py:523
